TPU v7x, 32 devices: a whole 2x2x4 slice. The times are simulated.
32 devices in a mesh: ctx: 8 (over y, x, core), tp: 4 (over z).
Axes of the slice: x: 2, y: 2, z: 4, core: 2. Of those that a mesh axis runs over, the one named last changes fastest.
Arguments:
- tokens: bfloat16 [4096, 2048], P(('ctx', 'tp')), may hold values from -8 to 8
- projection: bfloat16 [2048, 640], P(None, 'tp'), may hold values from -0.125 to 0.125
- conv_weight: float32 [4, 640], P(None, 'tp'), may hold values from -2.5 to 2.5
Outputs:
- attended: bfloat16 [4096, 512], P('ctx', 'tp')
All inputs are finite; a program needn't handle non-finite values.
Results may differ from a plain program's by a relative error of at most 0.0032.
The roundings to bfloat16 on the way count: a program that leaves them out, or rounds other values in their place, can miss the bound.
Values may be sent and summed in bfloat16 or wider, within the bound.
No kernel may reach another device: no remote copies, remote signals or barrier semaphores. Data moves between devices by JAX's collectives and lax.ppermute only.
A program may use at most 64 MiB of HBM per device.

v0:
```python
import functools
import math

import jax
import jax.numpy as jnp
from jax import lax
from jax.experimental import pallas as pl
from jax.experimental.pallas import tpu as pltpu
from jax.sharding import PartitionSpec as P


FEAT = 16
HALO = 8
PIECES = 8
LANES = 128
QUAD_FEATS = FEAT * (FEAT + 1) // 2
NUM_FEAT = QUAD_FEATS + FEAT + 8
STATE_ROWS = NUM_FEAT + 8
F32 = jnp.float32
BF16 = jnp.bfloat16
VMEM = pl.BlockSpec(memory_space=pltpu.VMEM)
SMEM = pl.BlockSpec(memory_space=pltpu.SMEM)
LAST = (((1,), (1,)), ((), ()))


def call(kernel, outs, operands, scalars=0, scratch=(), flops=1 << 20, moved=1 << 20):
    return pl.pallas_call(
        kernel,
        out_shape=outs,
        in_specs=[SMEM] * scalars + [VMEM] * (len(operands) - scalars),
        out_specs=[VMEM] * len(outs),
        scratch_shapes=list(scratch),
        compiler_params=pltpu.CompilerParams(vmem_limit_bytes=16 << 20),
        cost_estimate=pl.CostEstimate(flops=flops, bytes_accessed=moved, transcendentals=0),
    )(*operands)


def dot_last(left, right):
    return lax.dot_general(left, right, LAST, preferred_element_type=F32)


def own_kernel(tokens_ref, weight_ref, own_ref):
    own_ref[...] = dot_last(weight_ref[...], tokens_ref[...]).astype(BF16)


def halo_kernel(tail_ref, weight_ref, halo_ref):
    padded = jnp.concatenate(
        [jnp.zeros((halo_ref.shape[1] - HALO, tail_ref.shape[1]), BF16), tail_ref[...]], axis=0
    )
    halo_ref[...] = dot_last(weight_ref[...], padded).astype(BF16)


def gathered(share, tokens_ref, pieces):
    depth = pieces[0].shape[1]
    total = None
    for index, piece in zip((0, 2, 4, 6, 1, 3, 5, 7), pieces):
        start = pl.multiple_of((share ^ index) * depth, depth)
        part = dot_last(piece[...], tokens_ref[:, pl.ds(start, depth)])
        total = part if total is None else total + part
    return total.astype(BF16)


def early_kernel(share_ref, tokens_ref, *refs):
    share = share_ref[0]
    count = len(refs) // (PIECES + 1)
    for turn in range(count):
        refs[PIECES * count + turn][...] = gathered(
            share, tokens_ref, refs[PIECES * turn : PIECES * turn + PIECES]
        )


def late_kernel(share_ref, tokens_ref, weight_ref, *refs):
    share = share_ref[0]
    count = len(refs) // (PIECES + 1)
    for turn in range(count):
        refs[PIECES * count + turn][...] = gathered(
            share, tokens_ref, refs[PIECES * turn : PIECES * turn + PIECES]
        )
    refs[-1][...] = dot_last(weight_ref[...], tokens_ref[...]).astype(BF16)


def features(raw, weighted):
    scale = 1.0 / (math.sqrt(2.0) * math.sqrt(FEAT))
    parts = []
    for shift in range(FEAT // 2 + 1):
        pair = raw * (pltpu.roll(raw, shift, 0) if shift else raw) * scale
        if shift == FEAT // 2:
            pair = pair[: FEAT // 2]
        pair = pair.astype(BF16).astype(F32)
        parts.append(pair * 2.0 if weighted and shift else pair)
    parts.append(raw * FEAT ** (-0.25))
    row = lax.broadcasted_iota(jnp.int32, (8, raw.shape[1]), 0)
    parts.append(jnp.where(row == 0, 1.0, 0.0).astype(F32))
    return jnp.concatenate(parts, axis=0).astype(BF16)


def feature_kernel(place_ref, conv_ref, halo_ref, *refs):
    count = place_ref.shape[0]
    blocks = refs[:count]
    query_ref, key_ref, value_ref, state_ref, wide = refs[count:]
    width = halo_ref.shape[1]
    local_rows = width * count
    wide[:, :width] = halo_ref[...].astype(F32)
    for index, block in enumerate(blocks):
        start = pl.multiple_of((place_ref[index] + 1) * width, LANES)
        wide[:, pl.ds(start, width)] = block[...].astype(F32)
    padded = wide[...]
    convolved = jnp.zeros((padded.shape[0], local_rows), F32)
    for offset in range(conv_ref.shape[1]):
        moved = pltpu.roll(padded, offset, 1) if offset else padded
        convolved += conv_ref[:, offset : offset + 1] * moved[:, width:]
    value = convolved[2 * FEAT :].astype(BF16)
    value_ref[...] = value
    query = features(convolved[:FEAT], False)
    query_ref[...] = query.T
    key = features(convolved[FEAT : 2 * FEAT], True)
    key_ref[...] = key
    state_ref[:NUM_FEAT, :] = dot_last(key, value)
    total = dot_last(jnp.ones((8, local_rows), BF16), key)
    lanes = state_ref.shape[1]
    rest = NUM_FEAT - lanes
    more = jnp.concatenate([total[:, lanes:], jnp.zeros((8, lanes - rest), F32)], axis=1)
    row = lax.broadcasted_iota(jnp.int32, (8, lanes), 0)
    state_ref[NUM_FEAT:, :] = jnp.where(row == 0, total[:, :lanes], jnp.where(row == 1, more, 0.0))


def inner_kernel(query_ref, key_ref, value_ref, numerator_ref, denominator_ref):
    local_rows = query_ref.shape[0]
    width = value_ref.shape[0]
    step = LANES
    for start in range(0, local_rows, step):
        size = start + step
        scores = jnp.dot(query_ref[start:size, :], key_ref[:, :size], preferred_element_type=F32)
        row = lax.broadcasted_iota(jnp.int32, (step, size), 0) + start
        column = lax.broadcasted_iota(jnp.int32, (step, size), 1)
        scores = jnp.where(row >= column, scores, 0.0)
        numerator_ref[start:size, :] = dot_last(scores.astype(BF16), value_ref[:, :size])
        denominator_ref[start:size, :] = jnp.broadcast_to(
            jnp.sum(scores, axis=1, keepdims=True), (step, width)
        )


def finish_kernel(query_ref, numerator_ref, denominator_ref, *refs):
    states, out_ref = refs[:-1], refs[-1]
    state = states[0][...]
    for other in states[1:]:
        state += other[...]
    width = numerator_ref.shape[1]
    query = query_ref[...]
    rest = state[:NUM_FEAT, :]
    numerator = numerator_ref[...]
    for _ in range(3):
        part = rest.astype(BF16)
        rest = rest - part.astype(F32)
        numerator += jnp.dot(query, part, preferred_element_type=F32)
    totals = jnp.concatenate(
        [state[NUM_FEAT : NUM_FEAT + 1, :], state[NUM_FEAT + 1 : NUM_FEAT + 2, : NUM_FEAT - width]], axis=1
    )
    denominator = denominator_ref[:, :1] + jnp.sum(query.astype(F32) * totals, axis=1, keepdims=True)
    out_ref[...] = (numerator / denominator).astype(BF16)


def per_device(ctx, tp, tokens, projection, conv_weight):
    both = ("ctx", "tp")
    rows, depth = tokens.shape
    row_width = projection.shape[1]
    val_width = row_width - 2 * FEAT
    local_rows = rows * tp
    turns = range(1, tp // 2)
    me = lax.axis_index("ctx")
    head = lax.axis_index("tp")
    weight = projection.T
    piece = depth // PIECES
    share = me & PIECES - 1

    def swap(array, bit):
        return lax.ppermute(array, "ctx", [(i, i ^ bit) for i in range(ctx)])

    mine = lax.dynamic_slice(weight, (0, share * piece), (row_width, piece))
    pieces = []
    for turn in turns:
        first = lax.ppermute(mine, "tp", [((z + 2 * turn) % tp, z) for z in range(tp)])
        parts = [first] + [swap(first, bits) for bits in (2, 4, 6)]
        pieces += parts + [swap(part, 1) for part in parts]
    paired = lax.ppermute(tokens, "tp", [(z, z ^ 1) for z in range(tp)])

    last_rows = tokens[rows - HALO :]
    tail = None
    for z in range(tp):
        pairs = [((c - 1) * tp + tp - 1, c * tp + z) for c in range(1, ctx)]
        part = lax.ppermute(last_rows, both, pairs)
        tail = part if tail is None else tail + part

    shape = jax.ShapeDtypeStruct((row_width, rows), BF16)
    work = 2 * rows * depth * row_width
    side = share.astype(jnp.int32).reshape(1)
    own = call(own_kernel, [shape], [tokens, weight], flops=work)[0]
    halo = call(halo_kernel, [shape], [tail, weight], flops=work)[0]
    early = call(early_kernel, [shape] * len(turns), [side, tokens] + pieces, 1, flops=work)
    *late, other = call(
        late_kernel, [shape] * (len(turns) + 1), [side, paired, weight] + pieces, 1, flops=2 * work
    )
    blocks, places = [own, other], [head, head ^ 1]
    for turn, one, two in zip(turns, early, late):
        pairs = [(z, (z + 2 * turn) % tp) for z in range(tp)]
        source = (head + tp - 2 * turn) % tp
        blocks += [lax.ppermute(one, "tp", pairs), lax.ppermute(two, "tp", pairs)]
        places += [source, source ^ 1]
    place = jnp.stack(places).astype(jnp.int32)
    query, key, value, state = call(
        feature_kernel,
        [
            jax.ShapeDtypeStruct((local_rows, NUM_FEAT), BF16),
            jax.ShapeDtypeStruct((NUM_FEAT, local_rows), BF16),
            jax.ShapeDtypeStruct((val_width, local_rows), BF16),
            jax.ShapeDtypeStruct((STATE_ROWS, val_width), F32),
        ],
        [place, conv_weight.T, halo] + blocks,
        1,
        [pltpu.VMEM((row_width, rows + local_rows), F32)],
    )
    numerator, denominator = call(
        inner_kernel,
        [jax.ShapeDtypeStruct((local_rows, val_width), F32)] * 2,
        [query, key, value],
        flops=2 * local_rows * local_rows * (NUM_FEAT + val_width),
    )
    received = swap(state, 1)
    terms = [jnp.where(me % 2 == 1, received, 0.0)]
    total = state + received
    bit = 2
    while bit < ctx:
        radix = min(4, ctx // bit)
        last = bit * radix >= ctx
        digit = me // bit % radix
        parts = []
        for delta in range(1, radix):
            pairs = [(c, c ^ delta * bit) for c in range(ctx)]
            parts.append(lax.ppermute(total, "ctx", pairs))
            terms.append(jnp.where(digit > digit ^ delta, parts[-1], 0.0))
        if not last:
            total = functools.reduce(jnp.add, parts, total)
        bit *= radix
    return call(
        finish_kernel,
        [jax.ShapeDtypeStruct((local_rows, val_width), BF16)],
        [query, numerator, denominator] + terms,
        flops=6 * local_rows * NUM_FEAT * val_width,
    )[0]


def solution(mesh):
    ctx, tp = mesh.shape["ctx"], mesh.shape["tp"]
    if tp % 2 or tp < 4 or ctx < 8 or ctx & (ctx - 1):
        raise ValueError("unsupported mesh")

    def body(*arrays):
        return per_device(ctx, tp, *arrays)

    return jax.shard_map(
        body,
        mesh=mesh,
        in_specs=(P(("ctx", "tp"), None), P(None, "tp"), P(None, "tp")),
        out_specs=P("ctx", "tp"),
        check_vma=False,
    )
```

profile of v0, /device:TPU:8, one launch (start us, length us, event | category | flops | bytes accessed | tf_op | source)
XLA Modules:
  0.0 56.3 jit_solution(1816237723139800957)
XLA Ops:
  0.0 0.9 %dynamic-slice_bitcast_fusion = bf16[160,256]{1,0:T(8,128)(2,1)S(1)} fusion(bf16[2048,160]{0,1:T(8,128)(2,1)} %param.4, s32[]{:T(128)S(6)} %select_n.49), kind=kLoop, calls=%fused_computation | loop fusion | bytes 163844 | tf_op jit(solution)/shard_map/dynamic_slice | solution.py:179
  0.9 3.0 %collective-permute-start.5 = (bf16[160,256]{1,0:T(8,128)(2,1)S(1)}, bf16[160,256]{1,0:T(8,128)(2,1)S(1)}, u32[]{:S(2)}, u32[]{:S(2)}) collective-permute-start(bf16[160,256]{1,0:T(8,128)(2,1)S(1)} %dynamic-slice_bitcast_fusion), channel_id=1, source_target_pairs={{2,0},{3,1},{0,2},{1,3},{6,4},{7,5},{4,6},{5,7},{10,8},{11,9},{8,1... | collective-permute-start | bytes 245768 | tf_op jit(solution)/shard_map/ppermute | solution.py:182
  3.9 12.7 %collective-permute-done.5.refs_0_ = bf16[160,256]{1,0:T(8,128)(2,1)S(1)} collective-permute-done((bf16[160,256]{1,0:T(8,128)(2,1)S(1)}, bf16[160,256]{1,0:T(8,128)(2,1)S(1)}, u32[]{:S(2)}, u32[]{:S(2)}) %collective-permute-start.5) | collective-permute-done | bytes 81952 | tf_op jit(solution)/shard_map/ppermute | solution.py:182
  16.6 1.5 %collective-permute-start.6 = (bf16[160,256]{1,0:T(8,128)(2,1)S(1)}, bf16[160,256]{1,0:T(8,128)(2,1)S(1)}, u32[]{:S(2)}, u32[]{:S(2)}) collective-permute-start(bf16[160,256]{1,0:T(8,128)(2,1)S(1)} %collective-permute-done.5.refs_0_), channel_id=1, source_target_pairs={{0,8},{4,12},{8,0},{12,4},{16,24},{20,28},{24,16},{28,20},{1,9},{5... | collective-permute-start | bytes 245768 | tf_op jit(solution)/shard_map/ppermute | solution.py:177
  18.1 1.5 %collective-permute-start.7 = (bf16[160,256]{1,0:T(8,128)(2,1)S(1)}, bf16[160,256]{1,0:T(8,128)(2,1)S(1)}, u32[]{:S(2)}, u32[]{:S(2)}) collective-permute-start(bf16[160,256]{1,0:T(8,128)(2,1)S(1)} %collective-permute-done.5.refs_0_), channel_id=1, source_target_pairs={{0,16},{4,20},{8,24},{12,28},{16,0},{20,4},{24,8},{28,12},{1,17},{... | collective-permute-start | bytes 245768 | tf_op jit(solution)/shard_map/ppermute | solution.py:177
  20.1 1.7 %collective-permute-done.6.refs_1_ = bf16[160,256]{1,0:T(8,128)(2,1)S(1)} collective-permute-done((bf16[160,256]{1,0:T(8,128)(2,1)S(1)}, bf16[160,256]{1,0:T(8,128)(2,1)S(1)}, u32[]{:S(2)}, u32[]{:S(2)}) %collective-permute-start.6) | collective-permute-done | bytes 81952 | tf_op jit(solution)/shard_map/ppermute | solution.py:177
  21.9 1.4 %collective-permute-done.7.refs_2_ = bf16[160,256]{1,0:T(8,128)(2,1)S(1)} collective-permute-done((bf16[160,256]{1,0:T(8,128)(2,1)S(1)}, bf16[160,256]{1,0:T(8,128)(2,1)S(1)}, u32[]{:S(2)}, u32[]{:S(2)}) %collective-permute-start.7) | collective-permute-done | bytes 81952 | tf_op jit(solution)/shard_map/ppermute | solution.py:177
  23.2 1.7 %collective-permute-done.8.refs_3_ = bf16[160,256]{1,0:T(8,128)(2,1)S(1)} collective-permute-done((bf16[160,256]{1,0:T(8,128)(2,1)S(1)}, bf16[160,256]{1,0:T(8,128)(2,1)S(1)}, u32[]{:S(2)}, u32[]{:S(2)}) %collective-permute-start.8) | collective-permute-done | bytes 81952 | tf_op jit(solution)/shard_map/ppermute | solution.py:177
  25.0 0.8 %slice.3 = bf16[8,2048]{1,0:T(8,128)(2,1)S(1)} slice(bf16[128,2048]{1,0:T(8,128)(2,1)} %tokens_ref.3), slice={[120:128], [0:2048]} | slice | bytes 65536 | tf_op jit(solution)/shard_map/slice | solution.py:187
  26.4 0.7 %collective-permute-start.1 = (bf16[8,2048]{1,0:T(8,128)(2,1)S(1)}, bf16[8,2048]{1,0:T(8,128)(2,1)S(1)}, u32[]{:S(2)}, u32[]{:S(2)}) collective-permute-start(bf16[8,2048]{1,0:T(8,128)(2,1)S(1)} %slice.3), channel_id=1, source_target_pairs={{3,5},{7,9},{11,13},{15,17},{19,21},{23,25},{27,29}} | collective-permute-start | bytes 98312 | tf_op jit(solution)/shard_map/ppermute | solution.py:191
  27.1 0.7 %collective-permute-start.2 = (bf16[8,2048]{1,0:T(8,128)(2,1)S(1)}, bf16[8,2048]{1,0:T(8,128)(2,1)S(1)}, u32[]{:S(2)}, u32[]{:S(2)}) collective-permute-start(bf16[8,2048]{1,0:T(8,128)(2,1)S(1)} %slice.3), channel_id=1, source_target_pairs={{3,6},{7,10},{11,14},{15,18},{19,22},{23,26},{27,30}} | collective-permute-start | bytes 98312 | tf_op jit(solution)/shard_map/ppermute | solution.py:191
  29.3 1.1 %copy-done = bf16[2048,160]{0,1:T(8,128)(2,1)S(1)} copy-done((bf16[2048,160]{0,1:T(8,128)(2,1)S(1)}, bf16[2048,160]{0,1:T(8,128)(2,1)}, u32[]{:S(2)}) %copy-start) | copy-done | bytes 655384
  30.4 1.0 %copy-done.2 = bf16[128,2048]{1,0:T(8,128)(2,1)S(1)} copy-done((bf16[128,2048]{1,0:T(8,128)(2,1)S(1)}, bf16[128,2048]{1,0:T(8,128)(2,1)}, u32[]{:S(2)}) %copy-start.2) | copy-done | bytes 524312
  31.8 0.7 %copy-done.3 = bf16[128,2048]{1,0:T(8,128)(2,1)S(1)} copy-done((bf16[128,2048]{1,0:T(8,128)(2,1)S(1)}, bf16[128,2048]{1,0:T(8,128)(2,1)}, u32[]{:S(2)}) %copy-start.3) | copy-done | bytes 524312
  32.8 6.2 %collective-permute-start.13 = (bf16[160,128]{1,0:T(8,128)(2,1)S(1)}, bf16[160,128]{1,0:T(8,128)(2,1)S(1)}, u32[]{:S(2)}, u32[]{:S(2)}) collective-permute-start(bf16[160,128]{1,0:T(8,128)(2,1)S(1)} %shard_map.40), channel_id=1, source_target_pairs={{0,2},{1,3},{2,0},{3,1},{4,6},{5,7},{6,4},{7,5},{8,10},{9,11},{10,... | collective-permute-start | bytes 122888 | tf_op jit(solution)/shard_map/ppermute | solution.py:207
  40.0 1.4 %collective-permute-done.13.refs_2_ = bf16[160,128]{1,0:T(8,128)(2,1)S(1)} collective-permute-done((bf16[160,128]{1,0:T(8,128)(2,1)S(1)}, bf16[160,128]{1,0:T(8,128)(2,1)S(1)}, u32[]{:S(2)}, u32[]{:S(2)}) %collective-permute-start.13) | collective-permute-done | bytes 40992 | tf_op jit(solution)/shard_map/ppermute | solution.py:207
  41.4 3.1 %collective-permute-done.14.refs_3_ = bf16[160,128]{1,0:T(8,128)(2,1)S(1)} collective-permute-done((bf16[160,128]{1,0:T(8,128)(2,1)S(1)}, bf16[160,128]{1,0:T(8,128)(2,1)S(1)}, u32[]{:S(2)}, u32[]{:S(2)}) %collective-permute-start.14) | collective-permute-done | bytes 40992 | tf_op jit(solution)/shard_map/ppermute | solution.py:207
  44.5 1.2 %shard_map.41 = (bf16[512,160]{1,0:T(8,128)(2,1)S(1)}, bf16[160,512]{1,0:T(8,128)(2,1)S(1)}, bf16[128,512]{1,0:T(8,128)(2,1)S(1)}, f32[168,128]{1,0:T(8,128)S(1)}) custom-call(s32[4]{0:T(128)S(1)} %pad_add_fusion.place_ref, f32[160,4]{1,0:T(8,128)S(1)} %bitcast.12, bf16[160,128]{1,0:T(8,128)(2,1)S(1)} %shard_map.37.halo_ref, ...), custom_call_target="tpu_custom_call" | custom-call | flops 1048576 | bytes 1048576 | tf_op jit(solution)/shard_map/pallas_call | solution.py:27
  45.8 1.3 %collective-permute-done.15 = f32[168,128]{1,0:T(8,128)S(1)} collective-permute-done((f32[168,128]{1,0:T(8,128)S(1)}, f32[168,128]{1,0:T(8,128)S(1)}, u32[]{:S(2)}, u32[]{:S(2)}) %collective-permute-start.15) | collective-permute-done | bytes 86048 | tf_op jit(solution)/shard_map/ppermute | solution.py:177
  48.3 2.4 %collective-permute-start.17 = (f32[168,128]{1,0:T(8,128)S(1)}, f32[168,128]{1,0:T(8,128)S(1)}, u32[]{:S(2)}, u32[]{:S(2)}) collective-permute-start(f32[168,128]{1,0:T(8,128)S(1)} %get-tuple-element.21), channel_id=1, source_target_pairs={{0,16},{4,20},{8,24},{12,28},{16,0},{20,4},{24,8},{28,12},{1,17},{... | collective-permute-start | bytes 258056 | tf_op jit(solution)/shard_map/ppermute | solution.py:239
  51.4 1.4 %collective-permute-done.18 = f32[168,128]{1,0:T(8,128)S(1)} collective-permute-done((f32[168,128]{1,0:T(8,128)S(1)}, f32[168,128]{1,0:T(8,128)S(1)}, u32[]{:S(2)}, u32[]{:S(2)}) %collective-permute-start.18) | collective-permute-done | bytes 86048 | tf_op jit(solution)/shard_map/ppermute | solution.py:239
  52.8 1.7 %collective-permute-done.17 = f32[168,128]{1,0:T(8,128)S(1)} collective-permute-done((f32[168,128]{1,0:T(8,128)S(1)}, f32[168,128]{1,0:T(8,128)S(1)}, u32[]{:S(2)}, u32[]{:S(2)}) %collective-permute-start.17) | collective-permute-done | bytes 86048 | tf_op jit(solution)/shard_map/ppermute | solution.py:239
  54.5 0.7 %collective-permute-done.16 = f32[168,128]{1,0:T(8,128)S(1)} collective-permute-done((f32[168,128]{1,0:T(8,128)S(1)}, f32[168,128]{1,0:T(8,128)S(1)}, u32[]{:S(2)}, u32[]{:S(2)}) %collective-permute-start.16) | collective-permute-done | bytes 86048 | tf_op jit(solution)/shard_map/ppermute | solution.py:239
  55.3 1.0 %shard_map.43 = bf16[512,128]{1,0:T(8,128)(2,1)} custom-call(bf16[512,160]{1,0:T(8,128)(2,1)S(1)} %get-tuple-element.15.query_ref, f32[512,128]{1,0:T(8,128)S(1)} %get-tuple-element.18.numerator_ref, f32[512,128]{1,0:T(8,128)S(1)} %get-tuple-element.19.denominator_ref, f32[168,128]{1,0:T(8,128)S(1)} %get-tuple-element.22.refs_0_, ...), custom_call_target="tpu_custom_call" | custom-call | flops 62914560 | bytes 1048576 | tf_op jit(solution)/shard_map/pallas_call | solution.py:27
  (40 shorter events, 6.2 us)
Async XLA Ops:
  0.0 32.8 %collective-permute-start.4 = (bf16[128,2048]{1,0:T(8,128)(2,1)}, bf16[128,2048]{1,0:T(8,128)(2,1)S(1)}, u32[]{:S(2)}, u32[]{:S(2)}) collective-permute-start(bf16[128,2048]{1,0:T(8,128)(2,1)} %tokens_ref.3), channel_id=1, source_target_pairs={{0,1},{1,0},{2,3},{3,2},{4,5},{5,4},{6,7},{7,6},{8,9},{9,8},{10,11... | collective-permute-start | bytes 1572872 | tf_op jit(solution)/shard_map/ppermute | solution.py:185
  0.9 15.7 %collective-permute-start.5 = (bf16[160,256]{1,0:T(8,128)(2,1)S(1)}, bf16[160,256]{1,0:T(8,128)(2,1)S(1)}, u32[]{:S(2)}, u32[]{:S(2)}) collective-permute-start(bf16[160,256]{1,0:T(8,128)(2,1)S(1)} %dynamic-slice_bitcast_fusion), channel_id=1, source_target_pairs={{2,0},{3,1},{0,2},{1,3},{6,4},{7,5},{4,6},{5,7},{10,8},{11,9},{8,1... | collective-permute-start | bytes 245768 | tf_op jit(solution)/shard_map/ppermute | solution.py:182
  16.6 5.2 %collective-permute-start.6 = (bf16[160,256]{1,0:T(8,128)(2,1)S(1)}, bf16[160,256]{1,0:T(8,128)(2,1)S(1)}, u32[]{:S(2)}, u32[]{:S(2)}) collective-permute-start(bf16[160,256]{1,0:T(8,128)(2,1)S(1)} %collective-permute-done.5.refs_0_), channel_id=1, source_target_pairs={{0,8},{4,12},{8,0},{12,4},{16,24},{20,28},{24,16},{28,20},{1,9},{5... | collective-permute-start | bytes 245768 | tf_op jit(solution)/shard_map/ppermute | solution.py:177
  18.1 5.1 %collective-permute-start.7 = (bf16[160,256]{1,0:T(8,128)(2,1)S(1)}, bf16[160,256]{1,0:T(8,128)(2,1)S(1)}, u32[]{:S(2)}, u32[]{:S(2)}) collective-permute-start(bf16[160,256]{1,0:T(8,128)(2,1)S(1)} %collective-permute-done.5.refs_0_), channel_id=1, source_target_pairs={{0,16},{4,20},{8,24},{12,28},{16,0},{20,4},{24,8},{28,12},{1,17},{... | collective-permute-start | bytes 245768 | tf_op jit(solution)/shard_map/ppermute | solution.py:177
  19.7 5.3 %collective-permute-start.8 = (bf16[160,256]{1,0:T(8,128)(2,1)S(1)}, bf16[160,256]{1,0:T(8,128)(2,1)S(1)}, u32[]{:S(2)}, u32[]{:S(2)}) collective-permute-start(bf16[160,256]{1,0:T(8,128)(2,1)S(1)} %collective-permute-done.5.refs_0_), channel_id=1, source_target_pairs={{0,24},{4,28},{8,16},{12,20},{16,8},{20,12},{24,0},{28,4},{1,25},{... | collective-permute-start | bytes 245768 | tf_op jit(solution)/shard_map/ppermute | solution.py:177
  20.1 5.6 %collective-permute-start.9 = (bf16[160,256]{1,0:T(8,128)(2,1)S(1)}, bf16[160,256]{1,0:T(8,128)(2,1)S(1)}, u32[]{:S(2)}, u32[]{:S(2)}) collective-permute-start(bf16[160,256]{1,0:T(8,128)(2,1)S(1)} %collective-permute-done.5.refs_0_), channel_id=1, source_target_pairs={{0,4},{4,0},{8,12},{12,8},{16,20},{20,16},{24,28},{28,24},{1,5},{5... | collective-permute-start | bytes 245768 | tf_op jit(solution)/shard_map/ppermute | solution.py:177
  21.8 4.6 %collective-permute-start.10 = (bf16[160,256]{1,0:T(8,128)(2,1)S(1)}, bf16[160,256]{1,0:T(8,128)(2,1)S(1)}, u32[]{:S(2)}, u32[]{:S(2)}) collective-permute-start(bf16[160,256]{1,0:T(8,128)(2,1)S(1)} %collective-permute-done.6.refs_1_), channel_id=1, source_target_pairs={{0,4},{4,0},{8,12},{12,8},{16,20},{20,16},{24,28},{28,24},{1,5},{5... | collective-permute-start | bytes 245768 | tf_op jit(solution)/shard_map/ppermute | solution.py:177
  23.2 3.9 %collective-permute-start.11 = (bf16[160,256]{1,0:T(8,128)(2,1)S(1)}, bf16[160,256]{1,0:T(8,128)(2,1)S(1)}, u32[]{:S(2)}, u32[]{:S(2)}) collective-permute-start(bf16[160,256]{1,0:T(8,128)(2,1)S(1)} %collective-permute-done.7.refs_2_), channel_id=1, source_target_pairs={{0,4},{4,0},{8,12},{12,8},{16,20},{20,16},{24,28},{28,24},{1,5},{5... | collective-permute-start | bytes 245768 | tf_op jit(solution)/shard_map/ppermute | solution.py:177
  25.0 2.8 %collective-permute-start.12 = (bf16[160,256]{1,0:T(8,128)(2,1)S(1)}, bf16[160,256]{1,0:T(8,128)(2,1)S(1)}, u32[]{:S(2)}, u32[]{:S(2)}) collective-permute-start(bf16[160,256]{1,0:T(8,128)(2,1)S(1)} %collective-permute-done.8.refs_3_), channel_id=1, source_target_pairs={{0,4},{4,0},{8,12},{12,8},{16,20},{20,16},{24,28},{28,24},{1,5},{5... | collective-permute-start | bytes 245768 | tf_op jit(solution)/shard_map/ppermute | solution.py:177
  25.8 13.8 %collective-permute-start = (bf16[8,2048]{1,0:T(8,128)(2,1)S(1)}, bf16[8,2048]{1,0:T(8,128)(2,1)S(1)}, u32[]{:S(2)}, u32[]{:S(2)}) collective-permute-start(bf16[8,2048]{1,0:T(8,128)(2,1)S(1)} %slice.3), channel_id=1, source_target_pairs={{3,4},{7,8},{11,12},{15,16},{19,20},{23,24},{27,28}} | collective-permute-start | bytes 98312 | tf_op jit(solution)/shard_map/ppermute | solution.py:191
  26.4 13.2 %collective-permute-start.1 = (bf16[8,2048]{1,0:T(8,128)(2,1)S(1)}, bf16[8,2048]{1,0:T(8,128)(2,1)S(1)}, u32[]{:S(2)}, u32[]{:S(2)}) collective-permute-start(bf16[8,2048]{1,0:T(8,128)(2,1)S(1)} %slice.3), channel_id=1, source_target_pairs={{3,5},{7,9},{11,13},{15,17},{19,21},{23,25},{27,29}} | collective-permute-start | bytes 98312 | tf_op jit(solution)/shard_map/ppermute | solution.py:191
  27.1 12.5 %collective-permute-start.2 = (bf16[8,2048]{1,0:T(8,128)(2,1)S(1)}, bf16[8,2048]{1,0:T(8,128)(2,1)S(1)}, u32[]{:S(2)}, u32[]{:S(2)}) collective-permute-start(bf16[8,2048]{1,0:T(8,128)(2,1)S(1)} %slice.3), channel_id=1, source_target_pairs={{3,6},{7,10},{11,14},{15,18},{19,22},{23,26},{27,30}} | collective-permute-start | bytes 98312 | tf_op jit(solution)/shard_map/ppermute | solution.py:191
  27.8 11.8 %collective-permute-start.3 = (bf16[8,2048]{1,0:T(8,128)(2,1)S(1)}, bf16[8,2048]{1,0:T(8,128)(2,1)S(1)}, u32[]{:S(2)}, u32[]{:S(2)}) collective-permute-start(bf16[8,2048]{1,0:T(8,128)(2,1)S(1)} %slice.3), channel_id=1, source_target_pairs={{3,7},{7,11},{11,15},{15,19},{19,23},{23,27},{27,31}} | collective-permute-start | bytes 98312 | tf_op jit(solution)/shard_map/ppermute | solution.py:191
  28.5 0.7 %copy-start.4 = (f32[4,160]{1,0:T(4,128)S(1)}, f32[4,160]{1,0:T(4,128)}, u32[]{:S(2)}) copy-start(f32[4,160]{1,0:T(4,128)} %param.5) | copy-start | bytes 7684
  29.3 1.1 %copy-start = (bf16[2048,160]{0,1:T(8,128)(2,1)S(1)}, bf16[2048,160]{0,1:T(8,128)(2,1)}, u32[]{:S(2)}) copy-start(bf16[2048,160]{0,1:T(8,128)(2,1)} %param.4) | copy-start | bytes 1966084
  30.4 1.0 %copy-start.2 = (bf16[128,2048]{1,0:T(8,128)(2,1)S(1)}, bf16[128,2048]{1,0:T(8,128)(2,1)}, u32[]{:S(2)}) copy-start(bf16[128,2048]{1,0:T(8,128)(2,1)} %tokens_ref.3) | copy-start | bytes 1572868
  31.4 1.0 %copy-start.3 = (bf16[128,2048]{1,0:T(8,128)(2,1)S(1)}, bf16[128,2048]{1,0:T(8,128)(2,1)}, u32[]{:S(2)}) copy-start(bf16[128,2048]{1,0:T(8,128)(2,1)} %tokens_ref.3) | copy-start | bytes 1572868
  31.8 7.3 %copy-start.1 = (bf16[2048,160]{0,1:T(8,128)(2,1)S(1)}, bf16[2048,160]{0,1:T(8,128)(2,1)}, u32[]{:S(2)}) copy-start(bf16[2048,160]{0,1:T(8,128)(2,1)} %param.4) | copy-start | bytes 1966084
  32.8 8.6 %collective-permute-start.13 = (bf16[160,128]{1,0:T(8,128)(2,1)S(1)}, bf16[160,128]{1,0:T(8,128)(2,1)S(1)}, u32[]{:S(2)}, u32[]{:S(2)}) collective-permute-start(bf16[160,128]{1,0:T(8,128)(2,1)S(1)} %shard_map.40), channel_id=1, source_target_pairs={{0,2},{1,3},{2,0},{3,1},{4,6},{5,7},{6,4},{7,5},{8,10},{9,11},{10,... | collective-permute-start | bytes 122888 | tf_op jit(solution)/shard_map/ppermute | solution.py:207
  39.5 5.0 %collective-permute-start.14 = (bf16[160,128]{1,0:T(8,128)(2,1)S(1)}, bf16[160,128]{1,0:T(8,128)(2,1)S(1)}, u32[]{:S(2)}, u32[]{:S(2)}) collective-permute-start(bf16[160,128]{1,0:T(8,128)(2,1)S(1)} %get-tuple-element.14), channel_id=1, source_target_pairs={{0,2},{1,3},{2,0},{3,1},{4,6},{5,7},{6,4},{7,5},{8,10},{9,11},{10,... | collective-permute-start | bytes 122888 | tf_op jit(solution)/shard_map/ppermute | solution.py:207
  45.7 1.3 %collective-permute-start.15 = (f32[168,128]{1,0:T(8,128)S(1)}, f32[168,128]{1,0:T(8,128)S(1)}, u32[]{:S(2)}, u32[]{:S(2)}) collective-permute-start(f32[168,128]{1,0:T(8,128)S(1)} %get-tuple-element.20), channel_id=1, source_target_pairs={{0,4},{4,0},{8,12},{12,8},{16,20},{20,16},{24,28},{28,24},{1,5},{5... | collective-permute-start | bytes 258056 | tf_op jit(solution)/shard_map/ppermute | solution.py:177
  47.1 5.7 %collective-permute-start.18 = (f32[168,128]{1,0:T(8,128)S(1)}, f32[168,128]{1,0:T(8,128)S(1)}, u32[]{:S(2)}, u32[]{:S(2)}) collective-permute-start(f32[168,128]{1,0:T(8,128)S(1)} %get-tuple-element.21), channel_id=1, source_target_pairs={{0,24},{4,28},{8,16},{12,20},{16,8},{20,12},{24,0},{28,4},{1,25},{... | collective-permute-start | bytes 258056 | tf_op jit(solution)/shard_map/ppermute | solution.py:239
  48.3 6.2 %collective-permute-start.17 = (f32[168,128]{1,0:T(8,128)S(1)}, f32[168,128]{1,0:T(8,128)S(1)}, u32[]{:S(2)}, u32[]{:S(2)}) collective-permute-start(f32[168,128]{1,0:T(8,128)S(1)} %get-tuple-element.21), channel_id=1, source_target_pairs={{0,16},{4,20},{8,24},{12,28},{16,0},{20,4},{24,8},{28,12},{1,17},{... | collective-permute-start | bytes 258056 | tf_op jit(solution)/shard_map/ppermute | solution.py:239
  50.8 4.5 %collective-permute-start.16 = (f32[168,128]{1,0:T(8,128)S(1)}, f32[168,128]{1,0:T(8,128)S(1)}, u32[]{:S(2)}, u32[]{:S(2)}) collective-permute-start(f32[168,128]{1,0:T(8,128)S(1)} %get-tuple-element.21), channel_id=1, source_target_pairs={{0,8},{4,12},{8,0},{12,4},{16,24},{20,28},{24,16},{28,20},{1,9},{5... | collective-permute-start | bytes 258056 | tf_op jit(solution)/shard_map/ppermute | solution.py:239
where the time goes:
time: 56.7 us; the launch traced here: 56.3 us
  waiting for transfers between devices  27.2 us (48%)
  starting transfers between devices  19.2 us (34%)
  local copies, waits for them, and re-layouts  5.19 us (9%)
  Pallas kernels  4.43 us (8%)
    ppermute x1, waiting for transfers between devices, per_device(): lax.ppermute(mine, 'tp', [((z + 2 * turn) % tp, z) for z in range(tp)])  12.7 us
    ppermute x2, starting transfers between devices, per_device(): blocks += [lax.ppermute(one, 'tp', pairs), lax.ppermute(two, 'tp', pairs)]  6.28 us
    ppermute x8, waiting for transfers between devices, swap(): return lax.ppermute(array, 'ctx', [(i, i ^ bit) for i in range(ctx)])  6.12 us
    ppermute x2, waiting for transfers between devices, per_device(): blocks += [lax.ppermute(one, 'tp', pairs), lax.ppermute(two, 'tp', pairs)]  4.5 us
    pallas_call x7, Pallas kernels, call(): pl.pallas_call(kernel, out_shape=outs, in_specs=[SMEM] * scalars + [VMEM]...  4.43 us
    ppermute x3, waiting for transfers between devices, per_device(): parts.append(lax.ppermute(total, 'ctx', pairs))  3.87 us
    ppermute x3, starting transfers between devices, per_device(): parts.append(lax.ppermute(total, 'ctx', pairs))  3.62 us
    ppermute x8, starting transfers between devices, swap(): return lax.ppermute(array, 'ctx', [(i, i ^ bit) for i in range(ctx)])  3.57 us
  transfers between devices with their start and end apart: 19, of which 10 were waited for; matrix products, arithmetic and copies ran while one was open for 3% of the time, Pallas kernels for 4%

commit v1 on v0

--- a/solution.py
+++ b/solution.py
@@ -18,16 +18,17 @@
 STATE_ROWS = NUM_FEAT + 8
 F32 = jnp.float32
 BF16 = jnp.bfloat16
+HBM = pl.BlockSpec(memory_space=pltpu.HBM)
 VMEM = pl.BlockSpec(memory_space=pltpu.VMEM)
 SMEM = pl.BlockSpec(memory_space=pltpu.SMEM)
 LAST = (((1,), (1,)), ((), ()))
 
 
-def call(kernel, outs, operands, scalars=0, scratch=(), flops=1 << 20, moved=1 << 20):
+def call(kernel, outs, operands, scalars=0, scratch=(), flops=1 << 20, moved=1 << 20, space=VMEM):
     return pl.pallas_call(
         kernel,
         out_shape=outs,
-        in_specs=[SMEM] * scalars + [VMEM] * (len(operands) - scalars),
+        in_specs=[SMEM] * scalars + [space] * (len(operands) - scalars),
         out_specs=[VMEM] * len(outs),
         scratch_shapes=list(scratch),
         compiler_params=pltpu.CompilerParams(vmem_limit_bytes=16 << 20),
@@ -39,15 +40,23 @@
     return lax.dot_general(left, right, LAST, preferred_element_type=F32)
 
 
-def own_kernel(tokens_ref, weight_ref, own_ref):
-    own_ref[...] = dot_last(weight_ref[...], tokens_ref[...]).astype(BF16)
-
-
-def halo_kernel(tail_ref, weight_ref, halo_ref):
+def fetch_kernel(tokens_ref, all_ref, last_ref, sems):
+    rows = tokens_ref.shape[0]
+    last = pltpu.make_async_copy(tokens_ref.at[rows - HALO :, :], last_ref, sems.at[0])
+    whole = pltpu.make_async_copy(tokens_ref, all_ref, sems.at[1])
+    last.start()
+    whole.start()
+    last.wait()
+    whole.wait()
+
+
+def own_kernel(tail_ref, tokens_ref, weight_ref, halo_ref, own_ref):
+    weight = weight_ref[...]
+    own_ref[...] = dot_last(weight, tokens_ref[...]).astype(BF16)
     padded = jnp.concatenate(
         [jnp.zeros((halo_ref.shape[1] - HALO, tail_ref.shape[1]), BF16), tail_ref[...]], axis=0
     )
-    halo_ref[...] = dot_last(weight_ref[...], padded).astype(BF16)
+    halo_ref[...] = dot_last(weight, padded).astype(BF16)
 
 
 def gathered(share, tokens_ref, pieces):
@@ -106,9 +115,10 @@
         wide[:, pl.ds(start, width)] = block[...].astype(F32)
     padded = wide[...]
     convolved = jnp.zeros((padded.shape[0], local_rows), F32)
-    for offset in range(conv_ref.shape[1]):
+    taps = conv_ref[...].T
+    for offset in range(taps.shape[1]):
         moved = pltpu.roll(padded, offset, 1) if offset else padded
-        convolved += conv_ref[:, offset : offset + 1] * moved[:, width:]
+        convolved += taps[:, offset : offset + 1] * moved[:, width:]
     value = convolved[2 * FEAT :].astype(BF16)
     value_ref[...] = value
     query = features(convolved[:FEAT], False)
@@ -176,6 +186,7 @@
     def swap(array, bit):
         return lax.ppermute(array, "ctx", [(i, i ^ bit) for i in range(ctx)])
 
+    side = share.astype(jnp.int32).reshape(1)
     mine = lax.dynamic_slice(weight, (0, share * piece), (row_width, piece))
     pieces = []
     for turn in turns:
@@ -184,7 +195,14 @@
         pieces += parts + [swap(part, 1) for part in parts]
     paired = lax.ppermute(tokens, "tp", [(z, z ^ 1) for z in range(tp)])
 
-    last_rows = tokens[rows - HALO :]
+    held, last_rows = call(
+        fetch_kernel,
+        [tokens, jax.ShapeDtypeStruct((HALO, depth), BF16)],
+        [tokens],
+        0,
+        [pltpu.SemaphoreType.DMA((2,))],
+        space=HBM,
+    )
     tail = None
     for z in range(tp):
         pairs = [((c - 1) * tp + tp - 1, c * tp + z) for c in range(1, ctx)]
@@ -193,10 +211,8 @@
 
     shape = jax.ShapeDtypeStruct((row_width, rows), BF16)
     work = 2 * rows * depth * row_width
-    side = share.astype(jnp.int32).reshape(1)
-    own = call(own_kernel, [shape], [tokens, weight], flops=work)[0]
-    halo = call(halo_kernel, [shape], [tail, weight], flops=work)[0]
-    early = call(early_kernel, [shape] * len(turns), [side, tokens] + pieces, 1, flops=work)
+    halo, own = call(own_kernel, [shape] * 2, [tail, held, weight], flops=2 * work)
+    early = call(early_kernel, [shape] * len(turns), [side, held] + pieces, 1, flops=work)
     *late, other = call(
         late_kernel, [shape] * (len(turns) + 1), [side, paired, weight] + pieces, 1, flops=2 * work
     )
@@ -215,7 +231,7 @@
             jax.ShapeDtypeStruct((val_width, local_rows), BF16),
             jax.ShapeDtypeStruct((STATE_ROWS, val_width), F32),
         ],
-        [place, conv_weight.T, halo] + blocks,
+        [place, conv_weight, halo] + blocks,
         1,
         [pltpu.VMEM((row_width, rows + local_rows), F32)],
     )

time: 56.7 us -> 51.1 us (0.901)
  the two profiles are of different devices: /device:TPU:8 before, /device:TPU:0 now
where the time goes in v1:
time: 51.1 us; the launch traced here: 50.9 us
  waiting for transfers between devices  24.7 us (48%)
  starting transfers between devices  19.5 us (38%)
  Pallas kernels  4.44 us (9%)
  local copies, waits for them, and re-layouts  1.95 us (4%)
    ppermute x1, waiting for transfers between devices, per_device(): lax.ppermute(mine, 'tp', [((z + 2 * turn) % tp, z) for z in range(tp)])  9.67 us
    ppermute x2, waiting for transfers between devices, per_device(): blocks += [lax.ppermute(one, 'tp', pairs), lax.ppermute(two, 'tp', pairs)]  6.2 us
    ppermute x8, waiting for transfers between devices, swap(): return lax.ppermute(array, 'ctx', [(i, i ^ bit) for i in range(ctx)])  5.16 us
    pallas_call x7, Pallas kernels, call(): pl.pallas_call(kernel, out_shape=outs, in_specs=[SMEM] * scalars + [space...  4.44 us
    ppermute x3, starting transfers between devices, per_device(): parts.append(lax.ppermute(total, 'ctx', pairs))  3.93 us
    ppermute x3, waiting for transfers between devices, per_device(): parts.append(lax.ppermute(total, 'ctx', pairs))  3.64 us
    ppermute x8, starting transfers between devices, swap(): return lax.ppermute(array, 'ctx', [(i, i ^ bit) for i in range(ctx)])  3.57 us
    ppermute x2, starting transfers between devices, per_device(): blocks += [lax.ppermute(one, 'tp', pairs), lax.ppermute(two, 'tp', pairs)]  3.56 us
  transfers between devices with their start and end apart: 19, of which 10 were waited for; matrix products, arithmetic and copies ran while one was open for 2% of the time, Pallas kernels for 4%

profile of v1, /device:TPU:0, one launch (start us, length us, event | category | flops | bytes accessed | tf_op | source)
XLA Modules:
  0.0 50.9 jit_solution(7452592345816776693)
XLA Ops:
  0.0 3.1 %collective-permute-start.4 = (bf16[128,2048]{1,0:T(8,128)(2,1)}, bf16[128,2048]{1,0:T(8,128)(2,1)S(1)}, u32[]{:S(2)}, u32[]{:S(2)}) collective-permute-start(bf16[128,2048]{1,0:T(8,128)(2,1)} %tokens_ref.1), channel_id=1, source_target_pairs={{0,1},{1,0},{2,3},{3,2},{4,5},{5,4},{6,7},{7,6},{8,9},{9,8},{10,11... | collective-permute-start | bytes 1572872 | tf_op jit(solution)/shard_map/ppermute | solution.py:196
  3.1 0.9 %dynamic-slice_bitcast_fusion = bf16[160,256]{1,0:T(8,128)(2,1)S(1)} fusion(bf16[2048,160]{0,1:T(8,128)(2,1)} %param.4, s32[]{:T(128)S(6)} %select_n.49), kind=kLoop, calls=%fused_computation | loop fusion | bytes 163844 | tf_op jit(solution)/shard_map/dynamic_slice | solution.py:190
  3.9 2.6 %collective-permute-start.5 = (bf16[160,256]{1,0:T(8,128)(2,1)S(1)}, bf16[160,256]{1,0:T(8,128)(2,1)S(1)}, u32[]{:S(2)}, u32[]{:S(2)}) collective-permute-start(bf16[160,256]{1,0:T(8,128)(2,1)S(1)} %dynamic-slice_bitcast_fusion), channel_id=1, source_target_pairs={{2,0},{3,1},{0,2},{1,3},{6,4},{7,5},{4,6},{5,7},{10,8},{11,9},{8,1... | collective-permute-start | bytes 245768 | tf_op jit(solution)/shard_map/ppermute | solution.py:193
  6.5 9.7 %collective-permute-done.5.refs_0_ = bf16[160,256]{1,0:T(8,128)(2,1)S(1)} collective-permute-done((bf16[160,256]{1,0:T(8,128)(2,1)S(1)}, bf16[160,256]{1,0:T(8,128)(2,1)S(1)}, u32[]{:S(2)}, u32[]{:S(2)}) %collective-permute-start.5) | collective-permute-done | bytes 81952 | tf_op jit(solution)/shard_map/ppermute | solution.py:193
  16.2 2.4 %collective-permute-start.8 = (bf16[160,256]{1,0:T(8,128)(2,1)S(1)}, bf16[160,256]{1,0:T(8,128)(2,1)S(1)}, u32[]{:S(2)}, u32[]{:S(2)}) collective-permute-start(bf16[160,256]{1,0:T(8,128)(2,1)S(1)} %collective-permute-done.5.refs_0_), channel_id=1, source_target_pairs={{0,24},{4,28},{8,16},{12,20},{16,8},{20,12},{24,0},{28,4},{1,25},{... | collective-permute-start | bytes 245768 | tf_op jit(solution)/shard_map/ppermute | solution.py:187
  19.7 2.3 %collective-permute-done.8.refs_3_ = bf16[160,256]{1,0:T(8,128)(2,1)S(1)} collective-permute-done((bf16[160,256]{1,0:T(8,128)(2,1)S(1)}, bf16[160,256]{1,0:T(8,128)(2,1)S(1)}, u32[]{:S(2)}, u32[]{:S(2)}) %collective-permute-start.8) | collective-permute-done | bytes 81952 | tf_op jit(solution)/shard_map/ppermute | solution.py:187
  22.0 1.1 %collective-permute-done.7.refs_2_ = bf16[160,256]{1,0:T(8,128)(2,1)S(1)} collective-permute-done((bf16[160,256]{1,0:T(8,128)(2,1)S(1)}, bf16[160,256]{1,0:T(8,128)(2,1)S(1)}, u32[]{:S(2)}, u32[]{:S(2)}) %collective-permute-start.7) | collective-permute-done | bytes 81952 | tf_op jit(solution)/shard_map/ppermute | solution.py:187
  23.6 1.0 %copy-done.1 = bf16[128,2048]{1,0:T(8,128)(2,1)S(1)} copy-done((bf16[128,2048]{1,0:T(8,128)(2,1)S(1)}, bf16[128,2048]{1,0:T(8,128)(2,1)}, u32[]{:S(2)}) %copy-start.1) | copy-done | bytes 524312
  24.7 0.8 %collective-permute-start.3 = (bf16[8,2048]{1,0:T(8,128)(2,1)S(1)}, bf16[8,2048]{1,0:T(8,128)(2,1)S(1)}, u32[]{:S(2)}, u32[]{:S(2)}) collective-permute-start(bf16[8,2048]{1,0:T(8,128)(2,1)S(1)} %get-tuple-element.17), channel_id=1, source_target_pairs={{3,7},{7,11},{11,15},{15,19},{19,23},{23,27},{27,31}} | collective-permute-start | bytes 98312 | tf_op jit(solution)/shard_map/ppermute | solution.py:209
  25.6 0.7 %collective-permute-start.2 = (bf16[8,2048]{1,0:T(8,128)(2,1)S(1)}, bf16[8,2048]{1,0:T(8,128)(2,1)S(1)}, u32[]{:S(2)}, u32[]{:S(2)}) collective-permute-start(bf16[8,2048]{1,0:T(8,128)(2,1)S(1)} %get-tuple-element.17), channel_id=1, source_target_pairs={{3,6},{7,10},{11,14},{15,18},{19,22},{23,26},{27,30}} | collective-permute-start | bytes 98312 | tf_op jit(solution)/shard_map/ppermute | solution.py:209
  26.2 0.7 %collective-permute-start.1 = (bf16[8,2048]{1,0:T(8,128)(2,1)S(1)}, bf16[8,2048]{1,0:T(8,128)(2,1)S(1)}, u32[]{:S(2)}, u32[]{:S(2)}) collective-permute-start(bf16[8,2048]{1,0:T(8,128)(2,1)S(1)} %get-tuple-element.17), channel_id=1, source_target_pairs={{3,5},{7,9},{11,13},{15,17},{19,21},{23,25},{27,29}} | collective-permute-start | bytes 98312 | tf_op jit(solution)/shard_map/ppermute | solution.py:209
  26.9 0.7 %collective-permute-start = (bf16[8,2048]{1,0:T(8,128)(2,1)S(1)}, bf16[8,2048]{1,0:T(8,128)(2,1)S(1)}, u32[]{:S(2)}, u32[]{:S(2)}) collective-permute-start(bf16[8,2048]{1,0:T(8,128)(2,1)S(1)} %get-tuple-element.17), channel_id=1, source_target_pairs={{3,4},{7,8},{11,12},{15,16},{19,20},{23,24},{27,28}} | collective-permute-start | bytes 98312 | tf_op jit(solution)/shard_map/ppermute | solution.py:209
  28.0 3.5 %collective-permute-start.13 = (bf16[160,128]{1,0:T(8,128)(2,1)S(1)}, bf16[160,128]{1,0:T(8,128)(2,1)S(1)}, u32[]{:S(2)}, u32[]{:S(2)}) collective-permute-start(bf16[160,128]{1,0:T(8,128)(2,1)S(1)} %shard_map.40), channel_id=1, source_target_pairs={{0,2},{1,3},{2,0},{3,1},{4,6},{5,7},{6,4},{7,5},{8,10},{9,11},{10,... | collective-permute-start | bytes 122888 | tf_op jit(solution)/shard_map/ppermute | solution.py:223
  32.7 0.8 %collective-permute-done.13.refs_2_ = bf16[160,128]{1,0:T(8,128)(2,1)S(1)} collective-permute-done((bf16[160,128]{1,0:T(8,128)(2,1)S(1)}, bf16[160,128]{1,0:T(8,128)(2,1)S(1)}, u32[]{:S(2)}, u32[]{:S(2)}) %collective-permute-start.13) | collective-permute-done | bytes 40992 | tf_op jit(solution)/shard_map/ppermute | solution.py:223
  33.5 5.4 %collective-permute-done.14.refs_3_ = bf16[160,128]{1,0:T(8,128)(2,1)S(1)} collective-permute-done((bf16[160,128]{1,0:T(8,128)(2,1)S(1)}, bf16[160,128]{1,0:T(8,128)(2,1)S(1)}, u32[]{:S(2)}, u32[]{:S(2)}) %collective-permute-start.14) | collective-permute-done | bytes 40992 | tf_op jit(solution)/shard_map/ppermute | solution.py:223
  38.9 1.3 %shard_map.41 = (bf16[512,160]{1,0:T(8,128)(2,1)S(1)}, bf16[160,512]{1,0:T(8,128)(2,1)S(1)}, bf16[128,512]{1,0:T(8,128)(2,1)S(1)}, f32[168,128]{1,0:T(8,128)S(1)}) custom-call(s32[4]{0:T(128)S(1)} %pad_add_fusion.place_ref, f32[4,160]{1,0:T(4,128)S(1)} %copy-done.2, bf16[160,128]{1,0:T(8,128)(2,1)S(1)} %get-tuple-element.19.halo_ref, ...), custom_call_target="tpu_custom_call" | custom-call | flops 1048576 | bytes 1048576 | tf_op jit(solution)/shard_map/pallas_call | solution.py:28
  40.3 1.3 %collective-permute-done.15 = f32[168,128]{1,0:T(8,128)S(1)} collective-permute-done((f32[168,128]{1,0:T(8,128)S(1)}, f32[168,128]{1,0:T(8,128)S(1)}, u32[]{:S(2)}, u32[]{:S(2)}) %collective-permute-start.15) | collective-permute-done | bytes 86048 | tf_op jit(solution)/shard_map/ppermute | solution.py:187
  41.6 1.4 %collective-permute-start.18 = (f32[168,128]{1,0:T(8,128)S(1)}, f32[168,128]{1,0:T(8,128)S(1)}, u32[]{:S(2)}, u32[]{:S(2)}) collective-permute-start(f32[168,128]{1,0:T(8,128)S(1)} %get-tuple-element.29), channel_id=1, source_target_pairs={{0,24},{4,28},{8,16},{12,20},{16,8},{20,12},{24,0},{28,4},{1,25},{... | collective-permute-start | bytes 258056 | tf_op jit(solution)/shard_map/ppermute | solution.py:255
  43.6 1.1 %collective-permute-start.17 = (f32[168,128]{1,0:T(8,128)S(1)}, f32[168,128]{1,0:T(8,128)S(1)}, u32[]{:S(2)}, u32[]{:S(2)}) collective-permute-start(f32[168,128]{1,0:T(8,128)S(1)} %get-tuple-element.29), channel_id=1, source_target_pairs={{0,16},{4,20},{8,24},{12,28},{16,0},{20,4},{24,8},{28,12},{1,17},{... | collective-permute-start | bytes 258056 | tf_op jit(solution)/shard_map/ppermute | solution.py:255
  44.7 1.4 %collective-permute-start.16 = (f32[168,128]{1,0:T(8,128)S(1)}, f32[168,128]{1,0:T(8,128)S(1)}, u32[]{:S(2)}, u32[]{:S(2)}) collective-permute-start(f32[168,128]{1,0:T(8,128)S(1)} %get-tuple-element.29), channel_id=1, source_target_pairs={{0,8},{4,12},{8,0},{12,4},{16,24},{20,28},{24,16},{28,20},{1,9},{5... | collective-permute-start | bytes 258056 | tf_op jit(solution)/shard_map/ppermute | solution.py:255
  46.2 1.1 %collective-permute-done.18 = f32[168,128]{1,0:T(8,128)S(1)} collective-permute-done((f32[168,128]{1,0:T(8,128)S(1)}, f32[168,128]{1,0:T(8,128)S(1)}, u32[]{:S(2)}, u32[]{:S(2)}) %collective-permute-start.18) | collective-permute-done | bytes 86048 | tf_op jit(solution)/shard_map/ppermute | solution.py:255
  47.3 1.7 %collective-permute-done.17 = f32[168,128]{1,0:T(8,128)S(1)} collective-permute-done((f32[168,128]{1,0:T(8,128)S(1)}, f32[168,128]{1,0:T(8,128)S(1)}, u32[]{:S(2)}, u32[]{:S(2)}) %collective-permute-start.17) | collective-permute-done | bytes 86048 | tf_op jit(solution)/shard_map/ppermute | solution.py:255
  49.0 0.8 %collective-permute-done.16 = f32[168,128]{1,0:T(8,128)S(1)} collective-permute-done((f32[168,128]{1,0:T(8,128)S(1)}, f32[168,128]{1,0:T(8,128)S(1)}, u32[]{:S(2)}, u32[]{:S(2)}) %collective-permute-start.16) | collective-permute-done | bytes 86048 | tf_op jit(solution)/shard_map/ppermute | solution.py:255
  49.8 1.0 %shard_map.43 = bf16[512,128]{1,0:T(8,128)(2,1)} custom-call(bf16[512,160]{1,0:T(8,128)(2,1)S(1)} %get-tuple-element.23.query_ref, f32[512,128]{1,0:T(8,128)S(1)} %get-tuple-element.26.numerator_ref, f32[512,128]{1,0:T(8,128)S(1)} %get-tuple-element.27.denominator_ref, f32[168,128]{1,0:T(8,128)S(1)} %get-tuple-element.30.refs_0_, ...), custom_call_target="tpu_custom_call" | custom-call | flops 62914560 | bytes 1048576 | tf_op jit(solution)/shard_map/pallas_call | solution.py:28
  (34 shorter events, 3.9 us)
Async XLA Ops:
  0.0 28.0 %collective-permute-start.4 = (bf16[128,2048]{1,0:T(8,128)(2,1)}, bf16[128,2048]{1,0:T(8,128)(2,1)S(1)}, u32[]{:S(2)}, u32[]{:S(2)}) collective-permute-start(bf16[128,2048]{1,0:T(8,128)(2,1)} %tokens_ref.1), channel_id=1, source_target_pairs={{0,1},{1,0},{2,3},{3,2},{4,5},{5,4},{6,7},{7,6},{8,9},{9,8},{10,11... | collective-permute-start | bytes 1572872 | tf_op jit(solution)/shard_map/ppermute | solution.py:196
  3.9 12.3 %collective-permute-start.5 = (bf16[160,256]{1,0:T(8,128)(2,1)S(1)}, bf16[160,256]{1,0:T(8,128)(2,1)S(1)}, u32[]{:S(2)}, u32[]{:S(2)}) collective-permute-start(bf16[160,256]{1,0:T(8,128)(2,1)S(1)} %dynamic-slice_bitcast_fusion), channel_id=1, source_target_pairs={{2,0},{3,1},{0,2},{1,3},{6,4},{7,5},{4,6},{5,7},{10,8},{11,9},{8,1... | collective-permute-start | bytes 245768 | tf_op jit(solution)/shard_map/ppermute | solution.py:193
  16.2 5.8 %collective-permute-start.8 = (bf16[160,256]{1,0:T(8,128)(2,1)S(1)}, bf16[160,256]{1,0:T(8,128)(2,1)S(1)}, u32[]{:S(2)}, u32[]{:S(2)}) collective-permute-start(bf16[160,256]{1,0:T(8,128)(2,1)S(1)} %collective-permute-done.5.refs_0_), channel_id=1, source_target_pairs={{0,24},{4,28},{8,16},{12,20},{16,8},{20,12},{24,0},{28,4},{1,25},{... | collective-permute-start | bytes 245768 | tf_op jit(solution)/shard_map/ppermute | solution.py:187
  18.6 4.4 %collective-permute-start.7 = (bf16[160,256]{1,0:T(8,128)(2,1)S(1)}, bf16[160,256]{1,0:T(8,128)(2,1)S(1)}, u32[]{:S(2)}, u32[]{:S(2)}) collective-permute-start(bf16[160,256]{1,0:T(8,128)(2,1)S(1)} %collective-permute-done.5.refs_0_), channel_id=1, source_target_pairs={{0,16},{4,20},{8,24},{12,28},{16,0},{20,4},{24,8},{28,12},{1,17},{... | collective-permute-start | bytes 245768 | tf_op jit(solution)/shard_map/ppermute | solution.py:187
  19.2 4.4 %collective-permute-start.6 = (bf16[160,256]{1,0:T(8,128)(2,1)S(1)}, bf16[160,256]{1,0:T(8,128)(2,1)S(1)}, u32[]{:S(2)}, u32[]{:S(2)}) collective-permute-start(bf16[160,256]{1,0:T(8,128)(2,1)S(1)} %collective-permute-done.5.refs_0_), channel_id=1, source_target_pairs={{0,8},{4,12},{8,0},{12,4},{16,24},{20,28},{24,16},{28,20},{1,9},{5... | collective-permute-start | bytes 245768 | tf_op jit(solution)/shard_map/ppermute | solution.py:187
  19.7 5.0 %collective-permute-start.9 = (bf16[160,256]{1,0:T(8,128)(2,1)S(1)}, bf16[160,256]{1,0:T(8,128)(2,1)S(1)}, u32[]{:S(2)}, u32[]{:S(2)}) collective-permute-start(bf16[160,256]{1,0:T(8,128)(2,1)S(1)} %collective-permute-done.5.refs_0_), channel_id=1, source_target_pairs={{0,4},{4,0},{8,12},{12,8},{16,20},{20,16},{24,28},{28,24},{1,5},{5... | collective-permute-start | bytes 245768 | tf_op jit(solution)/shard_map/ppermute | solution.py:187
  22.0 3.6 %collective-permute-start.12 = (bf16[160,256]{1,0:T(8,128)(2,1)S(1)}, bf16[160,256]{1,0:T(8,128)(2,1)S(1)}, u32[]{:S(2)}, u32[]{:S(2)}) collective-permute-start(bf16[160,256]{1,0:T(8,128)(2,1)S(1)} %collective-permute-done.8.refs_3_), channel_id=1, source_target_pairs={{0,4},{4,0},{8,12},{12,8},{16,20},{20,16},{24,28},{28,24},{1,5},{5... | collective-permute-start | bytes 245768 | tf_op jit(solution)/shard_map/ppermute | solution.py:187
  23.1 3.1 %collective-permute-start.11 = (bf16[160,256]{1,0:T(8,128)(2,1)S(1)}, bf16[160,256]{1,0:T(8,128)(2,1)S(1)}, u32[]{:S(2)}, u32[]{:S(2)}) collective-permute-start(bf16[160,256]{1,0:T(8,128)(2,1)S(1)} %collective-permute-done.7.refs_2_), channel_id=1, source_target_pairs={{0,4},{4,0},{8,12},{12,8},{16,20},{20,16},{24,28},{28,24},{1,5},{5... | collective-permute-start | bytes 245768 | tf_op jit(solution)/shard_map/ppermute | solution.py:187
  23.6 3.3 %collective-permute-start.10 = (bf16[160,256]{1,0:T(8,128)(2,1)S(1)}, bf16[160,256]{1,0:T(8,128)(2,1)S(1)}, u32[]{:S(2)}, u32[]{:S(2)}) collective-permute-start(bf16[160,256]{1,0:T(8,128)(2,1)S(1)} %collective-permute-done.6.refs_1_), channel_id=1, source_target_pairs={{0,4},{4,0},{8,12},{12,8},{16,20},{20,16},{24,28},{28,24},{1,5},{5... | collective-permute-start | bytes 245768 | tf_op jit(solution)/shard_map/ppermute | solution.py:187
  23.6 1.0 %copy-start.1 = (bf16[128,2048]{1,0:T(8,128)(2,1)S(1)}, bf16[128,2048]{1,0:T(8,128)(2,1)}, u32[]{:S(2)}) copy-start(bf16[128,2048]{1,0:T(8,128)(2,1)} %tokens_ref.1) | copy-start | bytes 1572868
  24.7 6.8 %copy-start = (bf16[2048,160]{0,1:T(8,128)(2,1)S(1)}, bf16[2048,160]{0,1:T(8,128)(2,1)}, u32[]{:S(2)}) copy-start(bf16[2048,160]{0,1:T(8,128)(2,1)} %param.4) | copy-start | bytes 1966084
  24.7 7.3 %collective-permute-start.3 = (bf16[8,2048]{1,0:T(8,128)(2,1)S(1)}, bf16[8,2048]{1,0:T(8,128)(2,1)S(1)}, u32[]{:S(2)}, u32[]{:S(2)}) collective-permute-start(bf16[8,2048]{1,0:T(8,128)(2,1)S(1)} %get-tuple-element.17), channel_id=1, source_target_pairs={{3,7},{7,11},{11,15},{15,19},{19,23},{23,27},{27,31}} | collective-permute-start | bytes 98312 | tf_op jit(solution)/shard_map/ppermute | solution.py:209
  25.6 6.6 %collective-permute-start.2 = (bf16[8,2048]{1,0:T(8,128)(2,1)S(1)}, bf16[8,2048]{1,0:T(8,128)(2,1)S(1)}, u32[]{:S(2)}, u32[]{:S(2)}) collective-permute-start(bf16[8,2048]{1,0:T(8,128)(2,1)S(1)} %get-tuple-element.17), channel_id=1, source_target_pairs={{3,6},{7,10},{11,14},{15,18},{19,22},{23,26},{27,30}} | collective-permute-start | bytes 98312 | tf_op jit(solution)/shard_map/ppermute | solution.py:209
  26.2 5.9 %collective-permute-start.1 = (bf16[8,2048]{1,0:T(8,128)(2,1)S(1)}, bf16[8,2048]{1,0:T(8,128)(2,1)S(1)}, u32[]{:S(2)}, u32[]{:S(2)}) collective-permute-start(bf16[8,2048]{1,0:T(8,128)(2,1)S(1)} %get-tuple-element.17), channel_id=1, source_target_pairs={{3,5},{7,9},{11,13},{15,17},{19,21},{23,25},{27,29}} | collective-permute-start | bytes 98312 | tf_op jit(solution)/shard_map/ppermute | solution.py:209
  26.9 5.2 %collective-permute-start = (bf16[8,2048]{1,0:T(8,128)(2,1)S(1)}, bf16[8,2048]{1,0:T(8,128)(2,1)S(1)}, u32[]{:S(2)}, u32[]{:S(2)}) collective-permute-start(bf16[8,2048]{1,0:T(8,128)(2,1)S(1)} %get-tuple-element.17), channel_id=1, source_target_pairs={{3,4},{7,8},{11,12},{15,16},{19,20},{23,24},{27,28}} | collective-permute-start | bytes 98312 | tf_op jit(solution)/shard_map/ppermute | solution.py:209
  28.0 5.5 %collective-permute-start.13 = (bf16[160,128]{1,0:T(8,128)(2,1)S(1)}, bf16[160,128]{1,0:T(8,128)(2,1)S(1)}, u32[]{:S(2)}, u32[]{:S(2)}) collective-permute-start(bf16[160,128]{1,0:T(8,128)(2,1)S(1)} %shard_map.40), channel_id=1, source_target_pairs={{0,2},{1,3},{2,0},{3,1},{4,6},{5,7},{6,4},{7,5},{8,10},{9,11},{10,... | collective-permute-start | bytes 122888 | tf_op jit(solution)/shard_map/ppermute | solution.py:223
  32.0 6.9 %collective-permute-start.14 = (bf16[160,128]{1,0:T(8,128)(2,1)S(1)}, bf16[160,128]{1,0:T(8,128)(2,1)S(1)}, u32[]{:S(2)}, u32[]{:S(2)}) collective-permute-start(bf16[160,128]{1,0:T(8,128)(2,1)S(1)} %get-tuple-element.22), channel_id=1, source_target_pairs={{0,2},{1,3},{2,0},{3,1},{4,6},{5,7},{6,4},{7,5},{8,10},{9,11},{10,... | collective-permute-start | bytes 122888 | tf_op jit(solution)/shard_map/ppermute | solution.py:223
  32.7 6.2 %copy-start.2 = (f32[4,160]{1,0:T(4,128)S(1)}, f32[4,160]{1,0:T(4,128)}, u32[]{:S(2)}) copy-start(f32[4,160]{1,0:T(4,128)} %conv_ref.1) | copy-start | bytes 7684
  40.2 1.3 %collective-permute-start.15 = (f32[168,128]{1,0:T(8,128)S(1)}, f32[168,128]{1,0:T(8,128)S(1)}, u32[]{:S(2)}, u32[]{:S(2)}) collective-permute-start(f32[168,128]{1,0:T(8,128)S(1)} %get-tuple-element.28), channel_id=1, source_target_pairs={{0,4},{4,0},{8,12},{12,8},{16,20},{20,16},{24,28},{28,24},{1,5},{5... | collective-permute-start | bytes 258056 | tf_op jit(solution)/shard_map/ppermute | solution.py:187
  41.6 5.7 %collective-permute-start.18 = (f32[168,128]{1,0:T(8,128)S(1)}, f32[168,128]{1,0:T(8,128)S(1)}, u32[]{:S(2)}, u32[]{:S(2)}) collective-permute-start(f32[168,128]{1,0:T(8,128)S(1)} %get-tuple-element.29), channel_id=1, source_target_pairs={{0,24},{4,28},{8,16},{12,20},{16,8},{20,12},{24,0},{28,4},{1,25},{... | collective-permute-start | bytes 258056 | tf_op jit(solution)/shard_map/ppermute | solution.py:255
  43.6 5.4 %collective-permute-start.17 = (f32[168,128]{1,0:T(8,128)S(1)}, f32[168,128]{1,0:T(8,128)S(1)}, u32[]{:S(2)}, u32[]{:S(2)}) collective-permute-start(f32[168,128]{1,0:T(8,128)S(1)} %get-tuple-element.29), channel_id=1, source_target_pairs={{0,16},{4,20},{8,24},{12,28},{16,0},{20,4},{24,8},{28,12},{1,17},{... | collective-permute-start | bytes 258056 | tf_op jit(solution)/shard_map/ppermute | solution.py:255
  44.7 5.1 %collective-permute-start.16 = (f32[168,128]{1,0:T(8,128)S(1)}, f32[168,128]{1,0:T(8,128)S(1)}, u32[]{:S(2)}, u32[]{:S(2)}) collective-permute-start(f32[168,128]{1,0:T(8,128)S(1)} %get-tuple-element.29), channel_id=1, source_target_pairs={{0,8},{4,12},{8,0},{12,4},{16,24},{20,28},{24,16},{28,20},{1,9},{5... | collective-permute-start | bytes 258056 | tf_op jit(solution)/shard_map/ppermute | solution.py:255

commit v2 on v1

--- a/solution.py
+++ b/solution.py
@@ -36,26 +36,50 @@
     )(*operands)
 
 
+def hbm(array):
+    return pltpu.with_memory_space_constraint(array, pltpu.HBM)
+
+
 def dot_last(left, right):
     return lax.dot_general(left, right, LAST, preferred_element_type=F32)
 
 
-def fetch_kernel(tokens_ref, all_ref, last_ref, sems):
-    rows = tokens_ref.shape[0]
-    last = pltpu.make_async_copy(tokens_ref.at[rows - HALO :, :], last_ref, sems.at[0])
-    whole = pltpu.make_async_copy(tokens_ref, all_ref, sems.at[1])
-    last.start()
-    whole.start()
-    last.wait()
-    whole.wait()
+def pack_kernel(share_ref, weight_ref, tokens_ref, sent_ref, tail_ref, last_ref, sems):
+    height, width = weight_ref.shape[0], sent_ref.shape[1]
+    start = pl.multiple_of(share_ref[0] * width, LANES)
+    weight_copy = pltpu.make_async_copy(
+        weight_ref.at[:, pl.ds(start, width)], sent_ref.at[:height, :], sems.at[0]
+    )
+    tokens_copy = pltpu.make_async_copy(
+        tokens_ref.at[tokens_ref.shape[0] - HALO :, :], last_ref, sems.at[1]
+    )
+    tokens_copy.start()
+    weight_copy.start()
+    tokens_copy.wait()
+    lag = tail_ref.shape[0] // PIECES
+    rows = last_ref[...].astype(F32)
+    cuts = []
+    for row in range(HALO - lag, HALO):
+        cuts += [rows[row : row + 1, index * width : index * width + width] for index in range(PIECES)]
+    tail = jnp.concatenate(cuts, axis=0).astype(BF16)
+    sent_ref[height:, :] = tail
+    tail_ref[...] = tail
+    weight_copy.wait()
 
 
 def own_kernel(tail_ref, tokens_ref, weight_ref, halo_ref, own_ref):
     weight = weight_ref[...]
+    depth = weight.shape[1]
     own_ref[...] = dot_last(weight, tokens_ref[...]).astype(BF16)
-    padded = jnp.concatenate(
-        [jnp.zeros((halo_ref.shape[1] - HALO, tail_ref.shape[1]), BF16), tail_ref[...]], axis=0
-    )
+    cuts = tail_ref[...].astype(F32)
+    lag = cuts.shape[0] // PIECES
+    rows = [jnp.zeros((halo_ref.shape[1] - lag, depth), F32)]
+    for row in range(lag):
+        first = row * PIECES
+        rows.append(
+            jnp.concatenate([cuts[first + i : first + i + 1, :] for i in range(PIECES)], axis=1)
+        )
+    padded = jnp.concatenate(rows, axis=0).astype(BF16)
     halo_ref[...] = dot_last(weight, padded).astype(BF16)
 
 
@@ -187,32 +211,37 @@
         return lax.ppermute(array, "ctx", [(i, i ^ bit) for i in range(ctx)])
 
     side = share.astype(jnp.int32).reshape(1)
-    mine = lax.dynamic_slice(weight, (0, share * piece), (row_width, piece))
+    lag = conv_weight.shape[0] - 1
+    cut_rows = PIECES * lag
+    mine, tail = call(
+        pack_kernel,
+        [
+            jax.ShapeDtypeStruct((row_width + cut_rows, piece), BF16),
+            jax.ShapeDtypeStruct((cut_rows, piece), BF16),
+        ],
+        [side, hbm(weight), hbm(tokens)],
+        1,
+        [pltpu.VMEM((HALO, depth), BF16), pltpu.SemaphoreType.DMA((2,))],
+        space=HBM,
+    )
     pieces = []
     for turn in turns:
         first = lax.ppermute(mine, "tp", [((z + 2 * turn) % tp, z) for z in range(tp)])
+        tail = jnp.where(head + 2 * turn == tp - 1, first[row_width:], tail)
+        first = first[:row_width]
         parts = [first] + [swap(first, bits) for bits in (2, 4, 6)]
         pieces += parts + [swap(part, 1) for part in parts]
     paired = lax.ppermute(tokens, "tp", [(z, z ^ 1) for z in range(tp)])
 
-    held, last_rows = call(
-        fetch_kernel,
-        [tokens, jax.ShapeDtypeStruct((HALO, depth), BF16)],
-        [tokens],
-        0,
-        [pltpu.SemaphoreType.DMA((2,))],
-        space=HBM,
-    )
-    tail = None
-    for z in range(tp):
-        pairs = [((c - 1) * tp + tp - 1, c * tp + z) for c in range(1, ctx)]
-        part = lax.ppermute(last_rows, both, pairs)
-        tail = part if tail is None else tail + part
+    pairs = [(c * tp + z, (c + 1) * tp + z) for c in range(ctx - 1) for z in range(1, tp, 2)]
+    ahead = lax.ppermute(tail, both, pairs)
+    beside = lax.ppermute(ahead, "tp", [(z, z - 1) for z in range(1, tp, 2)])
+    tail = ahead + beside
 
     shape = jax.ShapeDtypeStruct((row_width, rows), BF16)
     work = 2 * rows * depth * row_width
-    halo, own = call(own_kernel, [shape] * 2, [tail, held, weight], flops=2 * work)
-    early = call(early_kernel, [shape] * len(turns), [side, held] + pieces, 1, flops=work)
+    halo, own = call(own_kernel, [shape] * 2, [tail, tokens, weight], flops=2 * work)
+    early = call(early_kernel, [shape] * len(turns), [side, tokens] + pieces, 1, flops=work)
     *late, other = call(
         late_kernel, [shape] * (len(turns) + 1), [side, paired, weight] + pieces, 1, flops=2 * work
     )

time: 51.1 us -> 47.4 us (0.928)
  local copies, waits for them, and re-layouts: 1.95 us -> 0.02 us
  waiting for transfers between devices: 24.7 us -> 22.9 us
  starting transfers between devices: 19.5 us -> 18.5 us
  Pallas kernels: 4.44 us -> 5.37 us
    ppermute x2, waiting for transfers between devices: 6.2 us -> 2.72 us  [per_device(): blocks += [lax.ppermute(one, 'tp', pairs), lax.ppermute(two, 'tp', pairs)]]
    ppermute x4 -> x2, waiting for transfers between devices: 0.01 us -> 1.67 us  [the longest x1 1.67 us: per_device(): beside = lax.ppermute(ahead, 'tp', [(z, z - 1) for z in range(1, tp, 2)])]
    unnamed x6, local copies, waits for them, and re-layouts: 1.05 us -> 0.01 us
    pallas_call x7, Pallas kernels: 4.44 us -> 5.37 us  [call(): pl.pallas_call(kernel, out_shape=outs, in_specs=[SMEM] * scalars + [space...]
    dynamic_slice x1 -> x0, local copies, waits for them, and re-layouts: 0.89 us -> none  [per_device(): mine = lax.dynamic_slice(weight, (0, share * piece), (row_width, piece))]
    ppermute x4 -> x2, starting transfers between devices: 2.78 us -> 1.93 us  [the longest x1 1.28 us: per_device(): beside = lax.ppermute(ahead, 'tp', [(z, z - 1) for z in range(1, tp, 2)])]
  transfers between devices with their start and end apart: 19 -> 17, of which waited for: 10 -> 10; matrix products, arithmetic and copies ran while one was open for 2% -> 0% of each run, Pallas kernels for 4% -> 6%
where the time goes in v2:
time: 47.4 us; the launch traced here: 47.1 us
  waiting for transfers between devices  22.9 us (48%)
  starting transfers between devices  18.5 us (39%)
  Pallas kernels  5.37 us (11%)
    ppermute x1, waiting for transfers between devices, per_device(): lax.ppermute(mine, 'tp', [((z + 2 * turn) % tp, z) for z in range(tp)])  9.77 us
    pallas_call x7, Pallas kernels, call(): pl.pallas_call(kernel, out_shape=outs, in_specs=[SMEM] * scalars + [space...  5.37 us
    ppermute x8, waiting for transfers between devices, swap(): return lax.ppermute(array, 'ctx', [(i, i ^ bit) for i in range(ctx)])  5.37 us
    ppermute x8, starting transfers between devices, swap(): return lax.ppermute(array, 'ctx', [(i, i ^ bit) for i in range(ctx)])  3.7 us
    ppermute x3, starting transfers between devices, per_device(): parts.append(lax.ppermute(total, 'ctx', pairs))  3.62 us
    ppermute x2, starting transfers between devices, per_device(): blocks += [lax.ppermute(one, 'tp', pairs), lax.ppermute(two, 'tp', pairs)]  3.55 us
    ppermute x3, waiting for transfers between devices, per_device(): parts.append(lax.ppermute(total, 'ctx', pairs))  3.37 us
    ppermute x1, starting transfers between devices, per_device(): paired = lax.ppermute(tokens, 'tp', [(z, z ^ 1) for z in range(tp)])  3.05 us
  transfers between devices with their start and end apart: 17, of which 10 were waited for; matrix products, arithmetic and copies ran while one was open for 0% of the time, Pallas kernels for 6%

profile of v2, /device:TPU:0, one launch (start us, length us, event | category | flops | bytes accessed | tf_op | source)
XLA Modules:
  0.0 47.1 jit_solution(4956530312457545781)
XLA Ops:
  0.0 3.1 %collective-permute-start.3 = (bf16[128,2048]{1,0:T(8,128)(2,1)}, bf16[128,2048]{1,0:T(8,128)(2,1)S(1)}, u32[]{:S(2)}, u32[]{:S(2)}) collective-permute-start(bf16[128,2048]{1,0:T(8,128)(2,1)} %tokens_ref.5), channel_id=1, source_target_pairs={{0,1},{1,0},{2,3},{3,2},{4,5},{5,4},{6,7},{7,6},{8,9},{9,8},{10,11... | collective-permute-start | bytes 1572872 | tf_op jit(solution)/shard_map/ppermute | solution.py:234
  3.1 1.0 %shard_map.37 = (bf16[184,256]{1,0:T(8,128)(2,1)S(1)}, bf16[24,256]{1,0:T(8,128)(2,1)S(1)}) custom-call(s32[1]{0:T(128)} %bitcast.4.share_ref, bf16[160,2048]{1,0:T(8,128)(2,1)} %bitcast.6, bf16[128,2048]{1,0:T(8,128)(2,1)} %tokens_ref.5), custom_call_target="tpu_custom_call" | custom-call | flops 1048576 | bytes 1048576 | tf_op jit(solution)/shard_map/pallas_call | solution.py:28
  4.0 2.7 %collective-permute-start = (bf16[184,256]{1,0:T(8,128)(2,1)S(1)}, bf16[184,256]{1,0:T(8,128)(2,1)S(1)}, u32[]{:S(2)}, u32[]{:S(2)}) collective-permute-start(bf16[184,256]{1,0:T(8,128)(2,1)S(1)} %get-tuple-element.17), channel_id=1, source_target_pairs={{2,0},{3,1},{0,2},{1,3},{6,4},{7,5},{4,6},{5,7},{10,8},{11,9},{8,1... | collective-permute-start | bytes 282632 | tf_op jit(solution)/shard_map/ppermute | solution.py:229
  6.7 9.8 %collective-permute-done = bf16[184,256]{1,0:T(8,128)(2,1)S(1)} collective-permute-done((bf16[184,256]{1,0:T(8,128)(2,1)S(1)}, bf16[184,256]{1,0:T(8,128)(2,1)S(1)}, u32[]{:S(2)}, u32[]{:S(2)}) %collective-permute-start) | collective-permute-done | bytes 94240 | tf_op jit(solution)/shard_map/ppermute | solution.py:229
  16.5 1.6 %collective-permute-start.4 = (bf16[160,256]{1,0:T(8,128)(2,1)S(1)}, bf16[160,256]{1,0:T(8,128)(2,1)S(1)}, u32[]{:S(2)}, u32[]{:S(2)}) collective-permute-start(bf16[160,256]{1,0:T(8,128)(2,1)S(1)} %slice.9.refs_0_), channel_id=1, source_target_pairs={{0,8},{4,12},{8,0},{12,4},{16,24},{20,28},{24,16},{28,20},{1,9},{5... | collective-permute-start | bytes 245768 | tf_op jit(solution)/shard_map/ppermute | solution.py:211
  18.0 1.5 %collective-permute-start.5 = (bf16[160,256]{1,0:T(8,128)(2,1)S(1)}, bf16[160,256]{1,0:T(8,128)(2,1)S(1)}, u32[]{:S(2)}, u32[]{:S(2)}) collective-permute-start(bf16[160,256]{1,0:T(8,128)(2,1)S(1)} %slice.9.refs_0_), channel_id=1, source_target_pairs={{0,16},{4,20},{8,24},{12,28},{16,0},{20,4},{24,8},{28,12},{1,17},{... | collective-permute-start | bytes 245768 | tf_op jit(solution)/shard_map/ppermute | solution.py:211
  20.0 0.7 %collective-permute-start.1 = (bf16[24,256]{1,0:T(8,128)(2,1)S(1)}, bf16[24,256]{1,0:T(8,128)(2,1)S(1)}, u32[]{:S(2)}, u32[]{:S(2)}) collective-permute-start(bf16[24,256]{1,0:T(8,128)(2,1)S(1)} %slice_select_fusion), channel_id=1, source_target_pairs={{1,5},{3,7},{5,9},{7,11},{9,13},{11,15},{13,17},{15,19},{17,21},{1... | collective-permute-start | bytes 36872 | tf_op jit(solution)/shard_map/ppermute | solution.py:237
  20.8 0.7 %collective-permute-done.4.refs_1_ = bf16[160,256]{1,0:T(8,128)(2,1)S(1)} collective-permute-done((bf16[160,256]{1,0:T(8,128)(2,1)S(1)}, bf16[160,256]{1,0:T(8,128)(2,1)S(1)}, u32[]{:S(2)}, u32[]{:S(2)}) %collective-permute-start.4) | collective-permute-done | bytes 81952 | tf_op jit(solution)/shard_map/ppermute | solution.py:211
  21.5 1.8 %collective-permute-done.5.refs_2_ = bf16[160,256]{1,0:T(8,128)(2,1)S(1)} collective-permute-done((bf16[160,256]{1,0:T(8,128)(2,1)S(1)}, bf16[160,256]{1,0:T(8,128)(2,1)S(1)}, u32[]{:S(2)}, u32[]{:S(2)}) %collective-permute-start.5) | collective-permute-done | bytes 81952 | tf_op jit(solution)/shard_map/ppermute | solution.py:211
  23.3 1.6 %collective-permute-done.6.refs_3_ = bf16[160,256]{1,0:T(8,128)(2,1)S(1)} collective-permute-done((bf16[160,256]{1,0:T(8,128)(2,1)S(1)}, bf16[160,256]{1,0:T(8,128)(2,1)S(1)}, u32[]{:S(2)}, u32[]{:S(2)}) %collective-permute-start.6) | collective-permute-done | bytes 81952 | tf_op jit(solution)/shard_map/ppermute | solution.py:211
  24.9 1.3 %collective-permute-start.2 = (bf16[24,256]{1,0:T(8,128)(2,1)S(1)}, bf16[24,256]{1,0:T(8,128)(2,1)S(1)}, u32[]{:S(2)}, u32[]{:S(2)}) collective-permute-start(bf16[24,256]{1,0:T(8,128)(2,1)S(1)} %collective-permute-done.1), channel_id=1, source_target_pairs={{1,0},{3,2},{5,4},{7,6},{9,8},{11,10},{13,12},{15,14},{17,16},{19,... | collective-permute-start | bytes 36872 | tf_op jit(solution)/shard_map/ppermute | solution.py:238
  26.6 3.4 %collective-permute-start.11 = (bf16[160,128]{1,0:T(8,128)(2,1)S(1)}, bf16[160,128]{1,0:T(8,128)(2,1)S(1)}, u32[]{:S(2)}, u32[]{:S(2)}) collective-permute-start(bf16[160,128]{1,0:T(8,128)(2,1)S(1)} %shard_map.40), channel_id=1, source_target_pairs={{0,2},{1,3},{2,0},{3,1},{4,6},{5,7},{6,4},{7,5},{8,10},{9,11},{10,... | collective-permute-start | bytes 122888 | tf_op jit(solution)/shard_map/ppermute | solution.py:252
  30.0 0.5 %shard_map.39 = (bf16[160,128]{1,0:T(8,128)(2,1)S(1)}, bf16[160,128]{1,0:T(8,128)(2,1)S(1)}) custom-call(s32[1]{0:T(128)} %bitcast.4.share_ref, bf16[128,2048]{1,0:T(8,128)(2,1)S(1)} %collective-permute-done.3.tokens_ref, bf16[160,2048]{1,0:T(8,128)(2,1)S(1)} %bitcast.7, bf16[160,256]{1,0:T(8,128)(2,1)S(1)} %slice.9.refs_0_, ...), custom_call_target="tpu_custom_call" | custom-call | flops 167772160 | bytes 1048576 | tf_op jit(solution)/shard_map/pallas_call | solution.py:28
  30.7 1.7 %collective-permute-done.2 = bf16[24,256]{1,0:T(8,128)(2,1)S(1)} collective-permute-done((bf16[24,256]{1,0:T(8,128)(2,1)S(1)}, bf16[24,256]{1,0:T(8,128)(2,1)S(1)}, u32[]{:S(2)}, u32[]{:S(2)}) %collective-permute-start.2) | collective-permute-done | bytes 12320 | tf_op jit(solution)/shard_map/ppermute | solution.py:238
  32.4 0.5 %shard_map.38 = (bf16[160,128]{1,0:T(8,128)(2,1)S(1)}, bf16[160,128]{1,0:T(8,128)(2,1)S(1)}) custom-call(bf16[24,256]{1,0:T(8,128)(2,1)S(1)} %add.23.tail_ref, bf16[128,2048]{1,0:T(8,128)(2,1)S(1)} %copy-done.1, bf16[160,2048]{1,0:T(8,128)(2,1)S(1)} %bitcast.8), custom_call_target="tpu_custom_call" | custom-call | flops 167772160 | bytes 1048576 | tf_op jit(solution)/shard_map/pallas_call | solution.py:28
  32.9 2.7 %collective-permute-done.12.refs_3_ = bf16[160,128]{1,0:T(8,128)(2,1)S(1)} collective-permute-done((bf16[160,128]{1,0:T(8,128)(2,1)S(1)}, bf16[160,128]{1,0:T(8,128)(2,1)S(1)}, u32[]{:S(2)}, u32[]{:S(2)}) %collective-permute-start.12) | collective-permute-done | bytes 40992 | tf_op jit(solution)/shard_map/ppermute | solution.py:252
  35.7 1.3 %shard_map.41 = (bf16[512,160]{1,0:T(8,128)(2,1)S(1)}, bf16[160,512]{1,0:T(8,128)(2,1)S(1)}, bf16[128,512]{1,0:T(8,128)(2,1)S(1)}, f32[168,128]{1,0:T(8,128)S(1)}) custom-call(s32[4]{0:T(128)S(1)} %pad_add_fusion.place_ref, f32[4,160]{1,0:T(4,128)S(1)} %copy-done.2, bf16[160,128]{1,0:T(8,128)(2,1)S(1)} %get-tuple-element.19.halo_ref, ...), custom_call_target="tpu_custom_call" | custom-call | flops 1048576 | bytes 1048576 | tf_op jit(solution)/shard_map/pallas_call | solution.py:28
  37.1 1.3 %collective-permute-done.13 = f32[168,128]{1,0:T(8,128)S(1)} collective-permute-done((f32[168,128]{1,0:T(8,128)S(1)}, f32[168,128]{1,0:T(8,128)S(1)}, u32[]{:S(2)}, u32[]{:S(2)}) %collective-permute-start.13) | collective-permute-done | bytes 86048 | tf_op jit(solution)/shard_map/ppermute | solution.py:211
  38.8 0.6 %shard_map.42 = (f32[512,128]{1,0:T(8,128)S(1)}, f32[512,128]{1,0:T(8,128)S(1)}) custom-call(bf16[512,160]{1,0:T(8,128)(2,1)S(1)} %get-tuple-element.23.query_ref, bf16[160,512]{1,0:T(8,128)(2,1)S(1)} %get-tuple-element.24.key_ref, bf16[128,512]{1,0:T(8,128)(2,1)S(1)} %get-tuple-element.25.value_ref), custom_call_target="tpu_custom_call" | custom-call | flops 150994944 | bytes 1048576 | tf_op jit(solution)/shard_map/pallas_call | solution.py:28
  39.5 1.2 %collective-permute-start.15 = (f32[168,128]{1,0:T(8,128)S(1)}, f32[168,128]{1,0:T(8,128)S(1)}, u32[]{:S(2)}, u32[]{:S(2)}) collective-permute-start(f32[168,128]{1,0:T(8,128)S(1)} %get-tuple-element.29), channel_id=1, source_target_pairs={{0,16},{4,20},{8,24},{12,28},{16,0},{20,4},{24,8},{28,12},{1,17},{... | collective-permute-start | bytes 258056 | tf_op jit(solution)/shard_map/ppermute | solution.py:284
  40.7 2.0 %collective-permute-start.16 = (f32[168,128]{1,0:T(8,128)S(1)}, f32[168,128]{1,0:T(8,128)S(1)}, u32[]{:S(2)}, u32[]{:S(2)}) collective-permute-start(f32[168,128]{1,0:T(8,128)S(1)} %get-tuple-element.29), channel_id=1, source_target_pairs={{0,24},{4,28},{8,16},{12,20},{16,8},{20,12},{24,0},{28,4},{1,25},{... | collective-permute-start | bytes 258056 | tf_op jit(solution)/shard_map/ppermute | solution.py:284
  43.0 1.9 %collective-permute-done.15 = f32[168,128]{1,0:T(8,128)S(1)} collective-permute-done((f32[168,128]{1,0:T(8,128)S(1)}, f32[168,128]{1,0:T(8,128)S(1)}, u32[]{:S(2)}, u32[]{:S(2)}) %collective-permute-start.15) | collective-permute-done | bytes 86048 | tf_op jit(solution)/shard_map/ppermute | solution.py:284
  45.0 1.1 %collective-permute-done.16 = f32[168,128]{1,0:T(8,128)S(1)} collective-permute-done((f32[168,128]{1,0:T(8,128)S(1)}, f32[168,128]{1,0:T(8,128)S(1)}, u32[]{:S(2)}, u32[]{:S(2)}) %collective-permute-start.16) | collective-permute-done | bytes 86048 | tf_op jit(solution)/shard_map/ppermute | solution.py:284
  46.0 1.0 %shard_map.43 = bf16[512,128]{1,0:T(8,128)(2,1)} custom-call(bf16[512,160]{1,0:T(8,128)(2,1)S(1)} %get-tuple-element.23.query_ref, f32[512,128]{1,0:T(8,128)S(1)} %get-tuple-element.26.numerator_ref, f32[512,128]{1,0:T(8,128)S(1)} %get-tuple-element.27.denominator_ref, f32[168,128]{1,0:T(8,128)S(1)} %get-tuple-element.30.refs_0_, ...), custom_call_target="tpu_custom_call" | custom-call | flops 62914560 | bytes 1048576 | tf_op jit(solution)/shard_map/pallas_call | solution.py:28
  (31 shorter events, 2.1 us)
Async XLA Ops:
  0.0 30.0 %collective-permute-start.3 = (bf16[128,2048]{1,0:T(8,128)(2,1)}, bf16[128,2048]{1,0:T(8,128)(2,1)S(1)}, u32[]{:S(2)}, u32[]{:S(2)}) collective-permute-start(bf16[128,2048]{1,0:T(8,128)(2,1)} %tokens_ref.5), channel_id=1, source_target_pairs={{0,1},{1,0},{2,3},{3,2},{4,5},{5,4},{6,7},{7,6},{8,9},{9,8},{10,11... | collective-permute-start | bytes 1572872 | tf_op jit(solution)/shard_map/ppermute | solution.py:234
  3.1 23.2 %copy-start.1 = (bf16[128,2048]{1,0:T(8,128)(2,1)S(1)}, bf16[128,2048]{1,0:T(8,128)(2,1)}, u32[]{:S(2)}) copy-start(bf16[128,2048]{1,0:T(8,128)(2,1)} %tokens_ref.5) | copy-start | bytes 1572868
  4.0 12.4 %collective-permute-start = (bf16[184,256]{1,0:T(8,128)(2,1)S(1)}, bf16[184,256]{1,0:T(8,128)(2,1)S(1)}, u32[]{:S(2)}, u32[]{:S(2)}) collective-permute-start(bf16[184,256]{1,0:T(8,128)(2,1)S(1)} %get-tuple-element.17), channel_id=1, source_target_pairs={{2,0},{3,1},{0,2},{1,3},{6,4},{7,5},{4,6},{5,7},{10,8},{11,9},{8,1... | collective-permute-start | bytes 282632 | tf_op jit(solution)/shard_map/ppermute | solution.py:229
  16.5 13.6 %copy-start = (bf16[2048,160]{0,1:T(8,128)(2,1)S(1)}, bf16[2048,160]{0,1:T(8,128)(2,1)}, u32[]{:S(2)}) copy-start(bf16[2048,160]{0,1:T(8,128)(2,1)} %param.4) | copy-start | bytes 1966084
  16.5 5.0 %collective-permute-start.4 = (bf16[160,256]{1,0:T(8,128)(2,1)S(1)}, bf16[160,256]{1,0:T(8,128)(2,1)S(1)}, u32[]{:S(2)}, u32[]{:S(2)}) collective-permute-start(bf16[160,256]{1,0:T(8,128)(2,1)S(1)} %slice.9.refs_0_), channel_id=1, source_target_pairs={{0,8},{4,12},{8,0},{12,4},{16,24},{20,28},{24,16},{28,20},{1,9},{5... | collective-permute-start | bytes 245768 | tf_op jit(solution)/shard_map/ppermute | solution.py:211
  18.0 5.3 %collective-permute-start.5 = (bf16[160,256]{1,0:T(8,128)(2,1)S(1)}, bf16[160,256]{1,0:T(8,128)(2,1)S(1)}, u32[]{:S(2)}, u32[]{:S(2)}) collective-permute-start(bf16[160,256]{1,0:T(8,128)(2,1)S(1)} %slice.9.refs_0_), channel_id=1, source_target_pairs={{0,16},{4,20},{8,24},{12,28},{16,0},{20,4},{24,8},{28,12},{1,17},{... | collective-permute-start | bytes 245768 | tf_op jit(solution)/shard_map/ppermute | solution.py:211
  19.6 5.3 %collective-permute-start.6 = (bf16[160,256]{1,0:T(8,128)(2,1)S(1)}, bf16[160,256]{1,0:T(8,128)(2,1)S(1)}, u32[]{:S(2)}, u32[]{:S(2)}) collective-permute-start(bf16[160,256]{1,0:T(8,128)(2,1)S(1)} %slice.9.refs_0_), channel_id=1, source_target_pairs={{0,24},{4,28},{8,16},{12,20},{16,8},{20,12},{24,0},{28,4},{1,25},{... | collective-permute-start | bytes 245768 | tf_op jit(solution)/shard_map/ppermute | solution.py:211
  20.0 0.7 %collective-permute-start.1 = (bf16[24,256]{1,0:T(8,128)(2,1)S(1)}, bf16[24,256]{1,0:T(8,128)(2,1)S(1)}, u32[]{:S(2)}, u32[]{:S(2)}) collective-permute-start(bf16[24,256]{1,0:T(8,128)(2,1)S(1)} %slice_select_fusion), channel_id=1, source_target_pairs={{1,5},{3,7},{5,9},{7,11},{9,13},{11,15},{13,17},{15,19},{17,21},{1... | collective-permute-start | bytes 36872 | tf_op jit(solution)/shard_map/ppermute | solution.py:237
  20.7 4.2 %collective-permute-start.7 = (bf16[160,256]{1,0:T(8,128)(2,1)S(1)}, bf16[160,256]{1,0:T(8,128)(2,1)S(1)}, u32[]{:S(2)}, u32[]{:S(2)}) collective-permute-start(bf16[160,256]{1,0:T(8,128)(2,1)S(1)} %slice.9.refs_0_), channel_id=1, source_target_pairs={{0,4},{4,0},{8,12},{12,8},{16,20},{20,16},{24,28},{28,24},{1,5},{5... | collective-permute-start | bytes 245768 | tf_op jit(solution)/shard_map/ppermute | solution.py:211
  21.5 4.7 %collective-permute-start.8 = (bf16[160,256]{1,0:T(8,128)(2,1)S(1)}, bf16[160,256]{1,0:T(8,128)(2,1)S(1)}, u32[]{:S(2)}, u32[]{:S(2)}) collective-permute-start(bf16[160,256]{1,0:T(8,128)(2,1)S(1)} %collective-permute-done.4.refs_1_), channel_id=1, source_target_pairs={{0,4},{4,0},{8,12},{12,8},{16,20},{20,16},{24,28},{28,24},{1,5},{5... | collective-permute-start | bytes 245768 | tf_op jit(solution)/shard_map/ppermute | solution.py:211
  23.3 2.9 %collective-permute-start.9 = (bf16[160,256]{1,0:T(8,128)(2,1)S(1)}, bf16[160,256]{1,0:T(8,128)(2,1)S(1)}, u32[]{:S(2)}, u32[]{:S(2)}) collective-permute-start(bf16[160,256]{1,0:T(8,128)(2,1)S(1)} %collective-permute-done.5.refs_2_), channel_id=1, source_target_pairs={{0,4},{4,0},{8,12},{12,8},{16,20},{20,16},{24,28},{28,24},{1,5},{5... | collective-permute-start | bytes 245768 | tf_op jit(solution)/shard_map/ppermute | solution.py:211
  24.9 1.3 %collective-permute-start.10 = (bf16[160,256]{1,0:T(8,128)(2,1)S(1)}, bf16[160,256]{1,0:T(8,128)(2,1)S(1)}, u32[]{:S(2)}, u32[]{:S(2)}) collective-permute-start(bf16[160,256]{1,0:T(8,128)(2,1)S(1)} %collective-permute-done.6.refs_3_), channel_id=1, source_target_pairs={{0,4},{4,0},{8,12},{12,8},{16,20},{20,16},{24,28},{28,24},{1,5},{5... | collective-permute-start | bytes 245768 | tf_op jit(solution)/shard_map/ppermute | solution.py:211
  24.9 7.5 %collective-permute-start.2 = (bf16[24,256]{1,0:T(8,128)(2,1)S(1)}, bf16[24,256]{1,0:T(8,128)(2,1)S(1)}, u32[]{:S(2)}, u32[]{:S(2)}) collective-permute-start(bf16[24,256]{1,0:T(8,128)(2,1)S(1)} %collective-permute-done.1), channel_id=1, source_target_pairs={{1,0},{3,2},{5,4},{7,6},{9,8},{11,10},{13,12},{15,14},{17,16},{19,... | collective-permute-start | bytes 36872 | tf_op jit(solution)/shard_map/ppermute | solution.py:238
  26.6 6.4 %collective-permute-start.11 = (bf16[160,128]{1,0:T(8,128)(2,1)S(1)}, bf16[160,128]{1,0:T(8,128)(2,1)S(1)}, u32[]{:S(2)}, u32[]{:S(2)}) collective-permute-start(bf16[160,128]{1,0:T(8,128)(2,1)S(1)} %shard_map.40), channel_id=1, source_target_pairs={{0,2},{1,3},{2,0},{3,1},{4,6},{5,7},{6,4},{7,5},{8,10},{9,11},{10,... | collective-permute-start | bytes 122888 | tf_op jit(solution)/shard_map/ppermute | solution.py:252
  30.6 5.1 %collective-permute-start.12 = (bf16[160,128]{1,0:T(8,128)(2,1)S(1)}, bf16[160,128]{1,0:T(8,128)(2,1)S(1)}, u32[]{:S(2)}, u32[]{:S(2)}) collective-permute-start(bf16[160,128]{1,0:T(8,128)(2,1)S(1)} %get-tuple-element.22), channel_id=1, source_target_pairs={{0,2},{1,3},{2,0},{3,1},{4,6},{5,7},{6,4},{7,5},{8,10},{9,11},{10,... | collective-permute-start | bytes 122888 | tf_op jit(solution)/shard_map/ppermute | solution.py:252
  32.9 2.7 %copy-start.2 = (f32[4,160]{1,0:T(4,128)S(1)}, f32[4,160]{1,0:T(4,128)}, u32[]{:S(2)}) copy-start(f32[4,160]{1,0:T(4,128)} %conv_ref.1) | copy-start | bytes 7684
  37.0 1.3 %collective-permute-start.13 = (f32[168,128]{1,0:T(8,128)S(1)}, f32[168,128]{1,0:T(8,128)S(1)}, u32[]{:S(2)}, u32[]{:S(2)}) collective-permute-start(f32[168,128]{1,0:T(8,128)S(1)} %get-tuple-element.28), channel_id=1, source_target_pairs={{0,4},{4,0},{8,12},{12,8},{16,20},{20,16},{24,28},{28,24},{1,5},{5... | collective-permute-start | bytes 258056 | tf_op jit(solution)/shard_map/ppermute | solution.py:211
  38.4 4.7 %collective-permute-start.14 = (f32[168,128]{1,0:T(8,128)S(1)}, f32[168,128]{1,0:T(8,128)S(1)}, u32[]{:S(2)}, u32[]{:S(2)}) collective-permute-start(f32[168,128]{1,0:T(8,128)S(1)} %get-tuple-element.29), channel_id=1, source_target_pairs={{0,8},{4,12},{8,0},{12,4},{16,24},{20,28},{24,16},{28,20},{1,9},{5... | collective-permute-start | bytes 258056 | tf_op jit(solution)/shard_map/ppermute | solution.py:284
  39.5 5.5 %collective-permute-start.15 = (f32[168,128]{1,0:T(8,128)S(1)}, f32[168,128]{1,0:T(8,128)S(1)}, u32[]{:S(2)}, u32[]{:S(2)}) collective-permute-start(f32[168,128]{1,0:T(8,128)S(1)} %get-tuple-element.29), channel_id=1, source_target_pairs={{0,16},{4,20},{8,24},{12,28},{16,0},{20,4},{24,8},{28,12},{1,17},{... | collective-permute-start | bytes 258056 | tf_op jit(solution)/shard_map/ppermute | solution.py:284
  40.7 5.4 %collective-permute-start.16 = (f32[168,128]{1,0:T(8,128)S(1)}, f32[168,128]{1,0:T(8,128)S(1)}, u32[]{:S(2)}, u32[]{:S(2)}) collective-permute-start(f32[168,128]{1,0:T(8,128)S(1)} %get-tuple-element.29), channel_id=1, source_target_pairs={{0,24},{4,28},{8,16},{12,20},{16,8},{20,12},{24,0},{28,4},{1,25},{... | collective-permute-start | bytes 258056 | tf_op jit(solution)/shard_map/ppermute | solution.py:284

commit v3 on v1

--- a/solution.py
+++ b/solution.py
@@ -36,18 +36,25 @@
     )(*operands)
 
 
+def hbm(array):
+    return pltpu.with_memory_space_constraint(array, pltpu.HBM)
+
+
 def dot_last(left, right):
     return lax.dot_general(left, right, LAST, preferred_element_type=F32)
 
 
-def fetch_kernel(tokens_ref, all_ref, last_ref, sems):
-    rows = tokens_ref.shape[0]
-    last = pltpu.make_async_copy(tokens_ref.at[rows - HALO :, :], last_ref, sems.at[0])
-    whole = pltpu.make_async_copy(tokens_ref, all_ref, sems.at[1])
+def pack_kernel(share_ref, weight_ref, tokens_ref, sent_ref, last_ref, sems):
+    width = sent_ref.shape[1]
+    start = pl.multiple_of(share_ref[0] * width, LANES)
+    weights = pltpu.make_async_copy(weight_ref.at[:, pl.ds(start, width)], sent_ref, sems.at[0])
+    last = pltpu.make_async_copy(
+        tokens_ref.at[tokens_ref.shape[0] - HALO :, :], last_ref, sems.at[1]
+    )
+    weights.start()
     last.start()
-    whole.start()
+    weights.wait()
     last.wait()
-    whole.wait()
 
 
 def own_kernel(tail_ref, tokens_ref, weight_ref, halo_ref, own_ref):
@@ -187,7 +194,17 @@
         return lax.ppermute(array, "ctx", [(i, i ^ bit) for i in range(ctx)])
 
     side = share.astype(jnp.int32).reshape(1)
-    mine = lax.dynamic_slice(weight, (0, share * piece), (row_width, piece))
+    mine, last_rows = call(
+        pack_kernel,
+        [
+            jax.ShapeDtypeStruct((row_width, piece), BF16),
+            jax.ShapeDtypeStruct((HALO, depth), BF16),
+        ],
+        [side, hbm(weight), hbm(tokens)],
+        1,
+        [pltpu.SemaphoreType.DMA((2,))],
+        space=HBM,
+    )
     pieces = []
     for turn in turns:
         first = lax.ppermute(mine, "tp", [((z + 2 * turn) % tp, z) for z in range(tp)])
@@ -195,14 +212,6 @@
         pieces += parts + [swap(part, 1) for part in parts]
     paired = lax.ppermute(tokens, "tp", [(z, z ^ 1) for z in range(tp)])
 
-    held, last_rows = call(
-        fetch_kernel,
-        [tokens, jax.ShapeDtypeStruct((HALO, depth), BF16)],
-        [tokens],
-        0,
-        [pltpu.SemaphoreType.DMA((2,))],
-        space=HBM,
-    )
     tail = None
     for z in range(tp):
         pairs = [((c - 1) * tp + tp - 1, c * tp + z) for c in range(1, ctx)]
@@ -211,8 +220,8 @@
 
     shape = jax.ShapeDtypeStruct((row_width, rows), BF16)
     work = 2 * rows * depth * row_width
-    halo, own = call(own_kernel, [shape] * 2, [tail, held, weight], flops=2 * work)
-    early = call(early_kernel, [shape] * len(turns), [side, held] + pieces, 1, flops=work)
+    halo, own = call(own_kernel, [shape] * 2, [tail, tokens, weight], flops=2 * work)
+    early = call(early_kernel, [shape] * len(turns), [side, tokens] + pieces, 1, flops=work)
     *late, other = call(
         late_kernel, [shape] * (len(turns) + 1), [side, paired, weight] + pieces, 1, flops=2 * work
     )

time: 51.1 us -> 50.1 us (0.980)
  local copies, waits for them, and re-layouts: 1.95 us -> 0.02 us
  Pallas kernels: 4.44 us -> 5.34 us
    unnamed x6, local copies, waits for them, and re-layouts: 1.05 us -> 0.02 us
    pallas_call x7, Pallas kernels: 4.44 us -> 5.34 us  [call(): pl.pallas_call(kernel, out_shape=outs, in_specs=[SMEM] * scalars + [space...]
    dynamic_slice x1 -> x0, local copies, waits for them, and re-layouts: 0.89 us -> none  [per_device(): mine = lax.dynamic_slice(weight, (0, share * piece), (row_width, piece))]
    ppermute x8, waiting for transfers between devices: 5.16 us -> 6.04 us  [swap(): return lax.ppermute(array, 'ctx', [(i, i ^ bit) for i in range(ctx)])]
  transfers between devices with their start and end apart: 19 -> 19, of which waited for: 10 -> 9; matrix products, arithmetic and copies ran while one was open for 2% -> 0% of each run, Pallas kernels for 4% -> 6%
where the time goes in v3:
time: 50.1 us; the launch traced here: 49.9 us
  waiting for transfers between devices  25 us (50%)
  starting transfers between devices  19.2 us (38%)
  Pallas kernels  5.34 us (11%)
    ppermute x1, waiting for transfers between devices, per_device(): lax.ppermute(mine, 'tp', [((z + 2 * turn) % tp, z) for z in range(tp)])  9.51 us
    ppermute x8, waiting for transfers between devices, swap(): return lax.ppermute(array, 'ctx', [(i, i ^ bit) for i in range(ctx)])  6.04 us
    ppermute x2, waiting for transfers between devices, per_device(): blocks += [lax.ppermute(one, 'tp', pairs), lax.ppermute(two, 'tp', pairs)]  5.82 us
    pallas_call x7, Pallas kernels, call(): pl.pallas_call(kernel, out_shape=outs, in_specs=[SMEM] * scalars + [space...  5.34 us
    ppermute x8, starting transfers between devices, swap(): return lax.ppermute(array, 'ctx', [(i, i ^ bit) for i in range(ctx)])  3.67 us
    ppermute x3, waiting for transfers between devices, per_device(): parts.append(lax.ppermute(total, 'ctx', pairs))  3.64 us
    ppermute x3, starting transfers between devices, per_device(): parts.append(lax.ppermute(total, 'ctx', pairs))  3.62 us
    ppermute x2, starting transfers between devices, per_device(): blocks += [lax.ppermute(one, 'tp', pairs), lax.ppermute(two, 'tp', pairs)]  3.54 us
  transfers between devices with their start and end apart: 19, of which 9 were waited for; matrix products, arithmetic and copies ran while one was open for 0% of the time, Pallas kernels for 6%

profile of v3, /device:TPU:0, one launch (start us, length us, event | category | flops | bytes accessed | tf_op | source)
XLA Modules:
  0.0 49.9 jit_solution(12643265572853620536)
XLA Ops:
  0.0 3.1 %collective-permute-start.4 = (bf16[128,2048]{1,0:T(8,128)(2,1)}, bf16[128,2048]{1,0:T(8,128)(2,1)S(1)}, u32[]{:S(2)}, u32[]{:S(2)}) collective-permute-start(bf16[128,2048]{1,0:T(8,128)(2,1)} %tokens_ref.5), channel_id=1, source_target_pairs={{0,1},{1,0},{2,3},{3,2},{4,5},{5,4},{6,7},{7,6},{8,9},{9,8},{10,11... | collective-permute-start | bytes 1572872 | tf_op jit(solution)/shard_map/ppermute | solution.py:213
  3.1 1.0 %shard_map.37 = (bf16[160,256]{1,0:T(8,128)(2,1)S(1)}, bf16[8,2048]{1,0:T(8,128)(2,1)S(1)}) custom-call(s32[1]{0:T(128)} %bitcast.4.share_ref, bf16[160,2048]{1,0:T(8,128)(2,1)} %bitcast.6, bf16[128,2048]{1,0:T(8,128)(2,1)} %tokens_ref.5), custom_call_target="tpu_custom_call" | custom-call | flops 1048576 | bytes 1048576 | tf_op jit(solution)/shard_map/pallas_call | solution.py:28
  4.0 2.7 %collective-permute-start.5 = (bf16[160,256]{1,0:T(8,128)(2,1)S(1)}, bf16[160,256]{1,0:T(8,128)(2,1)S(1)}, u32[]{:S(2)}, u32[]{:S(2)}) collective-permute-start(bf16[160,256]{1,0:T(8,128)(2,1)S(1)} %get-tuple-element.20), channel_id=1, source_target_pairs={{2,0},{3,1},{0,2},{1,3},{6,4},{7,5},{4,6},{5,7},{10,8},{11,9},{8,1... | collective-permute-start | bytes 245768 | tf_op jit(solution)/shard_map/ppermute | solution.py:210
  6.7 9.5 %collective-permute-done.5.refs_0_ = bf16[160,256]{1,0:T(8,128)(2,1)S(1)} collective-permute-done((bf16[160,256]{1,0:T(8,128)(2,1)S(1)}, bf16[160,256]{1,0:T(8,128)(2,1)S(1)}, u32[]{:S(2)}, u32[]{:S(2)}) %collective-permute-start.5) | collective-permute-done | bytes 81952 | tf_op jit(solution)/shard_map/ppermute | solution.py:210
  16.2 1.5 %collective-permute-start.6 = (bf16[160,256]{1,0:T(8,128)(2,1)S(1)}, bf16[160,256]{1,0:T(8,128)(2,1)S(1)}, u32[]{:S(2)}, u32[]{:S(2)}) collective-permute-start(bf16[160,256]{1,0:T(8,128)(2,1)S(1)} %collective-permute-done.5.refs_0_), channel_id=1, source_target_pairs={{0,8},{4,12},{8,0},{12,4},{16,24},{20,28},{24,16},{28,20},{1,9},{5... | collective-permute-start | bytes 245768 | tf_op jit(solution)/shard_map/ppermute | solution.py:194
  17.7 1.5 %collective-permute-start.7 = (bf16[160,256]{1,0:T(8,128)(2,1)S(1)}, bf16[160,256]{1,0:T(8,128)(2,1)S(1)}, u32[]{:S(2)}, u32[]{:S(2)}) collective-permute-start(bf16[160,256]{1,0:T(8,128)(2,1)S(1)} %collective-permute-done.5.refs_0_), channel_id=1, source_target_pairs={{0,16},{4,20},{8,24},{12,28},{16,0},{20,4},{24,8},{28,12},{1,17},{... | collective-permute-start | bytes 245768 | tf_op jit(solution)/shard_map/ppermute | solution.py:194
  19.7 1.4 %collective-permute-done.6.refs_1_ = bf16[160,256]{1,0:T(8,128)(2,1)S(1)} collective-permute-done((bf16[160,256]{1,0:T(8,128)(2,1)S(1)}, bf16[160,256]{1,0:T(8,128)(2,1)S(1)}, u32[]{:S(2)}, u32[]{:S(2)}) %collective-permute-start.6) | collective-permute-done | bytes 81952 | tf_op jit(solution)/shard_map/ppermute | solution.py:194
  21.1 1.8 %collective-permute-done.7.refs_2_ = bf16[160,256]{1,0:T(8,128)(2,1)S(1)} collective-permute-done((bf16[160,256]{1,0:T(8,128)(2,1)S(1)}, bf16[160,256]{1,0:T(8,128)(2,1)S(1)}, u32[]{:S(2)}, u32[]{:S(2)}) %collective-permute-start.7) | collective-permute-done | bytes 81952 | tf_op jit(solution)/shard_map/ppermute | solution.py:194
  22.9 1.6 %collective-permute-done.8.refs_3_ = bf16[160,256]{1,0:T(8,128)(2,1)S(1)} collective-permute-done((bf16[160,256]{1,0:T(8,128)(2,1)S(1)}, bf16[160,256]{1,0:T(8,128)(2,1)S(1)}, u32[]{:S(2)}, u32[]{:S(2)}) %collective-permute-start.8) | collective-permute-done | bytes 81952 | tf_op jit(solution)/shard_map/ppermute | solution.py:194
  24.6 0.7 %collective-permute-start.3 = (bf16[8,2048]{1,0:T(8,128)(2,1)S(1)}, bf16[8,2048]{1,0:T(8,128)(2,1)S(1)}, u32[]{:S(2)}, u32[]{:S(2)}) collective-permute-start(bf16[8,2048]{1,0:T(8,128)(2,1)S(1)} %get-tuple-element.17), channel_id=1, source_target_pairs={{3,7},{7,11},{11,15},{15,19},{19,23},{23,27},{27,31}} | collective-permute-start | bytes 98312 | tf_op jit(solution)/shard_map/ppermute | solution.py:218
  25.2 0.7 %collective-permute-start.2 = (bf16[8,2048]{1,0:T(8,128)(2,1)S(1)}, bf16[8,2048]{1,0:T(8,128)(2,1)S(1)}, u32[]{:S(2)}, u32[]{:S(2)}) collective-permute-start(bf16[8,2048]{1,0:T(8,128)(2,1)S(1)} %get-tuple-element.17), channel_id=1, source_target_pairs={{3,6},{7,10},{11,14},{15,18},{19,22},{23,26},{27,30}} | collective-permute-start | bytes 98312 | tf_op jit(solution)/shard_map/ppermute | solution.py:218
  25.9 0.7 %collective-permute-start = (bf16[8,2048]{1,0:T(8,128)(2,1)S(1)}, bf16[8,2048]{1,0:T(8,128)(2,1)S(1)}, u32[]{:S(2)}, u32[]{:S(2)}) collective-permute-start(bf16[8,2048]{1,0:T(8,128)(2,1)S(1)} %get-tuple-element.17), channel_id=1, source_target_pairs={{3,4},{7,8},{11,12},{15,16},{19,20},{23,24},{27,28}} | collective-permute-start | bytes 98312 | tf_op jit(solution)/shard_map/ppermute | solution.py:218
  26.6 0.7 %collective-permute-start.1 = (bf16[8,2048]{1,0:T(8,128)(2,1)S(1)}, bf16[8,2048]{1,0:T(8,128)(2,1)S(1)}, u32[]{:S(2)}, u32[]{:S(2)}) collective-permute-start(bf16[8,2048]{1,0:T(8,128)(2,1)S(1)} %get-tuple-element.17), channel_id=1, source_target_pairs={{3,5},{7,9},{11,13},{15,17},{19,21},{23,25},{27,29}} | collective-permute-start | bytes 98312 | tf_op jit(solution)/shard_map/ppermute | solution.py:218
  27.7 3.4 %collective-permute-start.13 = (bf16[160,128]{1,0:T(8,128)(2,1)S(1)}, bf16[160,128]{1,0:T(8,128)(2,1)S(1)}, u32[]{:S(2)}, u32[]{:S(2)}) collective-permute-start(bf16[160,128]{1,0:T(8,128)(2,1)S(1)} %shard_map.40), channel_id=1, source_target_pairs={{0,2},{1,3},{2,0},{3,1},{4,6},{5,7},{6,4},{7,5},{8,10},{9,11},{10,... | collective-permute-start | bytes 122888 | tf_op jit(solution)/shard_map/ppermute | solution.py:232
  31.2 0.5 %shard_map.39 = (bf16[160,128]{1,0:T(8,128)(2,1)S(1)}, bf16[160,128]{1,0:T(8,128)(2,1)S(1)}) custom-call(s32[1]{0:T(128)} %bitcast.4.share_ref, bf16[128,2048]{1,0:T(8,128)(2,1)S(1)} %collective-permute-done.4.tokens_ref, bf16[160,2048]{1,0:T(8,128)(2,1)S(1)} %bitcast.7, bf16[160,256]{1,0:T(8,128)(2,1)S(1)} %collective-permute-done.5.refs_0_, ...), custom_call_target="tpu_custom_call" | custom-call | flops 167772160 | bytes 1048576 | tf_op jit(solution)/shard_map/pallas_call | solution.py:28
  32.3 0.8 %collective-permute-done.13.refs_2_ = bf16[160,128]{1,0:T(8,128)(2,1)S(1)} collective-permute-done((bf16[160,128]{1,0:T(8,128)(2,1)S(1)}, bf16[160,128]{1,0:T(8,128)(2,1)S(1)}, u32[]{:S(2)}, u32[]{:S(2)}) %collective-permute-start.13) | collective-permute-done | bytes 40992 | tf_op jit(solution)/shard_map/ppermute | solution.py:232
  33.1 5.0 %collective-permute-done.14.refs_3_ = bf16[160,128]{1,0:T(8,128)(2,1)S(1)} collective-permute-done((bf16[160,128]{1,0:T(8,128)(2,1)S(1)}, bf16[160,128]{1,0:T(8,128)(2,1)S(1)}, u32[]{:S(2)}, u32[]{:S(2)}) %collective-permute-start.14) | collective-permute-done | bytes 40992 | tf_op jit(solution)/shard_map/ppermute | solution.py:232
  38.2 1.3 %shard_map.41 = (bf16[512,160]{1,0:T(8,128)(2,1)S(1)}, bf16[160,512]{1,0:T(8,128)(2,1)S(1)}, bf16[128,512]{1,0:T(8,128)(2,1)S(1)}, f32[168,128]{1,0:T(8,128)S(1)}) custom-call(s32[4]{0:T(128)S(1)} %pad_add_fusion.place_ref, f32[4,160]{1,0:T(4,128)S(1)} %copy-done.2, bf16[160,128]{1,0:T(8,128)(2,1)S(1)} %get-tuple-element.18.halo_ref, ...), custom_call_target="tpu_custom_call" | custom-call | flops 1048576 | bytes 1048576 | tf_op jit(solution)/shard_map/pallas_call | solution.py:28
  39.7 1.2 %collective-permute-done.15 = f32[168,128]{1,0:T(8,128)S(1)} collective-permute-done((f32[168,128]{1,0:T(8,128)S(1)}, f32[168,128]{1,0:T(8,128)S(1)}, u32[]{:S(2)}, u32[]{:S(2)}) %collective-permute-start.15) | collective-permute-done | bytes 86048 | tf_op jit(solution)/shard_map/ppermute | solution.py:194
  40.9 1.0 %collective-permute-start.16 = (f32[168,128]{1,0:T(8,128)S(1)}, f32[168,128]{1,0:T(8,128)S(1)}, u32[]{:S(2)}, u32[]{:S(2)}) collective-permute-start(f32[168,128]{1,0:T(8,128)S(1)} %get-tuple-element.29), channel_id=1, source_target_pairs={{0,8},{4,12},{8,0},{12,4},{16,24},{20,28},{24,16},{28,20},{1,9},{5... | collective-permute-start | bytes 258056 | tf_op jit(solution)/shard_map/ppermute | solution.py:264
  41.9 0.6 %shard_map.42 = (f32[512,128]{1,0:T(8,128)S(1)}, f32[512,128]{1,0:T(8,128)S(1)}) custom-call(bf16[512,160]{1,0:T(8,128)(2,1)S(1)} %get-tuple-element.23.query_ref, bf16[160,512]{1,0:T(8,128)(2,1)S(1)} %get-tuple-element.24.key_ref, bf16[128,512]{1,0:T(8,128)(2,1)S(1)} %get-tuple-element.25.value_ref), custom_call_target="tpu_custom_call" | custom-call | flops 150994944 | bytes 1048576 | tf_op jit(solution)/shard_map/pallas_call | solution.py:28
  42.6 2.5 %collective-permute-start.18 = (f32[168,128]{1,0:T(8,128)S(1)}, f32[168,128]{1,0:T(8,128)S(1)}, u32[]{:S(2)}, u32[]{:S(2)}) collective-permute-start(f32[168,128]{1,0:T(8,128)S(1)} %get-tuple-element.29), channel_id=1, source_target_pairs={{0,24},{4,28},{8,16},{12,20},{16,8},{20,12},{24,0},{28,4},{1,25},{... | collective-permute-start | bytes 258056 | tf_op jit(solution)/shard_map/ppermute | solution.py:264
  45.5 3.2 %collective-permute-done.17 = f32[168,128]{1,0:T(8,128)S(1)} collective-permute-done((f32[168,128]{1,0:T(8,128)S(1)}, f32[168,128]{1,0:T(8,128)S(1)}, u32[]{:S(2)}, u32[]{:S(2)}) %collective-permute-start.17) | collective-permute-done | bytes 86048 | tf_op jit(solution)/shard_map/ppermute | solution.py:264
  48.8 1.0 %shard_map.43 = bf16[512,128]{1,0:T(8,128)(2,1)} custom-call(bf16[512,160]{1,0:T(8,128)(2,1)S(1)} %get-tuple-element.23.query_ref, f32[512,128]{1,0:T(8,128)S(1)} %get-tuple-element.26.numerator_ref, f32[512,128]{1,0:T(8,128)S(1)} %get-tuple-element.27.denominator_ref, f32[168,128]{1,0:T(8,128)S(1)} %get-tuple-element.30.refs_0_, ...), custom_call_target="tpu_custom_call" | custom-call | flops 62914560 | bytes 1048576 | tf_op jit(solution)/shard_map/pallas_call | solution.py:28
  (33 shorter events, 2.2 us)
Async XLA Ops:
  0.0 27.7 %collective-permute-start.4 = (bf16[128,2048]{1,0:T(8,128)(2,1)}, bf16[128,2048]{1,0:T(8,128)(2,1)S(1)}, u32[]{:S(2)}, u32[]{:S(2)}) collective-permute-start(bf16[128,2048]{1,0:T(8,128)(2,1)} %tokens_ref.5), channel_id=1, source_target_pairs={{0,1},{1,0},{2,3},{3,2},{4,5},{5,4},{6,7},{7,6},{8,9},{9,8},{10,11... | collective-permute-start | bytes 1572872 | tf_op jit(solution)/shard_map/ppermute | solution.py:213
  3.1 24.3 %copy-start.1 = (bf16[128,2048]{1,0:T(8,128)(2,1)S(1)}, bf16[128,2048]{1,0:T(8,128)(2,1)}, u32[]{:S(2)}) copy-start(bf16[128,2048]{1,0:T(8,128)(2,1)} %tokens_ref.5) | copy-start | bytes 1572868
  4.0 27.1 %copy-start = (bf16[2048,160]{0,1:T(8,128)(2,1)S(1)}, bf16[2048,160]{0,1:T(8,128)(2,1)}, u32[]{:S(2)}) copy-start(bf16[2048,160]{0,1:T(8,128)(2,1)} %param.4) | copy-start | bytes 1966084
  4.0 12.2 %collective-permute-start.5 = (bf16[160,256]{1,0:T(8,128)(2,1)S(1)}, bf16[160,256]{1,0:T(8,128)(2,1)S(1)}, u32[]{:S(2)}, u32[]{:S(2)}) collective-permute-start(bf16[160,256]{1,0:T(8,128)(2,1)S(1)} %get-tuple-element.20), channel_id=1, source_target_pairs={{2,0},{3,1},{0,2},{1,3},{6,4},{7,5},{4,6},{5,7},{10,8},{11,9},{8,1... | collective-permute-start | bytes 245768 | tf_op jit(solution)/shard_map/ppermute | solution.py:210
  16.2 4.9 %collective-permute-start.6 = (bf16[160,256]{1,0:T(8,128)(2,1)S(1)}, bf16[160,256]{1,0:T(8,128)(2,1)S(1)}, u32[]{:S(2)}, u32[]{:S(2)}) collective-permute-start(bf16[160,256]{1,0:T(8,128)(2,1)S(1)} %collective-permute-done.5.refs_0_), channel_id=1, source_target_pairs={{0,8},{4,12},{8,0},{12,4},{16,24},{20,28},{24,16},{28,20},{1,9},{5... | collective-permute-start | bytes 245768 | tf_op jit(solution)/shard_map/ppermute | solution.py:194
  17.7 5.3 %collective-permute-start.7 = (bf16[160,256]{1,0:T(8,128)(2,1)S(1)}, bf16[160,256]{1,0:T(8,128)(2,1)S(1)}, u32[]{:S(2)}, u32[]{:S(2)}) collective-permute-start(bf16[160,256]{1,0:T(8,128)(2,1)S(1)} %collective-permute-done.5.refs_0_), channel_id=1, source_target_pairs={{0,16},{4,20},{8,24},{12,28},{16,0},{20,4},{24,8},{28,12},{1,17},{... | collective-permute-start | bytes 245768 | tf_op jit(solution)/shard_map/ppermute | solution.py:194
  19.2 5.3 %collective-permute-start.8 = (bf16[160,256]{1,0:T(8,128)(2,1)S(1)}, bf16[160,256]{1,0:T(8,128)(2,1)S(1)}, u32[]{:S(2)}, u32[]{:S(2)}) collective-permute-start(bf16[160,256]{1,0:T(8,128)(2,1)S(1)} %collective-permute-done.5.refs_0_), channel_id=1, source_target_pairs={{0,24},{4,28},{8,16},{12,20},{16,8},{20,12},{24,0},{28,4},{1,25},{... | collective-permute-start | bytes 245768 | tf_op jit(solution)/shard_map/ppermute | solution.py:194
  19.7 4.9 %collective-permute-start.9 = (bf16[160,256]{1,0:T(8,128)(2,1)S(1)}, bf16[160,256]{1,0:T(8,128)(2,1)S(1)}, u32[]{:S(2)}, u32[]{:S(2)}) collective-permute-start(bf16[160,256]{1,0:T(8,128)(2,1)S(1)} %collective-permute-done.5.refs_0_), channel_id=1, source_target_pairs={{0,4},{4,0},{8,12},{12,8},{16,20},{20,16},{24,28},{28,24},{1,5},{5... | collective-permute-start | bytes 245768 | tf_op jit(solution)/shard_map/ppermute | solution.py:194
  21.1 4.1 %collective-permute-start.10 = (bf16[160,256]{1,0:T(8,128)(2,1)S(1)}, bf16[160,256]{1,0:T(8,128)(2,1)S(1)}, u32[]{:S(2)}, u32[]{:S(2)}) collective-permute-start(bf16[160,256]{1,0:T(8,128)(2,1)S(1)} %collective-permute-done.6.refs_1_), channel_id=1, source_target_pairs={{0,4},{4,0},{8,12},{12,8},{16,20},{20,16},{24,28},{28,24},{1,5},{5... | collective-permute-start | bytes 245768 | tf_op jit(solution)/shard_map/ppermute | solution.py:194
  22.9 3.0 %collective-permute-start.11 = (bf16[160,256]{1,0:T(8,128)(2,1)S(1)}, bf16[160,256]{1,0:T(8,128)(2,1)S(1)}, u32[]{:S(2)}, u32[]{:S(2)}) collective-permute-start(bf16[160,256]{1,0:T(8,128)(2,1)S(1)} %collective-permute-done.7.refs_2_), channel_id=1, source_target_pairs={{0,4},{4,0},{8,12},{12,8},{16,20},{20,16},{24,28},{28,24},{1,5},{5... | collective-permute-start | bytes 245768 | tf_op jit(solution)/shard_map/ppermute | solution.py:194
  24.6 2.0 %collective-permute-start.12 = (bf16[160,256]{1,0:T(8,128)(2,1)S(1)}, bf16[160,256]{1,0:T(8,128)(2,1)S(1)}, u32[]{:S(2)}, u32[]{:S(2)}) collective-permute-start(bf16[160,256]{1,0:T(8,128)(2,1)S(1)} %collective-permute-done.8.refs_3_), channel_id=1, source_target_pairs={{0,4},{4,0},{8,12},{12,8},{16,20},{20,16},{24,28},{28,24},{1,5},{5... | collective-permute-start | bytes 245768 | tf_op jit(solution)/shard_map/ppermute | solution.py:194
  24.6 7.1 %collective-permute-start.3 = (bf16[8,2048]{1,0:T(8,128)(2,1)S(1)}, bf16[8,2048]{1,0:T(8,128)(2,1)S(1)}, u32[]{:S(2)}, u32[]{:S(2)}) collective-permute-start(bf16[8,2048]{1,0:T(8,128)(2,1)S(1)} %get-tuple-element.17), channel_id=1, source_target_pairs={{3,7},{7,11},{11,15},{15,19},{19,23},{23,27},{27,31}} | collective-permute-start | bytes 98312 | tf_op jit(solution)/shard_map/ppermute | solution.py:218
  25.2 6.5 %collective-permute-start.2 = (bf16[8,2048]{1,0:T(8,128)(2,1)S(1)}, bf16[8,2048]{1,0:T(8,128)(2,1)S(1)}, u32[]{:S(2)}, u32[]{:S(2)}) collective-permute-start(bf16[8,2048]{1,0:T(8,128)(2,1)S(1)} %get-tuple-element.17), channel_id=1, source_target_pairs={{3,6},{7,10},{11,14},{15,18},{19,22},{23,26},{27,30}} | collective-permute-start | bytes 98312 | tf_op jit(solution)/shard_map/ppermute | solution.py:218
  25.9 5.9 %collective-permute-start = (bf16[8,2048]{1,0:T(8,128)(2,1)S(1)}, bf16[8,2048]{1,0:T(8,128)(2,1)S(1)}, u32[]{:S(2)}, u32[]{:S(2)}) collective-permute-start(bf16[8,2048]{1,0:T(8,128)(2,1)S(1)} %get-tuple-element.17), channel_id=1, source_target_pairs={{3,4},{7,8},{11,12},{15,16},{19,20},{23,24},{27,28}} | collective-permute-start | bytes 98312 | tf_op jit(solution)/shard_map/ppermute | solution.py:218
  26.6 5.2 %collective-permute-start.1 = (bf16[8,2048]{1,0:T(8,128)(2,1)S(1)}, bf16[8,2048]{1,0:T(8,128)(2,1)S(1)}, u32[]{:S(2)}, u32[]{:S(2)}) collective-permute-start(bf16[8,2048]{1,0:T(8,128)(2,1)S(1)} %get-tuple-element.17), channel_id=1, source_target_pairs={{3,5},{7,9},{11,13},{15,17},{19,21},{23,25},{27,29}} | collective-permute-start | bytes 98312 | tf_op jit(solution)/shard_map/ppermute | solution.py:218
  27.7 5.4 %collective-permute-start.13 = (bf16[160,128]{1,0:T(8,128)(2,1)S(1)}, bf16[160,128]{1,0:T(8,128)(2,1)S(1)}, u32[]{:S(2)}, u32[]{:S(2)}) collective-permute-start(bf16[160,128]{1,0:T(8,128)(2,1)S(1)} %shard_map.40), channel_id=1, source_target_pairs={{0,2},{1,3},{2,0},{3,1},{4,6},{5,7},{6,4},{7,5},{8,10},{9,11},{10,... | collective-permute-start | bytes 122888 | tf_op jit(solution)/shard_map/ppermute | solution.py:232
  31.7 6.5 %collective-permute-start.14 = (bf16[160,128]{1,0:T(8,128)(2,1)S(1)}, bf16[160,128]{1,0:T(8,128)(2,1)S(1)}, u32[]{:S(2)}, u32[]{:S(2)}) collective-permute-start(bf16[160,128]{1,0:T(8,128)(2,1)S(1)} %get-tuple-element.22), channel_id=1, source_target_pairs={{0,2},{1,3},{2,0},{3,1},{4,6},{5,7},{6,4},{7,5},{8,10},{9,11},{10,... | collective-permute-start | bytes 122888 | tf_op jit(solution)/shard_map/ppermute | solution.py:232
  32.3 5.8 %copy-start.2 = (f32[4,160]{1,0:T(4,128)S(1)}, f32[4,160]{1,0:T(4,128)}, u32[]{:S(2)}) copy-start(f32[4,160]{1,0:T(4,128)} %conv_ref.1) | copy-start | bytes 7684
  39.5 1.3 %collective-permute-start.15 = (f32[168,128]{1,0:T(8,128)S(1)}, f32[168,128]{1,0:T(8,128)S(1)}, u32[]{:S(2)}, u32[]{:S(2)}) collective-permute-start(f32[168,128]{1,0:T(8,128)S(1)} %get-tuple-element.28), channel_id=1, source_target_pairs={{0,4},{4,0},{8,12},{12,8},{16,20},{20,16},{24,28},{28,24},{1,5},{5... | collective-permute-start | bytes 258056 | tf_op jit(solution)/shard_map/ppermute | solution.py:194
  40.9 4.7 %collective-permute-start.16 = (f32[168,128]{1,0:T(8,128)S(1)}, f32[168,128]{1,0:T(8,128)S(1)}, u32[]{:S(2)}, u32[]{:S(2)}) collective-permute-start(f32[168,128]{1,0:T(8,128)S(1)} %get-tuple-element.29), channel_id=1, source_target_pairs={{0,8},{4,12},{8,0},{12,4},{16,24},{20,28},{24,16},{28,20},{1,9},{5... | collective-permute-start | bytes 258056 | tf_op jit(solution)/shard_map/ppermute | solution.py:264
  42.5 6.3 %collective-permute-start.17 = (f32[168,128]{1,0:T(8,128)S(1)}, f32[168,128]{1,0:T(8,128)S(1)}, u32[]{:S(2)}, u32[]{:S(2)}) collective-permute-start(f32[168,128]{1,0:T(8,128)S(1)} %get-tuple-element.29), channel_id=1, source_target_pairs={{0,16},{4,20},{8,24},{12,28},{16,0},{20,4},{24,8},{28,12},{1,17},{... | collective-permute-start | bytes 258056 | tf_op jit(solution)/shard_map/ppermute | solution.py:264
  42.6 6.2 %collective-permute-start.18 = (f32[168,128]{1,0:T(8,128)S(1)}, f32[168,128]{1,0:T(8,128)S(1)}, u32[]{:S(2)}, u32[]{:S(2)}) collective-permute-start(f32[168,128]{1,0:T(8,128)S(1)} %get-tuple-element.29), channel_id=1, source_target_pairs={{0,24},{4,28},{8,16},{12,20},{16,8},{20,12},{24,0},{28,4},{1,25},{... | collective-permute-start | bytes 258056 | tf_op jit(solution)/shard_map/ppermute | solution.py:264

commit v4 on v2

--- a/solution.py
+++ b/solution.py
@@ -67,10 +67,12 @@
     weight_copy.wait()
 
 
-def own_kernel(tail_ref, tokens_ref, weight_ref, halo_ref, own_ref):
-    weight = weight_ref[...]
-    depth = weight.shape[1]
-    own_ref[...] = dot_last(weight, tokens_ref[...]).astype(BF16)
+def own_kernel(tokens_ref, weight_ref, own_ref):
+    own_ref[...] = dot_last(weight_ref[...], tokens_ref[...]).astype(BF16)
+
+
+def halo_kernel(tail_ref, weight_ref, halo_ref):
+    depth = weight_ref.shape[1]
     cuts = tail_ref[...].astype(F32)
     lag = cuts.shape[0] // PIECES
     rows = [jnp.zeros((halo_ref.shape[1] - lag, depth), F32)]
@@ -80,15 +82,15 @@
             jnp.concatenate([cuts[first + i : first + i + 1, :] for i in range(PIECES)], axis=1)
         )
     padded = jnp.concatenate(rows, axis=0).astype(BF16)
-    halo_ref[...] = dot_last(weight, padded).astype(BF16)
-
-
-def gathered(share, tokens_ref, pieces):
+    halo_ref[...] = dot_last(weight_ref[...], padded).astype(BF16)
+
+
+def gathered(share, tokens_ref, pieces, height):
     depth = pieces[0].shape[1]
     total = None
     for index, piece in zip((0, 2, 4, 6, 1, 3, 5, 7), pieces):
         start = pl.multiple_of((share ^ index) * depth, depth)
-        part = dot_last(piece[...], tokens_ref[:, pl.ds(start, depth)])
+        part = dot_last(piece[:height, :], tokens_ref[:, pl.ds(start, depth)])
         total = part if total is None else total + part
     return total.astype(BF16)
 
@@ -98,7 +100,7 @@
     count = len(refs) // (PIECES + 1)
     for turn in range(count):
         refs[PIECES * count + turn][...] = gathered(
-            share, tokens_ref, refs[PIECES * turn : PIECES * turn + PIECES]
+            share, tokens_ref, refs[PIECES * turn : PIECES * turn + PIECES], refs[-1].shape[0]
         )
 
 
@@ -107,7 +109,7 @@
     count = len(refs) // (PIECES + 1)
     for turn in range(count):
         refs[PIECES * count + turn][...] = gathered(
-            share, tokens_ref, refs[PIECES * turn : PIECES * turn + PIECES]
+            share, tokens_ref, refs[PIECES * turn : PIECES * turn + PIECES], refs[-1].shape[0]
         )
     refs[-1][...] = dot_last(weight_ref[...], tokens_ref[...]).astype(BF16)
 
@@ -211,8 +213,7 @@
         return lax.ppermute(array, "ctx", [(i, i ^ bit) for i in range(ctx)])
 
     side = share.astype(jnp.int32).reshape(1)
-    lag = conv_weight.shape[0] - 1
-    cut_rows = PIECES * lag
+    cut_rows = PIECES * (conv_weight.shape[0] - 1)
     mine, tail = call(
         pack_kernel,
         [
@@ -224,23 +225,36 @@
         [pltpu.VMEM((HALO, depth), BF16), pltpu.SemaphoreType.DMA((2,))],
         space=HBM,
     )
-    pieces = []
+    shape = jax.ShapeDtypeStruct((row_width, rows), BF16)
+    work = 2 * rows * depth * row_width
+    row = lax.broadcasted_iota(jnp.int32, mine.shape, 0)
+    replaced = (row >= row_width) & (head == tp - 1)
+    pieces, tails = [], []
     for turn in turns:
         first = lax.ppermute(mine, "tp", [((z + 2 * turn) % tp, z) for z in range(tp)])
-        tail = jnp.where(head + 2 * turn == tp - 1, first[row_width:], tail)
-        first = first[:row_width]
+        first = jnp.where(replaced, mine, first)
         parts = [first] + [swap(first, bits) for bits in (2, 4, 6)]
-        pieces += parts + [swap(part, 1) for part in parts]
+        parts += [swap(part, 1) for part in parts]
+        pieces += parts
+        one, two, three = (part[row_width:] for part in (parts[4], parts[5], parts[7]))
+        tails.append(jnp.where(me & 1 == 1, one, jnp.where(me & 2 == 2, two, three)))
+    tail = tails[0]
+    for turn in turns[1:]:
+        tail = jnp.where(head + 2 * turn == tp - 1, tails[turn - 1], tail)
+    odd = range(1, tp, 2)
+    if ctx > PIECES:
+        last = jnp.where(head == tp - 1, mine, first)[row_width:]
+        for turn in turns:
+            last = jnp.where(head + 2 * turn == tp - 1, pieces[PIECES * turn - PIECES][row_width:], last)
+        pairs = [((c - 1) * tp + z, c * tp + z) for c in range(PIECES, ctx, PIECES) for z in odd]
+        tail = jnp.where(me % PIECES == 0, lax.ppermute(last, both, pairs), tail)
+    else:
+        tail = jnp.where(me == 0, jnp.zeros_like(tail), tail)
+    beside = lax.ppermute(tail, "tp", [(z, z - 1) for z in odd])
+    tail = jnp.where(head % 2 == 1, tail, beside)
     paired = lax.ppermute(tokens, "tp", [(z, z ^ 1) for z in range(tp)])
-
-    pairs = [(c * tp + z, (c + 1) * tp + z) for c in range(ctx - 1) for z in range(1, tp, 2)]
-    ahead = lax.ppermute(tail, both, pairs)
-    beside = lax.ppermute(ahead, "tp", [(z, z - 1) for z in range(1, tp, 2)])
-    tail = ahead + beside
-
-    shape = jax.ShapeDtypeStruct((row_width, rows), BF16)
-    work = 2 * rows * depth * row_width
-    halo, own = call(own_kernel, [shape] * 2, [tail, tokens, weight], flops=2 * work)
+    own = call(own_kernel, [shape], [tokens, weight], flops=work)[0]
+    halo = call(halo_kernel, [shape], [tail, weight], flops=work)[0]
     early = call(early_kernel, [shape] * len(turns), [side, tokens] + pieces, 1, flops=work)
     *late, other = call(
         late_kernel, [shape] * (len(turns) + 1), [side, paired, weight] + pieces, 1, flops=2 * work

time: 47.4 us -> 48.2 us (1.017)
  Pallas kernels: 5.37 us -> 6.19 us
  waiting for transfers between devices: 22.9 us -> 23.6 us
  starting transfers between devices: 18.5 us -> 17.9 us
    ppermute x2 -> x1, waiting for transfers between devices: 1.67 us -> 3.9 us  [per_device(): beside = lax.ppermute(tail, 'tp', [(z, z - 1) for z in odd])]
    ppermute x2, waiting for transfers between devices: 2.72 us -> 0.59 us  [per_device(): blocks += [lax.ppermute(one, 'tp', pairs), lax.ppermute(two, 'tp', pairs)]]
    ppermute x8, waiting for transfers between devices: 5.37 us -> 6.52 us  [swap(): return lax.ppermute(array, 'ctx', [(i, i ^ bit) for i in range(ctx)])]
    pallas_call x7 -> x8, Pallas kernels: 5.37 us -> 6.19 us  [call(): pl.pallas_call(kernel, out_shape=outs, in_specs=[SMEM] * scalars + [space...]
    ppermute x2 -> x1, starting transfers between devices: 1.93 us -> 1.28 us  [per_device(): beside = lax.ppermute(tail, 'tp', [(z, z - 1) for z in odd])]
    ppermute x1, waiting for transfers between devices: 9.77 us -> 9.12 us  [per_device(): lax.ppermute(mine, 'tp', [((z + 2 * turn) % tp, z) for z in range(tp)])]
  transfers between devices with their start and end apart: 17 -> 16, of which waited for: 10 -> 12; matrix products, arithmetic and copies ran while one was open for 0% -> 0% of each run, Pallas kernels for 6% -> 8%
where the time goes in v4:
time: 48.2 us; the launch traced here: 48.1 us
  waiting for transfers between devices  23.6 us (49%)
  starting transfers between devices  17.9 us (37%)
  Pallas kernels  6.19 us (13%)
    ppermute x1, waiting for transfers between devices, per_device(): lax.ppermute(mine, 'tp', [((z + 2 * turn) % tp, z) for z in range(tp)])  9.12 us
    ppermute x8, waiting for transfers between devices, swap(): return lax.ppermute(array, 'ctx', [(i, i ^ bit) for i in range(ctx)])  6.52 us
    pallas_call x8, Pallas kernels, call(): pl.pallas_call(kernel, out_shape=outs, in_specs=[SMEM] * scalars + [space...  6.19 us
    ppermute x1, waiting for transfers between devices, per_device(): beside = lax.ppermute(tail, 'tp', [(z, z - 1) for z in odd])  3.9 us
    ppermute x8, starting transfers between devices, swap(): return lax.ppermute(array, 'ctx', [(i, i ^ bit) for i in range(ctx)])  3.7 us
    ppermute x3, starting transfers between devices, per_device(): parts.append(lax.ppermute(total, 'ctx', pairs))  3.62 us
    ppermute x2, starting transfers between devices, per_device(): blocks += [lax.ppermute(one, 'tp', pairs), lax.ppermute(two, 'tp', pairs)]  3.55 us
    ppermute x3, waiting for transfers between devices, per_device(): parts.append(lax.ppermute(total, 'ctx', pairs))  3.51 us
  transfers between devices with their start and end apart: 16, of which 12 were waited for; matrix products, arithmetic and copies ran while one was open for 0% of the time, Pallas kernels for 8%

profile of v4, /device:TPU:0, one launch (start us, length us, event | category | flops | bytes accessed | tf_op | source)
XLA Modules:
  0.0 48.1 jit_solution(3049552942957357852)
XLA Ops:
  0.0 3.1 %collective-permute-start.7 = (bf16[128,2048]{1,0:T(8,128)(2,1)}, bf16[128,2048]{1,0:T(8,128)(2,1)S(1)}, u32[]{:S(2)}, u32[]{:S(2)}) collective-permute-start(bf16[128,2048]{1,0:T(8,128)(2,1)} %tokens_ref.5), channel_id=1, source_target_pairs={{0,1},{1,0},{2,3},{3,2},{4,5},{5,4},{6,7},{7,6},{8,9},{9,8},{10,11... | collective-permute-start | bytes 1572872 | tf_op jit(solution)/shard_map/ppermute | solution.py:255
  3.1 1.6 %shard_map.37 = (bf16[184,256]{1,0:T(8,128)(2,1)S(1)}, bf16[24,256]{1,0:T(8,128)(2,1)}) custom-call(s32[1]{0:T(128)} %bitcast.4.share_ref, bf16[160,2048]{1,0:T(8,128)(2,1)} %bitcast.6, bf16[128,2048]{1,0:T(8,128)(2,1)} %tokens_ref.5), custom_call_target="tpu_custom_call" | custom-call | flops 1048576 | bytes 1048576 | tf_op jit(solution)/shard_map/pallas_call | solution.py:28
  4.7 2.7 %collective-permute-start = (bf16[184,256]{1,0:T(8,128)(2,1)S(1)}, bf16[184,256]{1,0:T(8,128)(2,1)S(1)}, u32[]{:S(2)}, u32[]{:S(2)}) collective-permute-start(bf16[184,256]{1,0:T(8,128)(2,1)S(1)} %get-tuple-element.14), channel_id=1, source_target_pairs={{2,0},{3,1},{0,2},{1,3},{6,4},{7,5},{4,6},{5,7},{10,8},{11,9},{8,1... | collective-permute-start | bytes 282632 | tf_op jit(solution)/shard_map/ppermute | solution.py:234
  7.3 9.1 %collective-permute-done = bf16[184,256]{1,0:T(8,128)(2,1)S(1)} collective-permute-done((bf16[184,256]{1,0:T(8,128)(2,1)S(1)}, bf16[184,256]{1,0:T(8,128)(2,1)S(1)}, u32[]{:S(2)}, u32[]{:S(2)}) %collective-permute-start) | collective-permute-done | bytes 94240 | tf_op jit(solution)/shard_map/ppermute | solution.py:234
  16.6 1.6 %collective-permute-start.2 = (bf16[184,256]{1,0:T(8,128)(2,1)S(1)}, bf16[184,256]{1,0:T(8,128)(2,1)S(1)}, u32[]{:S(2)}, u32[]{:S(2)}) collective-permute-start(bf16[184,256]{1,0:T(8,128)(2,1)S(1)} %broadcast_select_fusion.refs_0_), channel_id=1, source_target_pairs={{0,8},{4,12},{8,0},{12,4},{16,24},{20,28},{24,16},{28,20},{1,9},{5... | collective-permute-start | bytes 282632 | tf_op jit(solution)/shard_map/ppermute | solution.py:213
  18.1 1.5 %collective-permute-start.4 = (bf16[184,256]{1,0:T(8,128)(2,1)S(1)}, bf16[184,256]{1,0:T(8,128)(2,1)S(1)}, u32[]{:S(2)}, u32[]{:S(2)}) collective-permute-start(bf16[184,256]{1,0:T(8,128)(2,1)S(1)} %broadcast_select_fusion.refs_0_), channel_id=1, source_target_pairs={{0,24},{4,28},{8,16},{12,20},{16,8},{20,12},{24,0},{28,4},{1,25},{... | collective-permute-start | bytes 282632 | tf_op jit(solution)/shard_map/ppermute | solution.py:213
  20.5 1.5 %collective-permute-done.2.refs_1_ = bf16[184,256]{1,0:T(8,128)(2,1)S(1)} collective-permute-done((bf16[184,256]{1,0:T(8,128)(2,1)S(1)}, bf16[184,256]{1,0:T(8,128)(2,1)S(1)}, u32[]{:S(2)}, u32[]{:S(2)}) %collective-permute-start.2) | collective-permute-done | bytes 94240 | tf_op jit(solution)/shard_map/ppermute | solution.py:213
  22.0 1.6 %collective-permute-done.4.refs_3_ = bf16[184,256]{1,0:T(8,128)(2,1)S(1)} collective-permute-done((bf16[184,256]{1,0:T(8,128)(2,1)S(1)}, bf16[184,256]{1,0:T(8,128)(2,1)S(1)}, u32[]{:S(2)}, u32[]{:S(2)}) %collective-permute-start.4) | collective-permute-done | bytes 94240 | tf_op jit(solution)/shard_map/ppermute | solution.py:213
  23.6 1.0 %collective-permute-done.8.refs_2_ = bf16[184,256]{1,0:T(8,128)(2,1)S(1)} collective-permute-done((bf16[184,256]{1,0:T(8,128)(2,1)S(1)}, bf16[184,256]{1,0:T(8,128)(2,1)S(1)}, u32[]{:S(2)}, u32[]{:S(2)}) %collective-permute-start.8) | collective-permute-done | bytes 94240 | tf_op jit(solution)/shard_map/ppermute | solution.py:213
  24.9 1.0 %collective-permute-done.9.refs_6_ = bf16[184,256]{1,0:T(8,128)(2,1)S(1)} collective-permute-done((bf16[184,256]{1,0:T(8,128)(2,1)S(1)}, bf16[184,256]{1,0:T(8,128)(2,1)S(1)}, u32[]{:S(2)}, u32[]{:S(2)}) %collective-permute-start.9) | collective-permute-done | bytes 94240 | tf_op jit(solution)/shard_map/ppermute | solution.py:213
  26.2 3.4 %collective-permute-start.10 = (bf16[160,128]{1,0:T(8,128)(2,1)S(1)}, bf16[160,128]{1,0:T(8,128)(2,1)S(1)}, u32[]{:S(2)}, u32[]{:S(2)}) collective-permute-start(bf16[160,128]{1,0:T(8,128)(2,1)S(1)} %shard_map.41), channel_id=1, source_target_pairs={{0,2},{1,3},{2,0},{3,1},{4,6},{5,7},{6,4},{7,5},{8,10},{9,11},{10,... | collective-permute-start | bytes 122888 | tf_op jit(solution)/shard_map/ppermute | solution.py:266
  29.7 1.3 %collective-permute-start.6 = (bf16[24,256]{1,0:T(8,128)(2,1)S(1)}, bf16[24,256]{1,0:T(8,128)(2,1)S(1)}, u32[]{:S(2)}, u32[]{:S(2)}) collective-permute-start(bf16[24,256]{1,0:T(8,128)(2,1)S(1)} %fusion.1), channel_id=1, source_target_pairs={{1,0},{3,2},{5,4},{7,6},{9,8},{11,10},{13,12},{15,14},{17,16},{19,... | collective-permute-start | bytes 36872 | tf_op jit(solution)/shard_map/ppermute | solution.py:253
  31.0 0.5 %shard_map.40 = (bf16[160,128]{1,0:T(8,128)(2,1)S(1)}, bf16[160,128]{1,0:T(8,128)(2,1)S(1)}) custom-call(s32[1]{0:T(128)} %bitcast.4.share_ref, bf16[128,2048]{1,0:T(8,128)(2,1)S(1)} %collective-permute-done.7.tokens_ref, bf16[160,2048]{1,0:T(8,128)(2,1)S(1)} %bitcast.8, bf16[184,256]{1,0:T(8,128)(2,1)S(1)} %broadcast_select_fusion.refs_0_, ...), custom_call_target="tpu_custom_call" | custom-call | flops 167772160 | bytes 1048576 | tf_op jit(solution)/shard_map/pallas_call | solution.py:28
  31.6 3.9 %collective-permute-done.6 = bf16[24,256]{1,0:T(8,128)(2,1)S(1)} collective-permute-done((bf16[24,256]{1,0:T(8,128)(2,1)S(1)}, bf16[24,256]{1,0:T(8,128)(2,1)S(1)}, u32[]{:S(2)}, u32[]{:S(2)}) %collective-permute-start.6) | collective-permute-done | bytes 12320 | tf_op jit(solution)/shard_map/ppermute | solution.py:253
  35.9 0.6 %collective-permute-done.11.refs_3_ = bf16[160,128]{1,0:T(8,128)(2,1)S(1)} collective-permute-done((bf16[160,128]{1,0:T(8,128)(2,1)S(1)}, bf16[160,128]{1,0:T(8,128)(2,1)S(1)}, u32[]{:S(2)}, u32[]{:S(2)}) %collective-permute-start.11) | collective-permute-done | bytes 40992 | tf_op jit(solution)/shard_map/ppermute | solution.py:266
  36.5 1.3 %shard_map.42 = (bf16[512,160]{1,0:T(8,128)(2,1)S(1)}, bf16[160,512]{1,0:T(8,128)(2,1)S(1)}, bf16[128,512]{1,0:T(8,128)(2,1)S(1)}, f32[168,128]{1,0:T(8,128)S(1)}) custom-call(s32[4]{0:T(128)S(1)} %pad_add_fusion.place_ref, f32[4,160]{1,0:T(4,128)S(1)} %copy-done.2, bf16[160,128]{1,0:T(8,128)(2,1)S(1)} %shard_map.38.halo_ref, ...), custom_call_target="tpu_custom_call" | custom-call | flops 1048576 | bytes 1048576 | tf_op jit(solution)/shard_map/pallas_call | solution.py:28
  37.9 1.3 %collective-permute-done.12 = f32[168,128]{1,0:T(8,128)S(1)} collective-permute-done((f32[168,128]{1,0:T(8,128)S(1)}, f32[168,128]{1,0:T(8,128)S(1)}, u32[]{:S(2)}, u32[]{:S(2)}) %collective-permute-start.12) | collective-permute-done | bytes 86048 | tf_op jit(solution)/shard_map/ppermute | solution.py:213
  39.2 1.6 %collective-permute-start.15 = (f32[168,128]{1,0:T(8,128)S(1)}, f32[168,128]{1,0:T(8,128)S(1)}, u32[]{:S(2)}, u32[]{:S(2)}) collective-permute-start(f32[168,128]{1,0:T(8,128)S(1)} %get-tuple-element.23), channel_id=1, source_target_pairs={{0,24},{4,28},{8,16},{12,20},{16,8},{20,12},{24,0},{28,4},{1,25},{... | collective-permute-start | bytes 258056 | tf_op jit(solution)/shard_map/ppermute | solution.py:298
  40.8 0.6 %shard_map.43 = (f32[512,128]{1,0:T(8,128)S(1)}, f32[512,128]{1,0:T(8,128)S(1)}) custom-call(bf16[512,160]{1,0:T(8,128)(2,1)S(1)} %get-tuple-element.17.query_ref, bf16[160,512]{1,0:T(8,128)(2,1)S(1)} %get-tuple-element.18.key_ref, bf16[128,512]{1,0:T(8,128)(2,1)S(1)} %get-tuple-element.19.value_ref), custom_call_target="tpu_custom_call" | custom-call | flops 150994944 | bytes 1048576 | tf_op jit(solution)/shard_map/pallas_call | solution.py:28
  41.4 1.1 %collective-permute-start.14 = (f32[168,128]{1,0:T(8,128)S(1)}, f32[168,128]{1,0:T(8,128)S(1)}, u32[]{:S(2)}, u32[]{:S(2)}) collective-permute-start(f32[168,128]{1,0:T(8,128)S(1)} %get-tuple-element.23), channel_id=1, source_target_pairs={{0,16},{4,20},{8,24},{12,28},{16,0},{20,4},{24,8},{28,12},{1,17},{... | collective-permute-start | bytes 258056 | tf_op jit(solution)/shard_map/ppermute | solution.py:298
  42.5 1.0 %collective-permute-start.13 = (f32[168,128]{1,0:T(8,128)S(1)}, f32[168,128]{1,0:T(8,128)S(1)}, u32[]{:S(2)}, u32[]{:S(2)}) collective-permute-start(f32[168,128]{1,0:T(8,128)S(1)} %get-tuple-element.23), channel_id=1, source_target_pairs={{0,8},{4,12},{8,0},{12,4},{16,24},{20,28},{24,16},{28,20},{1,9},{5... | collective-permute-start | bytes 258056 | tf_op jit(solution)/shard_map/ppermute | solution.py:298
  43.5 1.4 %collective-permute-done.15 = f32[168,128]{1,0:T(8,128)S(1)} collective-permute-done((f32[168,128]{1,0:T(8,128)S(1)}, f32[168,128]{1,0:T(8,128)S(1)}, u32[]{:S(2)}, u32[]{:S(2)}) %collective-permute-start.15) | collective-permute-done | bytes 86048 | tf_op jit(solution)/shard_map/ppermute | solution.py:298
  44.9 1.7 %collective-permute-done.14 = f32[168,128]{1,0:T(8,128)S(1)} collective-permute-done((f32[168,128]{1,0:T(8,128)S(1)}, f32[168,128]{1,0:T(8,128)S(1)}, u32[]{:S(2)}, u32[]{:S(2)}) %collective-permute-start.14) | collective-permute-done | bytes 86048 | tf_op jit(solution)/shard_map/ppermute | solution.py:298
  47.0 1.0 %shard_map.44 = bf16[512,128]{1,0:T(8,128)(2,1)} custom-call(bf16[512,160]{1,0:T(8,128)(2,1)S(1)} %get-tuple-element.17.query_ref, f32[512,128]{1,0:T(8,128)S(1)} %get-tuple-element.20.numerator_ref, f32[512,128]{1,0:T(8,128)S(1)} %get-tuple-element.21.denominator_ref, f32[168,128]{1,0:T(8,128)S(1)} %get-tuple-element.24.refs_0_, ...), custom_call_target="tpu_custom_call" | custom-call | flops 62914560 | bytes 1048576 | tf_op jit(solution)/shard_map/pallas_call | solution.py:28
  (31 shorter events, 2.7 us)
Async XLA Ops:
  0.0 31.0 %collective-permute-start.7 = (bf16[128,2048]{1,0:T(8,128)(2,1)}, bf16[128,2048]{1,0:T(8,128)(2,1)S(1)}, u32[]{:S(2)}, u32[]{:S(2)}) collective-permute-start(bf16[128,2048]{1,0:T(8,128)(2,1)} %tokens_ref.5), channel_id=1, source_target_pairs={{0,1},{1,0},{2,3},{3,2},{4,5},{5,4},{6,7},{7,6},{8,9},{9,8},{10,11... | collective-permute-start | bytes 1572872 | tf_op jit(solution)/shard_map/ppermute | solution.py:255
  3.1 17.1 %copy-start = (bf16[2048,160]{0,1:T(8,128)(2,1)S(1)}, bf16[2048,160]{0,1:T(8,128)(2,1)}, u32[]{:S(2)}) copy-start(bf16[2048,160]{0,1:T(8,128)(2,1)} %param.4) | copy-start | bytes 1966084
  3.1 17.1 %copy-start.1 = (bf16[128,2048]{1,0:T(8,128)(2,1)S(1)}, bf16[128,2048]{1,0:T(8,128)(2,1)}, u32[]{:S(2)}) copy-start(bf16[128,2048]{1,0:T(8,128)(2,1)} %tokens_ref.5) | copy-start | bytes 1572868
  4.7 11.8 %collective-permute-start = (bf16[184,256]{1,0:T(8,128)(2,1)S(1)}, bf16[184,256]{1,0:T(8,128)(2,1)S(1)}, u32[]{:S(2)}, u32[]{:S(2)}) collective-permute-start(bf16[184,256]{1,0:T(8,128)(2,1)S(1)} %get-tuple-element.14), channel_id=1, source_target_pairs={{2,0},{3,1},{0,2},{1,3},{6,4},{7,5},{4,6},{5,7},{10,8},{11,9},{8,1... | collective-permute-start | bytes 282632 | tf_op jit(solution)/shard_map/ppermute | solution.py:234
  16.6 5.5 %collective-permute-start.2 = (bf16[184,256]{1,0:T(8,128)(2,1)S(1)}, bf16[184,256]{1,0:T(8,128)(2,1)S(1)}, u32[]{:S(2)}, u32[]{:S(2)}) collective-permute-start(bf16[184,256]{1,0:T(8,128)(2,1)S(1)} %broadcast_select_fusion.refs_0_), channel_id=1, source_target_pairs={{0,8},{4,12},{8,0},{12,4},{16,24},{20,28},{24,16},{28,20},{1,9},{5... | collective-permute-start | bytes 282632 | tf_op jit(solution)/shard_map/ppermute | solution.py:213
  18.1 5.5 %collective-permute-start.4 = (bf16[184,256]{1,0:T(8,128)(2,1)S(1)}, bf16[184,256]{1,0:T(8,128)(2,1)S(1)}, u32[]{:S(2)}, u32[]{:S(2)}) collective-permute-start(bf16[184,256]{1,0:T(8,128)(2,1)S(1)} %broadcast_select_fusion.refs_0_), channel_id=1, source_target_pairs={{0,24},{4,28},{8,16},{12,20},{16,8},{20,12},{24,0},{28,4},{1,25},{... | collective-permute-start | bytes 282632 | tf_op jit(solution)/shard_map/ppermute | solution.py:213
  19.6 5.0 %collective-permute-start.8 = (bf16[184,256]{1,0:T(8,128)(2,1)S(1)}, bf16[184,256]{1,0:T(8,128)(2,1)S(1)}, u32[]{:S(2)}, u32[]{:S(2)}) collective-permute-start(bf16[184,256]{1,0:T(8,128)(2,1)S(1)} %broadcast_select_fusion.refs_0_), channel_id=1, source_target_pairs={{0,16},{4,20},{8,24},{12,28},{16,0},{20,4},{24,8},{28,12},{1,17},{... | collective-permute-start | bytes 282632 | tf_op jit(solution)/shard_map/ppermute | solution.py:213
  20.5 4.2 %collective-permute-start.1 = (bf16[184,256]{1,0:T(8,128)(2,1)S(1)}, bf16[184,256]{1,0:T(8,128)(2,1)S(1)}, u32[]{:S(2)}, u32[]{:S(2)}) collective-permute-start(bf16[184,256]{1,0:T(8,128)(2,1)S(1)} %broadcast_select_fusion.refs_0_), channel_id=1, source_target_pairs={{0,4},{4,0},{8,12},{12,8},{16,20},{20,16},{24,28},{28,24},{1,5},{5... | collective-permute-start | bytes 282632 | tf_op jit(solution)/shard_map/ppermute | solution.py:213
  22.0 2.7 %collective-permute-start.3 = (bf16[184,256]{1,0:T(8,128)(2,1)S(1)}, bf16[184,256]{1,0:T(8,128)(2,1)S(1)}, u32[]{:S(2)}, u32[]{:S(2)}) collective-permute-start(bf16[184,256]{1,0:T(8,128)(2,1)S(1)} %collective-permute-done.2.refs_1_), channel_id=1, source_target_pairs={{0,4},{4,0},{8,12},{12,8},{16,20},{20,16},{24,28},{28,24},{1,5},{5... | collective-permute-start | bytes 282632 | tf_op jit(solution)/shard_map/ppermute | solution.py:213
  23.6 1.3 %collective-permute-start.5 = (bf16[184,256]{1,0:T(8,128)(2,1)S(1)}, bf16[184,256]{1,0:T(8,128)(2,1)S(1)}, u32[]{:S(2)}, u32[]{:S(2)}) collective-permute-start(bf16[184,256]{1,0:T(8,128)(2,1)S(1)} %collective-permute-done.4.refs_3_), channel_id=1, source_target_pairs={{0,4},{4,0},{8,12},{12,8},{16,20},{20,16},{24,28},{28,24},{1,5},{5... | collective-permute-start | bytes 282632 | tf_op jit(solution)/shard_map/ppermute | solution.py:213
  24.6 1.3 %collective-permute-start.9 = (bf16[184,256]{1,0:T(8,128)(2,1)S(1)}, bf16[184,256]{1,0:T(8,128)(2,1)S(1)}, u32[]{:S(2)}, u32[]{:S(2)}) collective-permute-start(bf16[184,256]{1,0:T(8,128)(2,1)S(1)} %collective-permute-done.8.refs_2_), channel_id=1, source_target_pairs={{0,4},{4,0},{8,12},{12,8},{16,20},{20,16},{24,28},{28,24},{1,5},{5... | collective-permute-start | bytes 282632 | tf_op jit(solution)/shard_map/ppermute | solution.py:213
  26.2 9.7 %collective-permute-start.10 = (bf16[160,128]{1,0:T(8,128)(2,1)S(1)}, bf16[160,128]{1,0:T(8,128)(2,1)S(1)}, u32[]{:S(2)}, u32[]{:S(2)}) collective-permute-start(bf16[160,128]{1,0:T(8,128)(2,1)S(1)} %shard_map.41), channel_id=1, source_target_pairs={{0,2},{1,3},{2,0},{3,1},{4,6},{5,7},{6,4},{7,5},{8,10},{9,11},{10,... | collective-permute-start | bytes 122888 | tf_op jit(solution)/shard_map/ppermute | solution.py:266
  29.7 5.8 %collective-permute-start.6 = (bf16[24,256]{1,0:T(8,128)(2,1)S(1)}, bf16[24,256]{1,0:T(8,128)(2,1)S(1)}, u32[]{:S(2)}, u32[]{:S(2)}) collective-permute-start(bf16[24,256]{1,0:T(8,128)(2,1)S(1)} %fusion.1), channel_id=1, source_target_pairs={{1,0},{3,2},{5,4},{7,6},{9,8},{11,10},{13,12},{15,14},{17,16},{19,... | collective-permute-start | bytes 36872 | tf_op jit(solution)/shard_map/ppermute | solution.py:253
  31.5 5.0 %collective-permute-start.11 = (bf16[160,128]{1,0:T(8,128)(2,1)S(1)}, bf16[160,128]{1,0:T(8,128)(2,1)S(1)}, u32[]{:S(2)}, u32[]{:S(2)}) collective-permute-start(bf16[160,128]{1,0:T(8,128)(2,1)S(1)} %get-tuple-element.16), channel_id=1, source_target_pairs={{0,2},{1,3},{2,0},{3,1},{4,6},{5,7},{6,4},{7,5},{8,10},{9,11},{10,... | collective-permute-start | bytes 122888 | tf_op jit(solution)/shard_map/ppermute | solution.py:266
  35.5 1.0 %copy-start.2 = (f32[4,160]{1,0:T(4,128)S(1)}, f32[4,160]{1,0:T(4,128)}, u32[]{:S(2)}) copy-start(f32[4,160]{1,0:T(4,128)} %conv_ref.1) | copy-start | bytes 7684
  37.9 1.3 %collective-permute-start.12 = (f32[168,128]{1,0:T(8,128)S(1)}, f32[168,128]{1,0:T(8,128)S(1)}, u32[]{:S(2)}, u32[]{:S(2)}) collective-permute-start(f32[168,128]{1,0:T(8,128)S(1)} %get-tuple-element.22), channel_id=1, source_target_pairs={{0,4},{4,0},{8,12},{12,8},{16,20},{20,16},{24,28},{28,24},{1,5},{5... | collective-permute-start | bytes 258056 | tf_op jit(solution)/shard_map/ppermute | solution.py:213
  39.2 5.6 %collective-permute-start.15 = (f32[168,128]{1,0:T(8,128)S(1)}, f32[168,128]{1,0:T(8,128)S(1)}, u32[]{:S(2)}, u32[]{:S(2)}) collective-permute-start(f32[168,128]{1,0:T(8,128)S(1)} %get-tuple-element.23), channel_id=1, source_target_pairs={{0,24},{4,28},{8,16},{12,20},{16,8},{20,12},{24,0},{28,4},{1,25},{... | collective-permute-start | bytes 258056 | tf_op jit(solution)/shard_map/ppermute | solution.py:298
  41.4 5.2 %collective-permute-start.14 = (f32[168,128]{1,0:T(8,128)S(1)}, f32[168,128]{1,0:T(8,128)S(1)}, u32[]{:S(2)}, u32[]{:S(2)}) collective-permute-start(f32[168,128]{1,0:T(8,128)S(1)} %get-tuple-element.23), channel_id=1, source_target_pairs={{0,16},{4,20},{8,24},{12,28},{16,0},{20,4},{24,8},{28,12},{1,17},{... | collective-permute-start | bytes 258056 | tf_op jit(solution)/shard_map/ppermute | solution.py:298
  42.5 4.5 %collective-permute-start.13 = (f32[168,128]{1,0:T(8,128)S(1)}, f32[168,128]{1,0:T(8,128)S(1)}, u32[]{:S(2)}, u32[]{:S(2)}) collective-permute-start(f32[168,128]{1,0:T(8,128)S(1)} %get-tuple-element.23), channel_id=1, source_target_pairs={{0,8},{4,12},{8,0},{12,4},{16,24},{20,28},{24,16},{28,20},{1,9},{5... | collective-permute-start | bytes 258056 | tf_op jit(solution)/shard_map/ppermute | solution.py:298

commit v5 on v3

--- a/solution.py
+++ b/solution.py
@@ -66,33 +66,24 @@
     halo_ref[...] = dot_last(weight, padded).astype(BF16)
 
 
-def gathered(share, tokens_ref, pieces):
-    depth = pieces[0].shape[1]
-    total = None
-    for index, piece in zip((0, 2, 4, 6, 1, 3, 5, 7), pieces):
-        start = pl.multiple_of((share ^ index) * depth, depth)
-        part = dot_last(piece[...], tokens_ref[:, pl.ds(start, depth)])
-        total = part if total is None else total + part
-    return total.astype(BF16)
-
-
-def early_kernel(share_ref, tokens_ref, *refs):
+def second_kernel(share_ref, tokens_ref, paired_ref, weight_ref, *refs):
     share = share_ref[0]
-    count = len(refs) // (PIECES + 1)
+    count = (len(refs) - 1) // (PIECES + 1)
+    height, rows = refs[-1].shape
     for turn in range(count):
-        refs[PIECES * count + turn][...] = gathered(
-            share, tokens_ref, refs[PIECES * turn : PIECES * turn + PIECES]
-        )
-
-
-def late_kernel(share_ref, tokens_ref, weight_ref, *refs):
-    share = share_ref[0]
-    count = len(refs) // (PIECES + 1)
-    for turn in range(count):
-        refs[PIECES * count + turn][...] = gathered(
-            share, tokens_ref, refs[PIECES * turn : PIECES * turn + PIECES]
-        )
-    refs[-1][...] = dot_last(weight_ref[...], tokens_ref[...]).astype(BF16)
+        total = None
+        for index, piece in zip((0, 2, 4, 6, 1, 3, 5, 7), refs[PIECES * turn : PIECES * turn + PIECES]):
+            depth = piece.shape[1]
+            start = pl.multiple_of((share ^ index) * depth, depth)
+            both = jnp.concatenate(
+                [tokens_ref[:, pl.ds(start, depth)], paired_ref[:, pl.ds(start, depth)]], axis=0
+            )
+            part = dot_last(piece[...], both)
+            total = part if total is None else total + part
+        out_ref = refs[PIECES * count + turn]
+        out_ref[:height, :] = total[:, :rows].astype(BF16)
+        out_ref[height:, :] = total[:, rows:].astype(BF16)
+    refs[-1][...] = dot_last(weight_ref[...], paired_ref[...]).astype(BF16)
 
 
 def features(raw, weighted):
@@ -112,14 +103,17 @@
 
 def feature_kernel(place_ref, conv_ref, halo_ref, *refs):
     count = place_ref.shape[0]
-    blocks = refs[:count]
-    query_ref, key_ref, value_ref, state_ref, wide = refs[count:]
+    query_ref, key_ref, value_ref, state_ref, wide = refs[-5:]
     width = halo_ref.shape[1]
+    height = wide.shape[0]
+    blocks = [refs[0][...], refs[1][...]]
+    for message in refs[2:-5]:
+        blocks += [message[:height, :], message[height:, :]]
     local_rows = width * count
     wide[:, :width] = halo_ref[...].astype(F32)
     for index, block in enumerate(blocks):
         start = pl.multiple_of((place_ref[index] + 1) * width, LANES)
-        wide[:, pl.ds(start, width)] = block[...].astype(F32)
+        wide[:, pl.ds(start, width)] = block.astype(F32)
     padded = wide[...]
     convolved = jnp.zeros((padded.shape[0], local_rows), F32)
     taps = conv_ref[...].T
@@ -221,15 +215,18 @@
     shape = jax.ShapeDtypeStruct((row_width, rows), BF16)
     work = 2 * rows * depth * row_width
     halo, own = call(own_kernel, [shape] * 2, [tail, tokens, weight], flops=2 * work)
-    early = call(early_kernel, [shape] * len(turns), [side, tokens] + pieces, 1, flops=work)
-    *late, other = call(
-        late_kernel, [shape] * (len(turns) + 1), [side, paired, weight] + pieces, 1, flops=2 * work
+    pair_shape = jax.ShapeDtypeStruct((2 * row_width, rows), BF16)
+    *messages, other = call(
+        second_kernel,
+        [pair_shape] * len(turns) + [shape],
+        [side, tokens, paired, weight] + pieces,
+        1,
+        flops=3 * work,
     )
     blocks, places = [own, other], [head, head ^ 1]
-    for turn, one, two in zip(turns, early, late):
-        pairs = [(z, (z + 2 * turn) % tp) for z in range(tp)]
+    for turn, message in zip(turns, messages):
+        blocks.append(lax.ppermute(message, "tp", [(z, (z + 2 * turn) % tp) for z in range(tp)]))
         source = (head + tp - 2 * turn) % tp
-        blocks += [lax.ppermute(one, "tp", pairs), lax.ppermute(two, "tp", pairs)]
         places += [source, source ^ 1]
     place = jnp.stack(places).astype(jnp.int32)
     query, key, value, state = call(

time: 50.1 us -> 49.1 us (0.980)
  waiting for transfers between devices: 25 us -> 21.8 us
  starting transfers between devices: 19.2 us -> 21.6 us
    ppermute x2 -> x1, waiting for transfers between devices: 5.82 us -> 2.64 us  [per_device(): lax.ppermute(message, 'tp', [(z, (z + 2 * turn) % tp) for z in range(tp)])]
    ppermute x8, starting transfers between devices: 3.67 us -> 5.18 us  [swap(): return lax.ppermute(array, 'ctx', [(i, i ^ bit) for i in range(ctx)])]
    ppermute x3, starting transfers between devices: 3.62 us -> 4.61 us  [per_device(): parts.append(lax.ppermute(total, 'ctx', pairs))]
    pallas_call x7 -> x6, Pallas kernels: 5.34 us -> 5.18 us  [call(): pl.pallas_call(kernel, out_shape=outs, in_specs=[SMEM] * scalars + [space...]
    ppermute x2 -> x1, starting transfers between devices: 3.54 us -> 3.45 us  [per_device(): lax.ppermute(message, 'tp', [(z, (z + 2 * turn) % tp) for z in range(tp)])]
  transfers between devices with their start and end apart: 19 -> 18, of which waited for: 9 -> 8; matrix products, arithmetic and copies ran while one was open for 0% -> 0% of each run, Pallas kernels for 6% -> 6%
where the time goes in v5:
time: 49.1 us; the launch traced here: 48.9 us
  waiting for transfers between devices  21.8 us (44%)
  starting transfers between devices  21.6 us (44%)
  Pallas kernels  5.18 us (11%)
    ppermute x1, waiting for transfers between devices, per_device(): lax.ppermute(mine, 'tp', [((z + 2 * turn) % tp, z) for z in range(tp)])  9.52 us
    ppermute x8, waiting for transfers between devices, swap(): return lax.ppermute(array, 'ctx', [(i, i ^ bit) for i in range(ctx)])  5.79 us
    pallas_call x6, Pallas kernels, call(): pl.pallas_call(kernel, out_shape=outs, in_specs=[SMEM] * scalars + [space...  5.18 us
    ppermute x8, starting transfers between devices, swap(): return lax.ppermute(array, 'ctx', [(i, i ^ bit) for i in range(ctx)])  5.18 us
    ppermute x3, starting transfers between devices, per_device(): parts.append(lax.ppermute(total, 'ctx', pairs))  4.61 us
    ppermute x3, waiting for transfers between devices, per_device(): parts.append(lax.ppermute(total, 'ctx', pairs))  3.87 us
    ppermute x1, starting transfers between devices, per_device(): lax.ppermute(message, 'tp', [(z, (z + 2 * turn) % tp) for z in range(tp)])  3.45 us
    ppermute x1, starting transfers between devices, per_device(): paired = lax.ppermute(tokens, 'tp', [(z, z ^ 1) for z in range(tp)])  3.05 us
  transfers between devices with their start and end apart: 18, of which 8 were waited for; matrix products, arithmetic and copies ran while one was open for 0% of the time, Pallas kernels for 6%

profile of v5, /device:TPU:0, one launch (start us, length us, event | category | flops | bytes accessed | tf_op | source)
XLA Modules:
  0.0 48.9 jit_solution(1593546028738788206)
XLA Ops:
  0.0 3.1 %collective-permute-start.4 = (bf16[128,2048]{1,0:T(8,128)(2,1)}, bf16[128,2048]{1,0:T(8,128)(2,1)S(1)}, u32[]{:S(2)}, u32[]{:S(2)}) collective-permute-start(bf16[128,2048]{1,0:T(8,128)(2,1)} %tokens_ref.5), channel_id=1, source_target_pairs={{0,1},{1,0},{2,3},{3,2},{4,5},{5,4},{6,7},{7,6},{8,9},{9,8},{10,11... | collective-permute-start | bytes 1572872 | tf_op jit(solution)/shard_map/ppermute | solution.py:207
  3.1 1.0 %shard_map.37 = (bf16[160,256]{1,0:T(8,128)(2,1)S(1)}, bf16[8,2048]{1,0:T(8,128)(2,1)S(1)}) custom-call(s32[1]{0:T(128)} %bitcast.4.share_ref, bf16[160,2048]{1,0:T(8,128)(2,1)} %bitcast.6, bf16[128,2048]{1,0:T(8,128)(2,1)} %tokens_ref.5), custom_call_target="tpu_custom_call" | custom-call | flops 1048576 | bytes 1048576 | tf_op jit(solution)/shard_map/pallas_call | solution.py:28
  4.0 2.7 %collective-permute-start.5 = (bf16[160,256]{1,0:T(8,128)(2,1)S(1)}, bf16[160,256]{1,0:T(8,128)(2,1)S(1)}, u32[]{:S(2)}, u32[]{:S(2)}) collective-permute-start(bf16[160,256]{1,0:T(8,128)(2,1)S(1)} %get-tuple-element.20), channel_id=1, source_target_pairs={{2,0},{3,1},{0,2},{1,3},{6,4},{7,5},{4,6},{5,7},{10,8},{11,9},{8,1... | collective-permute-start | bytes 245768 | tf_op jit(solution)/shard_map/ppermute | solution.py:204
  6.7 9.5 %collective-permute-done.5.refs_0_ = bf16[160,256]{1,0:T(8,128)(2,1)S(1)} collective-permute-done((bf16[160,256]{1,0:T(8,128)(2,1)S(1)}, bf16[160,256]{1,0:T(8,128)(2,1)S(1)}, u32[]{:S(2)}, u32[]{:S(2)}) %collective-permute-start.5) | collective-permute-done | bytes 81952 | tf_op jit(solution)/shard_map/ppermute | solution.py:204
  16.2 1.5 %collective-permute-start.6 = (bf16[160,256]{1,0:T(8,128)(2,1)S(1)}, bf16[160,256]{1,0:T(8,128)(2,1)S(1)}, u32[]{:S(2)}, u32[]{:S(2)}) collective-permute-start(bf16[160,256]{1,0:T(8,128)(2,1)S(1)} %collective-permute-done.5.refs_0_), channel_id=1, source_target_pairs={{0,8},{4,12},{8,0},{12,4},{16,24},{20,28},{24,16},{28,20},{1,9},{5... | collective-permute-start | bytes 245768 | tf_op jit(solution)/shard_map/ppermute | solution.py:188
  17.7 1.5 %collective-permute-start.7 = (bf16[160,256]{1,0:T(8,128)(2,1)S(1)}, bf16[160,256]{1,0:T(8,128)(2,1)S(1)}, u32[]{:S(2)}, u32[]{:S(2)}) collective-permute-start(bf16[160,256]{1,0:T(8,128)(2,1)S(1)} %collective-permute-done.5.refs_0_), channel_id=1, source_target_pairs={{0,16},{4,20},{8,24},{12,28},{16,0},{20,4},{24,8},{28,12},{1,17},{... | collective-permute-start | bytes 245768 | tf_op jit(solution)/shard_map/ppermute | solution.py:188
  19.7 1.4 %collective-permute-done.6.refs_1_ = bf16[160,256]{1,0:T(8,128)(2,1)S(1)} collective-permute-done((bf16[160,256]{1,0:T(8,128)(2,1)S(1)}, bf16[160,256]{1,0:T(8,128)(2,1)S(1)}, u32[]{:S(2)}, u32[]{:S(2)}) %collective-permute-start.6) | collective-permute-done | bytes 81952 | tf_op jit(solution)/shard_map/ppermute | solution.py:188
  21.1 1.8 %collective-permute-done.7.refs_2_ = bf16[160,256]{1,0:T(8,128)(2,1)S(1)} collective-permute-done((bf16[160,256]{1,0:T(8,128)(2,1)S(1)}, bf16[160,256]{1,0:T(8,128)(2,1)S(1)}, u32[]{:S(2)}, u32[]{:S(2)}) %collective-permute-start.7) | collective-permute-done | bytes 81952 | tf_op jit(solution)/shard_map/ppermute | solution.py:188
  23.0 1.6 %collective-permute-done.8.refs_3_ = bf16[160,256]{1,0:T(8,128)(2,1)S(1)} collective-permute-done((bf16[160,256]{1,0:T(8,128)(2,1)S(1)}, bf16[160,256]{1,0:T(8,128)(2,1)S(1)}, u32[]{:S(2)}, u32[]{:S(2)}) %collective-permute-start.8) | collective-permute-done | bytes 81952 | tf_op jit(solution)/shard_map/ppermute | solution.py:188
  25.2 0.7 %collective-permute-start.2 = (bf16[8,2048]{1,0:T(8,128)(2,1)S(1)}, bf16[8,2048]{1,0:T(8,128)(2,1)S(1)}, u32[]{:S(2)}, u32[]{:S(2)}) collective-permute-start(bf16[8,2048]{1,0:T(8,128)(2,1)S(1)} %get-tuple-element.17), channel_id=1, source_target_pairs={{3,6},{7,10},{11,14},{15,18},{19,22},{23,26},{27,30}} | collective-permute-start | bytes 98312 | tf_op jit(solution)/shard_map/ppermute | solution.py:212
  25.9 0.7 %collective-permute-start = (bf16[8,2048]{1,0:T(8,128)(2,1)S(1)}, bf16[8,2048]{1,0:T(8,128)(2,1)S(1)}, u32[]{:S(2)}, u32[]{:S(2)}) collective-permute-start(bf16[8,2048]{1,0:T(8,128)(2,1)S(1)} %get-tuple-element.17), channel_id=1, source_target_pairs={{3,4},{7,8},{11,12},{15,16},{19,20},{23,24},{27,28}} | collective-permute-start | bytes 98312 | tf_op jit(solution)/shard_map/ppermute | solution.py:212
  26.6 0.7 %collective-permute-start.1 = (bf16[8,2048]{1,0:T(8,128)(2,1)S(1)}, bf16[8,2048]{1,0:T(8,128)(2,1)S(1)}, u32[]{:S(2)}, u32[]{:S(2)}) collective-permute-start(bf16[8,2048]{1,0:T(8,128)(2,1)S(1)} %get-tuple-element.17), channel_id=1, source_target_pairs={{3,5},{7,9},{11,13},{15,17},{19,21},{23,25},{27,29}} | collective-permute-start | bytes 98312 | tf_op jit(solution)/shard_map/ppermute | solution.py:212
  27.4 0.7 %shard_map.39 = (bf16[320,128]{1,0:T(8,128)(2,1)S(1)}, bf16[160,128]{1,0:T(8,128)(2,1)S(1)}) custom-call(s32[1]{0:T(128)} %bitcast.4.share_ref, bf16[128,2048]{1,0:T(8,128)(2,1)S(1)} %copy-done.1, bf16[128,2048]{1,0:T(8,128)(2,1)S(1)} %collective-permute-done.4.paired_ref, bf16[160,2048]{1,0:T(8,128)(2,1)S(1)} %bitcast.7, ...), custom_call_target="tpu_custom_call" | custom-call | flops 251658240 | bytes 1048576 | tf_op jit(solution)/shard_map/pallas_call | solution.py:28
  28.0 3.4 %collective-permute-start.13 = (bf16[320,128]{1,0:T(8,128)(2,1)S(1)}, bf16[320,128]{1,0:T(8,128)(2,1)S(1)}, u32[]{:S(2)}, u32[]{:S(2)}) collective-permute-start(bf16[320,128]{1,0:T(8,128)(2,1)S(1)} %get-tuple-element.22), channel_id=1, source_target_pairs={{0,2},{1,3},{2,0},{3,1},{4,6},{5,7},{6,4},{7,5},{8,10},{9,11},{10,... | collective-permute-start | bytes 245768 | tf_op jit(solution)/shard_map/ppermute | solution.py:228
  32.1 2.6 %collective-permute-done.13.refs_2_ = bf16[320,128]{1,0:T(8,128)(2,1)S(1)} collective-permute-done((bf16[320,128]{1,0:T(8,128)(2,1)S(1)}, bf16[320,128]{1,0:T(8,128)(2,1)S(1)}, u32[]{:S(2)}, u32[]{:S(2)}) %collective-permute-start.13) | collective-permute-done | bytes 81952 | tf_op jit(solution)/shard_map/ppermute | solution.py:228
  34.7 1.3 %shard_map.40 = (bf16[512,160]{1,0:T(8,128)(2,1)S(1)}, bf16[160,512]{1,0:T(8,128)(2,1)S(1)}, bf16[128,512]{1,0:T(8,128)(2,1)S(1)}, f32[168,128]{1,0:T(8,128)S(1)}) custom-call(s32[4]{0:T(128)S(1)} %pad_add_fusion.place_ref, f32[4,160]{1,0:T(4,128)S(1)} %copy-done.2, bf16[160,128]{1,0:T(8,128)(2,1)S(1)} %get-tuple-element.18.halo_ref, ...), custom_call_target="tpu_custom_call" | custom-call | flops 1048576 | bytes 1048576 | tf_op jit(solution)/shard_map/pallas_call | solution.py:28
  36.0 1.7 %collective-permute-start.14 = (f32[168,128]{1,0:T(8,128)S(1)}, f32[168,128]{1,0:T(8,128)S(1)}, u32[]{:S(2)}, u32[]{:S(2)}) collective-permute-start(f32[168,128]{1,0:T(8,128)S(1)} %get-tuple-element.28), channel_id=1, source_target_pairs={{0,4},{4,0},{8,12},{12,8},{16,20},{20,16},{24,28},{28,24},{1,5},{5... | collective-permute-start | bytes 258056 | tf_op jit(solution)/shard_map/ppermute | solution.py:188
  37.7 0.9 %collective-permute-done.14 = f32[168,128]{1,0:T(8,128)S(1)} collective-permute-done((f32[168,128]{1,0:T(8,128)S(1)}, f32[168,128]{1,0:T(8,128)S(1)}, u32[]{:S(2)}, u32[]{:S(2)}) %collective-permute-start.14) | collective-permute-done | bytes 86048 | tf_op jit(solution)/shard_map/ppermute | solution.py:188
  38.7 1.4 %collective-permute-start.15 = (f32[168,128]{1,0:T(8,128)S(1)}, f32[168,128]{1,0:T(8,128)S(1)}, u32[]{:S(2)}, u32[]{:S(2)}) collective-permute-start(f32[168,128]{1,0:T(8,128)S(1)} %get-tuple-element.29), channel_id=1, source_target_pairs={{0,8},{4,12},{8,0},{12,4},{16,24},{20,28},{24,16},{28,20},{1,9},{5... | collective-permute-start | bytes 258056 | tf_op jit(solution)/shard_map/ppermute | solution.py:261
  40.8 1.7 %collective-permute-start.16 = (f32[168,128]{1,0:T(8,128)S(1)}, f32[168,128]{1,0:T(8,128)S(1)}, u32[]{:S(2)}, u32[]{:S(2)}) collective-permute-start(f32[168,128]{1,0:T(8,128)S(1)} %get-tuple-element.29), channel_id=1, source_target_pairs={{0,16},{4,20},{8,24},{12,28},{16,0},{20,4},{24,8},{28,12},{1,17},{... | collective-permute-start | bytes 258056 | tf_op jit(solution)/shard_map/ppermute | solution.py:261
  42.4 1.5 %collective-permute-start.17 = (f32[168,128]{1,0:T(8,128)S(1)}, f32[168,128]{1,0:T(8,128)S(1)}, u32[]{:S(2)}, u32[]{:S(2)}) collective-permute-start(f32[168,128]{1,0:T(8,128)S(1)} %get-tuple-element.29), channel_id=1, source_target_pairs={{0,24},{4,28},{8,16},{12,20},{16,8},{20,12},{24,0},{28,4},{1,25},{... | collective-permute-start | bytes 258056 | tf_op jit(solution)/shard_map/ppermute | solution.py:261
  43.9 2.5 %collective-permute-done.16 = f32[168,128]{1,0:T(8,128)S(1)} collective-permute-done((f32[168,128]{1,0:T(8,128)S(1)}, f32[168,128]{1,0:T(8,128)S(1)}, u32[]{:S(2)}, u32[]{:S(2)}) %collective-permute-start.16) | collective-permute-done | bytes 86048 | tf_op jit(solution)/shard_map/ppermute | solution.py:261
  46.4 1.4 %collective-permute-done.17 = f32[168,128]{1,0:T(8,128)S(1)} collective-permute-done((f32[168,128]{1,0:T(8,128)S(1)}, f32[168,128]{1,0:T(8,128)S(1)}, u32[]{:S(2)}, u32[]{:S(2)}) %collective-permute-start.17) | collective-permute-done | bytes 86048 | tf_op jit(solution)/shard_map/ppermute | solution.py:261
  47.8 1.0 %shard_map.42 = bf16[512,128]{1,0:T(8,128)(2,1)} custom-call(bf16[512,160]{1,0:T(8,128)(2,1)S(1)} %get-tuple-element.23.query_ref, f32[512,128]{1,0:T(8,128)S(1)} %get-tuple-element.26.numerator_ref, f32[512,128]{1,0:T(8,128)S(1)} %get-tuple-element.27.denominator_ref, f32[168,128]{1,0:T(8,128)S(1)} %get-tuple-element.30.refs_0_, ...), custom_call_target="tpu_custom_call" | custom-call | flops 62914560 | bytes 1048576 | tf_op jit(solution)/shard_map/pallas_call | solution.py:28
  (30 shorter events, 2.4 us)
Async XLA Ops:
  0.0 27.4 %copy-start = (bf16[2048,160]{0,1:T(8,128)(2,1)S(1)}, bf16[2048,160]{0,1:T(8,128)(2,1)}, u32[]{:S(2)}) copy-start(bf16[2048,160]{0,1:T(8,128)(2,1)} %param.4) | copy-start | bytes 1966084
  0.0 27.3 %collective-permute-start.4 = (bf16[128,2048]{1,0:T(8,128)(2,1)}, bf16[128,2048]{1,0:T(8,128)(2,1)S(1)}, u32[]{:S(2)}, u32[]{:S(2)}) collective-permute-start(bf16[128,2048]{1,0:T(8,128)(2,1)} %tokens_ref.5), channel_id=1, source_target_pairs={{0,1},{1,0},{2,3},{3,2},{4,5},{5,4},{6,7},{7,6},{8,9},{9,8},{10,11... | collective-permute-start | bytes 1572872 | tf_op jit(solution)/shard_map/ppermute | solution.py:207
  3.1 24.3 %copy-start.1 = (bf16[128,2048]{1,0:T(8,128)(2,1)S(1)}, bf16[128,2048]{1,0:T(8,128)(2,1)}, u32[]{:S(2)}) copy-start(bf16[128,2048]{1,0:T(8,128)(2,1)} %tokens_ref.5) | copy-start | bytes 1572868
  4.0 12.2 %collective-permute-start.5 = (bf16[160,256]{1,0:T(8,128)(2,1)S(1)}, bf16[160,256]{1,0:T(8,128)(2,1)S(1)}, u32[]{:S(2)}, u32[]{:S(2)}) collective-permute-start(bf16[160,256]{1,0:T(8,128)(2,1)S(1)} %get-tuple-element.20), channel_id=1, source_target_pairs={{2,0},{3,1},{0,2},{1,3},{6,4},{7,5},{4,6},{5,7},{10,8},{11,9},{8,1... | collective-permute-start | bytes 245768 | tf_op jit(solution)/shard_map/ppermute | solution.py:204
  16.2 4.9 %collective-permute-start.6 = (bf16[160,256]{1,0:T(8,128)(2,1)S(1)}, bf16[160,256]{1,0:T(8,128)(2,1)S(1)}, u32[]{:S(2)}, u32[]{:S(2)}) collective-permute-start(bf16[160,256]{1,0:T(8,128)(2,1)S(1)} %collective-permute-done.5.refs_0_), channel_id=1, source_target_pairs={{0,8},{4,12},{8,0},{12,4},{16,24},{20,28},{24,16},{28,20},{1,9},{5... | collective-permute-start | bytes 245768 | tf_op jit(solution)/shard_map/ppermute | solution.py:188
  17.7 5.3 %collective-permute-start.7 = (bf16[160,256]{1,0:T(8,128)(2,1)S(1)}, bf16[160,256]{1,0:T(8,128)(2,1)S(1)}, u32[]{:S(2)}, u32[]{:S(2)}) collective-permute-start(bf16[160,256]{1,0:T(8,128)(2,1)S(1)} %collective-permute-done.5.refs_0_), channel_id=1, source_target_pairs={{0,16},{4,20},{8,24},{12,28},{16,0},{20,4},{24,8},{28,12},{1,17},{... | collective-permute-start | bytes 245768 | tf_op jit(solution)/shard_map/ppermute | solution.py:188
  19.2 5.3 %collective-permute-start.8 = (bf16[160,256]{1,0:T(8,128)(2,1)S(1)}, bf16[160,256]{1,0:T(8,128)(2,1)S(1)}, u32[]{:S(2)}, u32[]{:S(2)}) collective-permute-start(bf16[160,256]{1,0:T(8,128)(2,1)S(1)} %collective-permute-done.5.refs_0_), channel_id=1, source_target_pairs={{0,24},{4,28},{8,16},{12,20},{16,8},{20,12},{24,0},{28,4},{1,25},{... | collective-permute-start | bytes 245768 | tf_op jit(solution)/shard_map/ppermute | solution.py:188
  19.7 4.9 %collective-permute-start.9 = (bf16[160,256]{1,0:T(8,128)(2,1)S(1)}, bf16[160,256]{1,0:T(8,128)(2,1)S(1)}, u32[]{:S(2)}, u32[]{:S(2)}) collective-permute-start(bf16[160,256]{1,0:T(8,128)(2,1)S(1)} %collective-permute-done.5.refs_0_), channel_id=1, source_target_pairs={{0,4},{4,0},{8,12},{12,8},{16,20},{20,16},{24,28},{28,24},{1,5},{5... | collective-permute-start | bytes 245768 | tf_op jit(solution)/shard_map/ppermute | solution.py:188
  21.1 4.1 %collective-permute-start.10 = (bf16[160,256]{1,0:T(8,128)(2,1)S(1)}, bf16[160,256]{1,0:T(8,128)(2,1)S(1)}, u32[]{:S(2)}, u32[]{:S(2)}) collective-permute-start(bf16[160,256]{1,0:T(8,128)(2,1)S(1)} %collective-permute-done.6.refs_1_), channel_id=1, source_target_pairs={{0,4},{4,0},{8,12},{12,8},{16,20},{20,16},{24,28},{28,24},{1,5},{5... | collective-permute-start | bytes 245768 | tf_op jit(solution)/shard_map/ppermute | solution.py:188
  22.9 3.0 %collective-permute-start.11 = (bf16[160,256]{1,0:T(8,128)(2,1)S(1)}, bf16[160,256]{1,0:T(8,128)(2,1)S(1)}, u32[]{:S(2)}, u32[]{:S(2)}) collective-permute-start(bf16[160,256]{1,0:T(8,128)(2,1)S(1)} %collective-permute-done.7.refs_2_), channel_id=1, source_target_pairs={{0,4},{4,0},{8,12},{12,8},{16,20},{20,16},{24,28},{28,24},{1,5},{5... | collective-permute-start | bytes 245768 | tf_op jit(solution)/shard_map/ppermute | solution.py:188
  24.6 2.0 %collective-permute-start.12 = (bf16[160,256]{1,0:T(8,128)(2,1)S(1)}, bf16[160,256]{1,0:T(8,128)(2,1)S(1)}, u32[]{:S(2)}, u32[]{:S(2)}) collective-permute-start(bf16[160,256]{1,0:T(8,128)(2,1)S(1)} %collective-permute-done.8.refs_3_), channel_id=1, source_target_pairs={{0,4},{4,0},{8,12},{12,8},{16,20},{20,16},{24,28},{28,24},{1,5},{5... | collective-permute-start | bytes 245768 | tf_op jit(solution)/shard_map/ppermute | solution.py:188
  24.6 6.9 %collective-permute-start.3 = (bf16[8,2048]{1,0:T(8,128)(2,1)S(1)}, bf16[8,2048]{1,0:T(8,128)(2,1)S(1)}, u32[]{:S(2)}, u32[]{:S(2)}) collective-permute-start(bf16[8,2048]{1,0:T(8,128)(2,1)S(1)} %get-tuple-element.17), channel_id=1, source_target_pairs={{3,7},{7,11},{11,15},{15,19},{19,23},{23,27},{27,31}} | collective-permute-start | bytes 98312 | tf_op jit(solution)/shard_map/ppermute | solution.py:212
  25.2 6.3 %collective-permute-start.2 = (bf16[8,2048]{1,0:T(8,128)(2,1)S(1)}, bf16[8,2048]{1,0:T(8,128)(2,1)S(1)}, u32[]{:S(2)}, u32[]{:S(2)}) collective-permute-start(bf16[8,2048]{1,0:T(8,128)(2,1)S(1)} %get-tuple-element.17), channel_id=1, source_target_pairs={{3,6},{7,10},{11,14},{15,18},{19,22},{23,26},{27,30}} | collective-permute-start | bytes 98312 | tf_op jit(solution)/shard_map/ppermute | solution.py:212
  25.9 5.6 %collective-permute-start = (bf16[8,2048]{1,0:T(8,128)(2,1)S(1)}, bf16[8,2048]{1,0:T(8,128)(2,1)S(1)}, u32[]{:S(2)}, u32[]{:S(2)}) collective-permute-start(bf16[8,2048]{1,0:T(8,128)(2,1)S(1)} %get-tuple-element.17), channel_id=1, source_target_pairs={{3,4},{7,8},{11,12},{15,16},{19,20},{23,24},{27,28}} | collective-permute-start | bytes 98312 | tf_op jit(solution)/shard_map/ppermute | solution.py:212
  26.6 4.9 %collective-permute-start.1 = (bf16[8,2048]{1,0:T(8,128)(2,1)S(1)}, bf16[8,2048]{1,0:T(8,128)(2,1)S(1)}, u32[]{:S(2)}, u32[]{:S(2)}) collective-permute-start(bf16[8,2048]{1,0:T(8,128)(2,1)S(1)} %get-tuple-element.17), channel_id=1, source_target_pairs={{3,5},{7,9},{11,13},{15,17},{19,21},{23,25},{27,29}} | collective-permute-start | bytes 98312 | tf_op jit(solution)/shard_map/ppermute | solution.py:212
  28.0 6.7 %collective-permute-start.13 = (bf16[320,128]{1,0:T(8,128)(2,1)S(1)}, bf16[320,128]{1,0:T(8,128)(2,1)S(1)}, u32[]{:S(2)}, u32[]{:S(2)}) collective-permute-start(bf16[320,128]{1,0:T(8,128)(2,1)S(1)} %get-tuple-element.22), channel_id=1, source_target_pairs={{0,2},{1,3},{2,0},{3,1},{4,6},{5,7},{6,4},{7,5},{8,10},{9,11},{10,... | collective-permute-start | bytes 245768 | tf_op jit(solution)/shard_map/ppermute | solution.py:228
  32.0 2.7 %copy-start.2 = (f32[4,160]{1,0:T(4,128)S(1)}, f32[4,160]{1,0:T(4,128)}, u32[]{:S(2)}) copy-start(f32[4,160]{1,0:T(4,128)} %conv_ref.1) | copy-start | bytes 7684
  36.0 2.6 %collective-permute-start.14 = (f32[168,128]{1,0:T(8,128)S(1)}, f32[168,128]{1,0:T(8,128)S(1)}, u32[]{:S(2)}, u32[]{:S(2)}) collective-permute-start(f32[168,128]{1,0:T(8,128)S(1)} %get-tuple-element.28), channel_id=1, source_target_pairs={{0,4},{4,0},{8,12},{12,8},{16,20},{20,16},{24,28},{28,24},{1,5},{5... | collective-permute-start | bytes 258056 | tf_op jit(solution)/shard_map/ppermute | solution.py:188
  38.7 5.3 %collective-permute-start.15 = (f32[168,128]{1,0:T(8,128)S(1)}, f32[168,128]{1,0:T(8,128)S(1)}, u32[]{:S(2)}, u32[]{:S(2)}) collective-permute-start(f32[168,128]{1,0:T(8,128)S(1)} %get-tuple-element.29), channel_id=1, source_target_pairs={{0,8},{4,12},{8,0},{12,4},{16,24},{20,28},{24,16},{28,20},{1,9},{5... | collective-permute-start | bytes 258056 | tf_op jit(solution)/shard_map/ppermute | solution.py:261
  40.8 5.7 %collective-permute-start.16 = (f32[168,128]{1,0:T(8,128)S(1)}, f32[168,128]{1,0:T(8,128)S(1)}, u32[]{:S(2)}, u32[]{:S(2)}) collective-permute-start(f32[168,128]{1,0:T(8,128)S(1)} %get-tuple-element.29), channel_id=1, source_target_pairs={{0,16},{4,20},{8,24},{12,28},{16,0},{20,4},{24,8},{28,12},{1,17},{... | collective-permute-start | bytes 258056 | tf_op jit(solution)/shard_map/ppermute | solution.py:261
  42.4 5.4 %collective-permute-start.17 = (f32[168,128]{1,0:T(8,128)S(1)}, f32[168,128]{1,0:T(8,128)S(1)}, u32[]{:S(2)}, u32[]{:S(2)}) collective-permute-start(f32[168,128]{1,0:T(8,128)S(1)} %get-tuple-element.29), channel_id=1, source_target_pairs={{0,24},{4,28},{8,16},{12,20},{16,8},{20,12},{24,0},{28,4},{1,25},{... | collective-permute-start | bytes 258056 | tf_op jit(solution)/shard_map/ppermute | solution.py:261

commit v6 on v3

--- a/solution.py
+++ b/solution.py
@@ -15,7 +15,7 @@
 LANES = 128
 QUAD_FEATS = FEAT * (FEAT + 1) // 2
 NUM_FEAT = QUAD_FEATS + FEAT + 8
-STATE_ROWS = NUM_FEAT + 8
+HALF = (NUM_FEAT + 16) // 2
 F32 = jnp.float32
 BF16 = jnp.bfloat16
 HBM = pl.BlockSpec(memory_space=pltpu.HBM)
@@ -110,10 +110,10 @@
     return jnp.concatenate(parts, axis=0).astype(BF16)
 
 
-def feature_kernel(place_ref, conv_ref, halo_ref, *refs):
+def feature_kernel(place_ref, side_ref, conv_ref, halo_ref, *refs):
     count = place_ref.shape[0]
     blocks = refs[:count]
-    query_ref, key_ref, value_ref, state_ref, wide = refs[count:]
+    query_ref, key_ref, value_ref, kept_ref, sent_ref, wide, state_ref = refs[count:]
     width = halo_ref.shape[1]
     local_rows = width * count
     wide[:, :width] = halo_ref[...].astype(F32)
@@ -138,7 +138,12 @@
     rest = NUM_FEAT - lanes
     more = jnp.concatenate([total[:, lanes:], jnp.zeros((8, lanes - rest), F32)], axis=1)
     row = lax.broadcasted_iota(jnp.int32, (8, lanes), 0)
-    state_ref[NUM_FEAT:, :] = jnp.where(row == 0, total[:, :lanes], jnp.where(row == 1, more, 0.0))
+    rows = jnp.where(row == 0, total[:, :lanes], jnp.where(row == 1, more, 0.0))
+    state_ref[NUM_FEAT : NUM_FEAT + 8, :] = rows
+    state_ref[NUM_FEAT + 8 :, :] = jnp.zeros((2 * HALF - NUM_FEAT - 8, lanes), F32)
+    core = side_ref[0] % 2
+    kept_ref[...] = state_ref[pl.ds(pl.multiple_of(core * HALF, 8), HALF), :]
+    sent_ref[...] = state_ref[pl.ds(pl.multiple_of(HALF - core * HALF, 8), HALF), :]
 
 
 def inner_kernel(query_ref, key_ref, value_ref, numerator_ref, denominator_ref):
@@ -157,11 +162,11 @@
         )
 
 
-def finish_kernel(query_ref, numerator_ref, denominator_ref, *refs):
-    states, out_ref = refs[:-1], refs[-1]
-    state = states[0][...]
-    for other in states[1:]:
-        state += other[...]
+def finish_kernel(side_ref, query_ref, numerator_ref, denominator_ref, kept_ref, other_ref, out_ref, state_ref):
+    core = side_ref[0] % 2
+    state_ref[pl.ds(pl.multiple_of(core * HALF, 8), HALF), :] = kept_ref[...]
+    state_ref[pl.ds(pl.multiple_of(HALF - core * HALF, 8), HALF), :] = other_ref[...]
+    state = state_ref[...]
     width = numerator_ref.shape[1]
     query = query_ref[...]
     rest = state[:NUM_FEAT, :]
@@ -232,17 +237,18 @@
         blocks += [lax.ppermute(one, "tp", pairs), lax.ppermute(two, "tp", pairs)]
         places += [source, source ^ 1]
     place = jnp.stack(places).astype(jnp.int32)
-    query, key, value, state = call(
+    query, key, value, mine, theirs = call(
         feature_kernel,
         [
             jax.ShapeDtypeStruct((local_rows, NUM_FEAT), BF16),
             jax.ShapeDtypeStruct((NUM_FEAT, local_rows), BF16),
             jax.ShapeDtypeStruct((val_width, local_rows), BF16),
-            jax.ShapeDtypeStruct((STATE_ROWS, val_width), F32),
+            jax.ShapeDtypeStruct((HALF, val_width), F32),
+            jax.ShapeDtypeStruct((HALF, val_width), F32),
         ],
-        [place, conv_weight, halo] + blocks,
-        1,
-        [pltpu.VMEM((row_width, rows + local_rows), F32)],
+        [place, side, conv_weight, halo] + blocks,
+        2,
+        [pltpu.VMEM((row_width, rows + local_rows), F32), pltpu.VMEM((2 * HALF, val_width), F32)],
     )
     numerator, denominator = call(
         inner_kernel,
@@ -250,9 +256,10 @@
         [query, key, value],
         flops=2 * local_rows * local_rows * (NUM_FEAT + val_width),
     )
-    received = swap(state, 1)
-    terms = [jnp.where(me % 2 == 1, received, 0.0)]
-    total = state + received
+    core = me % 2
+    received = swap(theirs, 1)
+    total = mine + received
+    earlier = jnp.zeros_like(total)
     bit = 2
     while bit < ctx:
         radix = min(4, ctx // bit)
@@ -262,14 +269,18 @@
         for delta in range(1, radix):
             pairs = [(c, c ^ delta * bit) for c in range(ctx)]
             parts.append(lax.ppermute(total, "ctx", pairs))
-            terms.append(jnp.where(digit > digit ^ delta, parts[-1], 0.0))
+            earlier = earlier + jnp.where(digit > digit ^ delta, parts[-1], 0.0)
         if not last:
             total = functools.reduce(jnp.add, parts, total)
         bit *= radix
+    other = swap(earlier + jnp.where(core == 0, mine, 0.0), 1)
+    kept = earlier + jnp.where(core == 1, received, 0.0)
     return call(
         finish_kernel,
         [jax.ShapeDtypeStruct((local_rows, val_width), BF16)],
-        [query, numerator, denominator] + terms,
+        [side, query, numerator, denominator, kept, other],
+        1,
+        [pltpu.VMEM((2 * HALF, val_width), F32)],
         flops=6 * local_rows * NUM_FEAT * val_width,
     )[0]
 

time: 50.1 us -> 52.3 us (1.044)
  the two profiles are of different devices: /device:TPU:0 before, /device:TPU:13 now
where the time goes in v6:
time: 52.3 us; the launch traced here: 52.1 us
  starting transfers between devices  26.7 us (51%)
  waiting for transfers between devices  19.8 us (38%)
  Pallas kernels  5.35 us (10%)
    ppermute x9, starting transfers between devices, swap(): return lax.ppermute(array, 'ctx', [(i, i ^ bit) for i in range(ctx)])  12.7 us
    ppermute x1, waiting for transfers between devices, per_device(): lax.ppermute(mine, 'tp', [((z + 2 * turn) % tp, z) for z in range(tp)])  12 us
    ppermute x2, starting transfers between devices, per_device(): blocks += [lax.ppermute(one, 'tp', pairs), lax.ppermute(two, 'tp', pairs)]  5.55 us
    pallas_call x7, Pallas kernels, call(): pl.pallas_call(kernel, out_shape=outs, in_specs=[SMEM] * scalars + [space...  5.35 us
    ppermute x4, starting transfers between devices, per_device(): part = lax.ppermute(last_rows, both, pairs)  3.27 us
    ppermute x2, waiting for transfers between devices, per_device(): blocks += [lax.ppermute(one, 'tp', pairs), lax.ppermute(two, 'tp', pairs)]  3.17 us
    ppermute x3, waiting for transfers between devices, per_device(): parts.append(lax.ppermute(total, 'ctx', pairs))  2.85 us
    ppermute x3, starting transfers between devices, per_device(): parts.append(lax.ppermute(total, 'ctx', pairs))  2.65 us
  transfers between devices with their start and end apart: 20, of which 7 were waited for; matrix products, arithmetic and copies ran while one was open for 0% of the time, Pallas kernels for 6%

profile of v6, /device:TPU:13, one launch (start us, length us, event | category | flops | bytes accessed | tf_op | source)
XLA Modules:
  0.0 52.1 jit_solution(6830804555356794111)
XLA Ops:
  0.2 1.0 %shard_map.37 = (bf16[160,256]{1,0:T(8,128)(2,1)S(1)}, bf16[8,2048]{1,0:T(8,128)(2,1)S(1)}) custom-call(s32[1]{0:T(128)} %bitcast.share_ref.side_ref, bf16[160,2048]{1,0:T(8,128)(2,1)} %bitcast.6, bf16[128,2048]{1,0:T(8,128)(2,1)} %tokens_ref.5), custom_call_target="tpu_custom_call" | custom-call | flops 1048576 | bytes 1048576 | tf_op jit(solution)/shard_map/pallas_call | solution.py:28
  1.2 2.4 %collective-permute-start.5 = (bf16[160,256]{1,0:T(8,128)(2,1)S(1)}, bf16[160,256]{1,0:T(8,128)(2,1)S(1)}, u32[]{:S(2)}, u32[]{:S(2)}) collective-permute-start(bf16[160,256]{1,0:T(8,128)(2,1)S(1)} %get-tuple-element.21), channel_id=1, source_target_pairs={{2,0},{3,1},{0,2},{1,3},{6,4},{7,5},{4,6},{5,7},{10,8},{11,9},{8,1... | collective-permute-start | bytes 245768 | tf_op jit(solution)/shard_map/ppermute | solution.py:215
  3.5 12.0 %collective-permute-done.5.refs_0_ = bf16[160,256]{1,0:T(8,128)(2,1)S(1)} collective-permute-done((bf16[160,256]{1,0:T(8,128)(2,1)S(1)}, bf16[160,256]{1,0:T(8,128)(2,1)S(1)}, u32[]{:S(2)}, u32[]{:S(2)}) %collective-permute-start.5) | collective-permute-done | bytes 81952 | tf_op jit(solution)/shard_map/ppermute | solution.py:215
  15.5 1.2 %collective-permute-start.6 = (bf16[160,256]{1,0:T(8,128)(2,1)S(1)}, bf16[160,256]{1,0:T(8,128)(2,1)S(1)}, u32[]{:S(2)}, u32[]{:S(2)}) collective-permute-start(bf16[160,256]{1,0:T(8,128)(2,1)S(1)} %collective-permute-done.5.refs_0_), channel_id=1, source_target_pairs={{0,8},{4,12},{8,0},{12,4},{16,24},{20,28},{24,16},{28,20},{1,9},{5... | collective-permute-start | bytes 245768 | tf_op jit(solution)/shard_map/ppermute | solution.py:199
  16.9 1.2 %collective-permute-start.8 = (bf16[160,256]{1,0:T(8,128)(2,1)S(1)}, bf16[160,256]{1,0:T(8,128)(2,1)S(1)}, u32[]{:S(2)}, u32[]{:S(2)}) collective-permute-start(bf16[160,256]{1,0:T(8,128)(2,1)S(1)} %collective-permute-done.5.refs_0_), channel_id=1, source_target_pairs={{0,24},{4,28},{8,16},{12,20},{16,8},{20,12},{24,0},{28,4},{1,25},{... | collective-permute-start | bytes 245768 | tf_op jit(solution)/shard_map/ppermute | solution.py:199
  18.1 2.7 %collective-permute-start.9 = (bf16[160,256]{1,0:T(8,128)(2,1)S(1)}, bf16[160,256]{1,0:T(8,128)(2,1)S(1)}, u32[]{:S(2)}, u32[]{:S(2)}) collective-permute-start(bf16[160,256]{1,0:T(8,128)(2,1)S(1)} %collective-permute-done.5.refs_0_), channel_id=1, source_target_pairs={{0,4},{4,0},{8,12},{12,8},{16,20},{20,16},{24,28},{28,24},{1,5},{5... | collective-permute-start | bytes 245768 | tf_op jit(solution)/shard_map/ppermute | solution.py:199
  20.8 1.7 %collective-permute-start.10 = (bf16[160,256]{1,0:T(8,128)(2,1)S(1)}, bf16[160,256]{1,0:T(8,128)(2,1)S(1)}, u32[]{:S(2)}, u32[]{:S(2)}) collective-permute-start(bf16[160,256]{1,0:T(8,128)(2,1)S(1)} %collective-permute-done.6.refs_1_), channel_id=1, source_target_pairs={{0,4},{4,0},{8,12},{12,8},{16,20},{20,16},{24,28},{28,24},{1,5},{5... | collective-permute-start | bytes 245768 | tf_op jit(solution)/shard_map/ppermute | solution.py:199
  22.5 0.9 %collective-permute-start.11 = (bf16[160,256]{1,0:T(8,128)(2,1)S(1)}, bf16[160,256]{1,0:T(8,128)(2,1)S(1)}, u32[]{:S(2)}, u32[]{:S(2)}) collective-permute-start(bf16[160,256]{1,0:T(8,128)(2,1)S(1)} %collective-permute-done.7.refs_2_), channel_id=1, source_target_pairs={{0,4},{4,0},{8,12},{12,8},{16,20},{20,16},{24,28},{28,24},{1,5},{5... | collective-permute-start | bytes 245768 | tf_op jit(solution)/shard_map/ppermute | solution.py:199
  23.4 1.2 %collective-permute-start.12 = (bf16[160,256]{1,0:T(8,128)(2,1)S(1)}, bf16[160,256]{1,0:T(8,128)(2,1)S(1)}, u32[]{:S(2)}, u32[]{:S(2)}) collective-permute-start(bf16[160,256]{1,0:T(8,128)(2,1)S(1)} %collective-permute-done.8.refs_3_), channel_id=1, source_target_pairs={{0,4},{4,0},{8,12},{12,8},{16,20},{20,16},{24,28},{28,24},{1,5},{5... | collective-permute-start | bytes 245768 | tf_op jit(solution)/shard_map/ppermute | solution.py:199
  25.3 1.3 %collective-permute-start.1 = (bf16[8,2048]{1,0:T(8,128)(2,1)S(1)}, bf16[8,2048]{1,0:T(8,128)(2,1)S(1)}, u32[]{:S(2)}, u32[]{:S(2)}) collective-permute-start(bf16[8,2048]{1,0:T(8,128)(2,1)S(1)} %get-tuple-element.18), channel_id=1, source_target_pairs={{3,5},{7,9},{11,13},{15,17},{19,21},{23,25},{27,29}} | collective-permute-start | bytes 98312 | tf_op jit(solution)/shard_map/ppermute | solution.py:223
  26.6 0.7 %collective-permute-start.2 = (bf16[8,2048]{1,0:T(8,128)(2,1)S(1)}, bf16[8,2048]{1,0:T(8,128)(2,1)S(1)}, u32[]{:S(2)}, u32[]{:S(2)}) collective-permute-start(bf16[8,2048]{1,0:T(8,128)(2,1)S(1)} %get-tuple-element.18), channel_id=1, source_target_pairs={{3,6},{7,10},{11,14},{15,18},{19,22},{23,26},{27,30}} | collective-permute-start | bytes 98312 | tf_op jit(solution)/shard_map/ppermute | solution.py:223
  27.3 0.7 %collective-permute-start.3 = (bf16[8,2048]{1,0:T(8,128)(2,1)S(1)}, bf16[8,2048]{1,0:T(8,128)(2,1)S(1)}, u32[]{:S(2)}, u32[]{:S(2)}) collective-permute-start(bf16[8,2048]{1,0:T(8,128)(2,1)S(1)} %get-tuple-element.18), channel_id=1, source_target_pairs={{3,7},{7,11},{11,15},{15,19},{19,23},{23,27},{27,31}} | collective-permute-start | bytes 98312 | tf_op jit(solution)/shard_map/ppermute | solution.py:223
  28.4 5.5 %collective-permute-start.13 = (bf16[160,128]{1,0:T(8,128)(2,1)S(1)}, bf16[160,128]{1,0:T(8,128)(2,1)S(1)}, u32[]{:S(2)}, u32[]{:S(2)}) collective-permute-start(bf16[160,128]{1,0:T(8,128)(2,1)S(1)} %shard_map.40), channel_id=1, source_target_pairs={{0,2},{1,3},{2,0},{3,1},{4,6},{5,7},{6,4},{7,5},{8,10},{9,11},{10,... | collective-permute-start | bytes 122888 | tf_op jit(solution)/shard_map/ppermute | solution.py:237
  35.1 0.9 %collective-permute-done.13.refs_2_ = bf16[160,128]{1,0:T(8,128)(2,1)S(1)} collective-permute-done((bf16[160,128]{1,0:T(8,128)(2,1)S(1)}, bf16[160,128]{1,0:T(8,128)(2,1)S(1)}, u32[]{:S(2)}, u32[]{:S(2)}) %collective-permute-start.13) | collective-permute-done | bytes 40992 | tf_op jit(solution)/shard_map/ppermute | solution.py:237
  36.0 2.3 %collective-permute-done.14.refs_3_ = bf16[160,128]{1,0:T(8,128)(2,1)S(1)} collective-permute-done((bf16[160,128]{1,0:T(8,128)(2,1)S(1)}, bf16[160,128]{1,0:T(8,128)(2,1)S(1)}, u32[]{:S(2)}, u32[]{:S(2)}) %collective-permute-start.14) | collective-permute-done | bytes 40992 | tf_op jit(solution)/shard_map/ppermute | solution.py:237
  38.2 1.4 %shard_map.41 = (bf16[512,160]{1,0:T(8,128)(2,1)S(1)}, bf16[160,512]{1,0:T(8,128)(2,1)S(1)}, bf16[128,512]{1,0:T(8,128)(2,1)S(1)}, f32[88,128]{1,0:T(8,128)S(1)}, f32[88,128]{1,0:T(8,128)S(1)}) custom-call(s32[4]{0:T(128)S(1)} %pad_add_fusion.place_ref, s32[1]{0:T(128)} %bitcast.share_ref.side_ref, f32[4,160]{1,0:T(4,128)S(1)} %copy-done.2, ...), custom_call_target="tpu_custom_call" | custom-call | flops 1048576 | bytes 1048576 | tf_op jit(solution)/shard_map/pallas_call | solution.py:28
  39.6 1.4 %collective-permute-start.15 = (f32[88,128]{1,0:T(8,128)S(1)}, f32[88,128]{1,0:T(8,128)S(1)}, u32[]{:S(2)}, u32[]{:S(2)}) collective-permute-start(f32[88,128]{1,0:T(8,128)S(1)} %get-tuple-element.30), channel_id=1, source_target_pairs={{0,4},{4,0},{8,12},{12,8},{16,20},{20,16},{24,28},{28,24},{1,5},{5... | collective-permute-start | bytes 135176 | tf_op jit(solution)/shard_map/ppermute | solution.py:199
  41.0 0.9 %collective-permute-done.15 = f32[88,128]{1,0:T(8,128)S(1)} collective-permute-done((f32[88,128]{1,0:T(8,128)S(1)}, f32[88,128]{1,0:T(8,128)S(1)}, u32[]{:S(2)}, u32[]{:S(2)}) %collective-permute-start.15) | collective-permute-done | bytes 45088 | tf_op jit(solution)/shard_map/ppermute | solution.py:199
  42.1 2.1 %collective-permute-start.17 = (f32[88,128]{1,0:T(8,128)S(1)}, f32[88,128]{1,0:T(8,128)S(1)}, u32[]{:S(2)}, u32[]{:S(2)}) collective-permute-start(f32[88,128]{1,0:T(8,128)S(1)} %add.44), channel_id=1, source_target_pairs={{0,16},{4,20},{8,24},{12,28},{16,0},{20,4},{24,8},{28,12},{1,17},{... | collective-permute-start | bytes 135176 | tf_op jit(solution)/shard_map/ppermute | solution.py:271
  45.1 0.8 %collective-permute-done.17 = f32[88,128]{1,0:T(8,128)S(1)} collective-permute-done((f32[88,128]{1,0:T(8,128)S(1)}, f32[88,128]{1,0:T(8,128)S(1)}, u32[]{:S(2)}, u32[]{:S(2)}) %collective-permute-start.17) | collective-permute-done | bytes 45088 | tf_op jit(solution)/shard_map/ppermute | solution.py:271
  45.9 2.1 %collective-permute-done.18 = f32[88,128]{1,0:T(8,128)S(1)} collective-permute-done((f32[88,128]{1,0:T(8,128)S(1)}, f32[88,128]{1,0:T(8,128)S(1)}, u32[]{:S(2)}, u32[]{:S(2)}) %collective-permute-start.18) | collective-permute-done | bytes 45088 | tf_op jit(solution)/shard_map/ppermute | solution.py:271
  48.0 2.2 %collective-permute-start.19 = (f32[88,128]{1,0:T(8,128)S(1)}, f32[88,128]{1,0:T(8,128)S(1)}, u32[]{:S(2)}, u32[]{:S(2)}) collective-permute-start(f32[88,128]{1,0:T(8,128)S(1)} %get-tuple-element.31), channel_id=1, source_target_pairs={{0,4},{4,0},{8,12},{12,8},{16,20},{20,16},{24,28},{28,24},{1,5},{5... | collective-permute-start | bytes 135176 | tf_op jit(solution)/shard_map/ppermute | solution.py:199
  50.2 0.9 %collective-permute-done.19.other_ref = f32[88,128]{1,0:T(8,128)S(1)} collective-permute-done((f32[88,128]{1,0:T(8,128)S(1)}, f32[88,128]{1,0:T(8,128)S(1)}, u32[]{:S(2)}, u32[]{:S(2)}) %collective-permute-start.19) | collective-permute-done | bytes 45088 | tf_op jit(solution)/shard_map/ppermute | solution.py:199
  51.1 1.0 %shard_map.43 = bf16[512,128]{1,0:T(8,128)(2,1)} custom-call(s32[1]{0:T(128)} %bitcast.share_ref.side_ref, bf16[512,160]{1,0:T(8,128)(2,1)S(1)} %get-tuple-element.24.query_ref, f32[512,128]{1,0:T(8,128)S(1)} %get-tuple-element.27.numerator_ref, f32[512,128]{1,0:T(8,128)S(1)} %get-tuple-element.28.denominator_ref, f32[88,128]{1,0:T(8,128)S(1)} %select_add_fusion.1.kept_ref, ...), custom_call_target="tpu_custom_call" | custom-call | flops 62914560 | bytes 1048576 | tf_op jit(solution)/shard_map/pallas_call | solution.py:28
  (34 shorter events, 3.8 us)
Async XLA Ops:
  0.0 28.4 %collective-permute-start.4 = (bf16[128,2048]{1,0:T(8,128)(2,1)}, bf16[128,2048]{1,0:T(8,128)(2,1)S(1)}, u32[]{:S(2)}, u32[]{:S(2)}) collective-permute-start(bf16[128,2048]{1,0:T(8,128)(2,1)} %tokens_ref.5), channel_id=1, source_target_pairs={{0,1},{1,0},{2,3},{3,2},{4,5},{5,4},{6,7},{7,6},{8,9},{9,8},{10,11... | collective-permute-start | bytes 1572872 | tf_op jit(solution)/shard_map/ppermute | solution.py:218
  0.2 27.9 %copy-start.1 = (bf16[128,2048]{1,0:T(8,128)(2,1)S(1)}, bf16[128,2048]{1,0:T(8,128)(2,1)}, u32[]{:S(2)}) copy-start(bf16[128,2048]{1,0:T(8,128)(2,1)} %tokens_ref.5) | copy-start | bytes 1572868
  1.1 32.7 %copy-start = (bf16[2048,160]{0,1:T(8,128)(2,1)S(1)}, bf16[2048,160]{0,1:T(8,128)(2,1)}, u32[]{:S(2)}) copy-start(bf16[2048,160]{0,1:T(8,128)(2,1)} %param.4) | copy-start | bytes 1966084
  1.2 14.3 %collective-permute-start.5 = (bf16[160,256]{1,0:T(8,128)(2,1)S(1)}, bf16[160,256]{1,0:T(8,128)(2,1)S(1)}, u32[]{:S(2)}, u32[]{:S(2)}) collective-permute-start(bf16[160,256]{1,0:T(8,128)(2,1)S(1)} %get-tuple-element.21), channel_id=1, source_target_pairs={{2,0},{3,1},{0,2},{1,3},{6,4},{7,5},{4,6},{5,7},{10,8},{11,9},{8,1... | collective-permute-start | bytes 245768 | tf_op jit(solution)/shard_map/ppermute | solution.py:215
  15.5 5.3 %collective-permute-start.6 = (bf16[160,256]{1,0:T(8,128)(2,1)S(1)}, bf16[160,256]{1,0:T(8,128)(2,1)S(1)}, u32[]{:S(2)}, u32[]{:S(2)}) collective-permute-start(bf16[160,256]{1,0:T(8,128)(2,1)S(1)} %collective-permute-done.5.refs_0_), channel_id=1, source_target_pairs={{0,8},{4,12},{8,0},{12,4},{16,24},{20,28},{24,16},{28,20},{1,9},{5... | collective-permute-start | bytes 245768 | tf_op jit(solution)/shard_map/ppermute | solution.py:199
  16.7 5.8 %collective-permute-start.7 = (bf16[160,256]{1,0:T(8,128)(2,1)S(1)}, bf16[160,256]{1,0:T(8,128)(2,1)S(1)}, u32[]{:S(2)}, u32[]{:S(2)}) collective-permute-start(bf16[160,256]{1,0:T(8,128)(2,1)S(1)} %collective-permute-done.5.refs_0_), channel_id=1, source_target_pairs={{0,16},{4,20},{8,24},{12,28},{16,0},{20,4},{24,8},{28,12},{1,17},{... | collective-permute-start | bytes 245768 | tf_op jit(solution)/shard_map/ppermute | solution.py:199
  16.9 6.5 %collective-permute-start.8 = (bf16[160,256]{1,0:T(8,128)(2,1)S(1)}, bf16[160,256]{1,0:T(8,128)(2,1)S(1)}, u32[]{:S(2)}, u32[]{:S(2)}) collective-permute-start(bf16[160,256]{1,0:T(8,128)(2,1)S(1)} %collective-permute-done.5.refs_0_), channel_id=1, source_target_pairs={{0,24},{4,28},{8,16},{12,20},{16,8},{20,12},{24,0},{28,4},{1,25},{... | collective-permute-start | bytes 245768 | tf_op jit(solution)/shard_map/ppermute | solution.py:199
  18.1 6.5 %collective-permute-start.9 = (bf16[160,256]{1,0:T(8,128)(2,1)S(1)}, bf16[160,256]{1,0:T(8,128)(2,1)S(1)}, u32[]{:S(2)}, u32[]{:S(2)}) collective-permute-start(bf16[160,256]{1,0:T(8,128)(2,1)S(1)} %collective-permute-done.5.refs_0_), channel_id=1, source_target_pairs={{0,4},{4,0},{8,12},{12,8},{16,20},{20,16},{24,28},{28,24},{1,5},{5... | collective-permute-start | bytes 245768 | tf_op jit(solution)/shard_map/ppermute | solution.py:199
  20.8 4.5 %collective-permute-start.10 = (bf16[160,256]{1,0:T(8,128)(2,1)S(1)}, bf16[160,256]{1,0:T(8,128)(2,1)S(1)}, u32[]{:S(2)}, u32[]{:S(2)}) collective-permute-start(bf16[160,256]{1,0:T(8,128)(2,1)S(1)} %collective-permute-done.6.refs_1_), channel_id=1, source_target_pairs={{0,4},{4,0},{8,12},{12,8},{16,20},{20,16},{24,28},{28,24},{1,5},{5... | collective-permute-start | bytes 245768 | tf_op jit(solution)/shard_map/ppermute | solution.py:199
  22.5 4.1 %collective-permute-start.11 = (bf16[160,256]{1,0:T(8,128)(2,1)S(1)}, bf16[160,256]{1,0:T(8,128)(2,1)S(1)}, u32[]{:S(2)}, u32[]{:S(2)}) collective-permute-start(bf16[160,256]{1,0:T(8,128)(2,1)S(1)} %collective-permute-done.7.refs_2_), channel_id=1, source_target_pairs={{0,4},{4,0},{8,12},{12,8},{16,20},{20,16},{24,28},{28,24},{1,5},{5... | collective-permute-start | bytes 245768 | tf_op jit(solution)/shard_map/ppermute | solution.py:199
  23.4 3.9 %collective-permute-start.12 = (bf16[160,256]{1,0:T(8,128)(2,1)S(1)}, bf16[160,256]{1,0:T(8,128)(2,1)S(1)}, u32[]{:S(2)}, u32[]{:S(2)}) collective-permute-start(bf16[160,256]{1,0:T(8,128)(2,1)S(1)} %collective-permute-done.8.refs_3_), channel_id=1, source_target_pairs={{0,4},{4,0},{8,12},{12,8},{16,20},{20,16},{24,28},{28,24},{1,5},{5... | collective-permute-start | bytes 245768 | tf_op jit(solution)/shard_map/ppermute | solution.py:199
  24.7 9.7 %collective-permute-start = (bf16[8,2048]{1,0:T(8,128)(2,1)S(1)}, bf16[8,2048]{1,0:T(8,128)(2,1)S(1)}, u32[]{:S(2)}, u32[]{:S(2)}) collective-permute-start(bf16[8,2048]{1,0:T(8,128)(2,1)S(1)} %get-tuple-element.18), channel_id=1, source_target_pairs={{3,4},{7,8},{11,12},{15,16},{19,20},{23,24},{27,28}} | collective-permute-start | bytes 98312 | tf_op jit(solution)/shard_map/ppermute | solution.py:223
  25.3 9.2 %collective-permute-start.1 = (bf16[8,2048]{1,0:T(8,128)(2,1)S(1)}, bf16[8,2048]{1,0:T(8,128)(2,1)S(1)}, u32[]{:S(2)}, u32[]{:S(2)}) collective-permute-start(bf16[8,2048]{1,0:T(8,128)(2,1)S(1)} %get-tuple-element.18), channel_id=1, source_target_pairs={{3,5},{7,9},{11,13},{15,17},{19,21},{23,25},{27,29}} | collective-permute-start | bytes 98312 | tf_op jit(solution)/shard_map/ppermute | solution.py:223
  26.6 7.9 %collective-permute-start.2 = (bf16[8,2048]{1,0:T(8,128)(2,1)S(1)}, bf16[8,2048]{1,0:T(8,128)(2,1)S(1)}, u32[]{:S(2)}, u32[]{:S(2)}) collective-permute-start(bf16[8,2048]{1,0:T(8,128)(2,1)S(1)} %get-tuple-element.18), channel_id=1, source_target_pairs={{3,6},{7,10},{11,14},{15,18},{19,22},{23,26},{27,30}} | collective-permute-start | bytes 98312 | tf_op jit(solution)/shard_map/ppermute | solution.py:223
  27.3 7.2 %collective-permute-start.3 = (bf16[8,2048]{1,0:T(8,128)(2,1)S(1)}, bf16[8,2048]{1,0:T(8,128)(2,1)S(1)}, u32[]{:S(2)}, u32[]{:S(2)}) collective-permute-start(bf16[8,2048]{1,0:T(8,128)(2,1)S(1)} %get-tuple-element.18), channel_id=1, source_target_pairs={{3,7},{7,11},{11,15},{15,19},{19,23},{23,27},{27,31}} | collective-permute-start | bytes 98312 | tf_op jit(solution)/shard_map/ppermute | solution.py:223
  28.4 7.5 %collective-permute-start.13 = (bf16[160,128]{1,0:T(8,128)(2,1)S(1)}, bf16[160,128]{1,0:T(8,128)(2,1)S(1)}, u32[]{:S(2)}, u32[]{:S(2)}) collective-permute-start(bf16[160,128]{1,0:T(8,128)(2,1)S(1)} %shard_map.40), channel_id=1, source_target_pairs={{0,2},{1,3},{2,0},{3,1},{4,6},{5,7},{6,4},{7,5},{8,10},{9,11},{10,... | collective-permute-start | bytes 122888 | tf_op jit(solution)/shard_map/ppermute | solution.py:237
  34.4 3.8 %collective-permute-start.14 = (bf16[160,128]{1,0:T(8,128)(2,1)S(1)}, bf16[160,128]{1,0:T(8,128)(2,1)S(1)}, u32[]{:S(2)}, u32[]{:S(2)}) collective-permute-start(bf16[160,128]{1,0:T(8,128)(2,1)S(1)} %get-tuple-element.23), channel_id=1, source_target_pairs={{0,2},{1,3},{2,0},{3,1},{4,6},{5,7},{6,4},{7,5},{8,10},{9,11},{10,... | collective-permute-start | bytes 122888 | tf_op jit(solution)/shard_map/ppermute | solution.py:237
  35.1 3.2 %copy-start.2 = (f32[4,160]{1,0:T(4,128)S(1)}, f32[4,160]{1,0:T(4,128)}, u32[]{:S(2)}) copy-start(f32[4,160]{1,0:T(4,128)} %conv_ref.1) | copy-start | bytes 7684
  39.6 2.2 %collective-permute-start.15 = (f32[88,128]{1,0:T(8,128)S(1)}, f32[88,128]{1,0:T(8,128)S(1)}, u32[]{:S(2)}, u32[]{:S(2)}) collective-permute-start(f32[88,128]{1,0:T(8,128)S(1)} %get-tuple-element.30), channel_id=1, source_target_pairs={{0,4},{4,0},{8,12},{12,8},{16,20},{20,16},{24,28},{28,24},{1,5},{5... | collective-permute-start | bytes 135176 | tf_op jit(solution)/shard_map/ppermute | solution.py:199
  41.8 3.3 %collective-permute-start.16 = (f32[88,128]{1,0:T(8,128)S(1)}, f32[88,128]{1,0:T(8,128)S(1)}, u32[]{:S(2)}, u32[]{:S(2)}) collective-permute-start(f32[88,128]{1,0:T(8,128)S(1)} %add.44), channel_id=1, source_target_pairs={{0,8},{4,12},{8,0},{12,4},{16,24},{20,28},{24,16},{28,20},{1,9},{5... | collective-permute-start | bytes 135176 | tf_op jit(solution)/shard_map/ppermute | solution.py:271
  42.1 3.8 %collective-permute-start.17 = (f32[88,128]{1,0:T(8,128)S(1)}, f32[88,128]{1,0:T(8,128)S(1)}, u32[]{:S(2)}, u32[]{:S(2)}) collective-permute-start(f32[88,128]{1,0:T(8,128)S(1)} %add.44), channel_id=1, source_target_pairs={{0,16},{4,20},{8,24},{12,28},{16,0},{20,4},{24,8},{28,12},{1,17},{... | collective-permute-start | bytes 135176 | tf_op jit(solution)/shard_map/ppermute | solution.py:271
  44.2 3.8 %collective-permute-start.18 = (f32[88,128]{1,0:T(8,128)S(1)}, f32[88,128]{1,0:T(8,128)S(1)}, u32[]{:S(2)}, u32[]{:S(2)}) collective-permute-start(f32[88,128]{1,0:T(8,128)S(1)} %add.44), channel_id=1, source_target_pairs={{0,24},{4,28},{8,16},{12,20},{16,8},{20,12},{24,0},{28,4},{1,25},{... | collective-permute-start | bytes 135176 | tf_op jit(solution)/shard_map/ppermute | solution.py:271
  48.0 3.1 %collective-permute-start.19 = (f32[88,128]{1,0:T(8,128)S(1)}, f32[88,128]{1,0:T(8,128)S(1)}, u32[]{:S(2)}, u32[]{:S(2)}) collective-permute-start(f32[88,128]{1,0:T(8,128)S(1)} %get-tuple-element.31), channel_id=1, source_target_pairs={{0,4},{4,0},{8,12},{12,8},{16,20},{20,16},{24,28},{28,24},{1,5},{5... | collective-permute-start | bytes 135176 | tf_op jit(solution)/shard_map/ppermute | solution.py:199

commit v7 on v3

--- a/solution.py
+++ b/solution.py
@@ -212,11 +212,12 @@
         pieces += parts + [swap(part, 1) for part in parts]
     paired = lax.ppermute(tokens, "tp", [(z, z ^ 1) for z in range(tp)])
 
-    tail = None
-    for z in range(tp):
-        pairs = [((c - 1) * tp + tp - 1, c * tp + z) for c in range(1, ctx)]
-        part = lax.ppermute(last_rows, both, pairs)
-        tail = part if tail is None else tail + part
+    pairs = [((c - 1) * tp + tp - 1, c * tp + tp - 1) for c in range(1, ctx)]
+    ahead = lax.ppermute(last_rows, both, pairs)
+    tail = ahead
+    for z in range(tp - 1):
+        pairs = [(c * tp + tp - 1, c * tp + z) for c in range(1, ctx)]
+        tail = tail + lax.ppermute(ahead, both, pairs)
 
     shape = jax.ShapeDtypeStruct((row_width, rows), BF16)
     work = 2 * rows * depth * row_width

time: 50.1 us -> 51.4 us (1.026); the launches traced: 49.9 us -> 50.6 us
    ppermute x2, waiting for transfers between devices: 5.82 us -> 4.31 us  [per_device(): blocks += [lax.ppermute(one, 'tp', pairs), lax.ppermute(two, 'tp', pairs)]]
    ppermute x8, waiting for transfers between devices: 6.04 us -> 7.01 us  [swap(): return lax.ppermute(array, 'ctx', [(i, i ^ bit) for i in range(ctx)])]
    ppermute x3, waiting for transfers between devices: 3.64 us -> 4.54 us  [per_device(): parts.append(lax.ppermute(total, 'ctx', pairs))]
  transfers between devices with their start and end apart: 19 -> 19, of which waited for: 9 -> 10; matrix products, arithmetic and copies ran while one was open for 0% -> 0% of each run, Pallas kernels for 6% -> 6%
where the time goes in v7:
time: 51.4 us; the launch traced here: 50.6 us
  waiting for transfers between devices  25.4 us (49%)
  starting transfers between devices  19.5 us (38%)
  Pallas kernels  5.35 us (10%)
    ppermute x1, waiting for transfers between devices, per_device(): lax.ppermute(mine, 'tp', [((z + 2 * turn) % tp, z) for z in range(tp)])  9.51 us
    ppermute x8, waiting for transfers between devices, swap(): return lax.ppermute(array, 'ctx', [(i, i ^ bit) for i in range(ctx)])  7.01 us
    pallas_call x7, Pallas kernels, call(): pl.pallas_call(kernel, out_shape=outs, in_specs=[SMEM] * scalars + [space...  5.35 us
    ppermute x3, waiting for transfers between devices, per_device(): parts.append(lax.ppermute(total, 'ctx', pairs))  4.54 us
    ppermute x2, waiting for transfers between devices, per_device(): blocks += [lax.ppermute(one, 'tp', pairs), lax.ppermute(two, 'tp', pairs)]  4.31 us
    ppermute x8, starting transfers between devices, swap(): return lax.ppermute(array, 'ctx', [(i, i ^ bit) for i in range(ctx)])  3.99 us
    ppermute x3, starting transfers between devices, per_device(): parts.append(lax.ppermute(total, 'ctx', pairs))  3.62 us
    ppermute x2, starting transfers between devices, per_device(): blocks += [lax.ppermute(one, 'tp', pairs), lax.ppermute(two, 'tp', pairs)]  3.54 us
  transfers between devices with their start and end apart: 19, of which 10 were waited for; matrix products, arithmetic and copies ran while one was open for 0% of the time, Pallas kernels for 6%

profile of v7, /device:TPU:0, one launch (start us, length us, event | category | flops | bytes accessed | tf_op | source)
XLA Modules:
  0.0 50.6 jit_solution(15107086021574065353)
XLA Ops:
  0.0 3.1 %collective-permute-start.4 = (bf16[128,2048]{1,0:T(8,128)(2,1)}, bf16[128,2048]{1,0:T(8,128)(2,1)S(1)}, u32[]{:S(2)}, u32[]{:S(2)}) collective-permute-start(bf16[128,2048]{1,0:T(8,128)(2,1)} %tokens_ref.5), channel_id=1, source_target_pairs={{0,1},{1,0},{2,3},{3,2},{4,5},{5,4},{6,7},{7,6},{8,9},{9,8},{10,11... | collective-permute-start | bytes 1572872 | tf_op jit(solution)/shard_map/ppermute | solution.py:213
  3.1 1.0 %shard_map.37 = (bf16[160,256]{1,0:T(8,128)(2,1)S(1)}, bf16[8,2048]{1,0:T(8,128)(2,1)S(1)}) custom-call(s32[1]{0:T(128)} %bitcast.4.share_ref, bf16[160,2048]{1,0:T(8,128)(2,1)} %bitcast.6, bf16[128,2048]{1,0:T(8,128)(2,1)} %tokens_ref.5), custom_call_target="tpu_custom_call" | custom-call | flops 1048576 | bytes 1048576 | tf_op jit(solution)/shard_map/pallas_call | solution.py:28
  4.0 2.7 %collective-permute-start.5 = (bf16[160,256]{1,0:T(8,128)(2,1)S(1)}, bf16[160,256]{1,0:T(8,128)(2,1)S(1)}, u32[]{:S(2)}, u32[]{:S(2)}) collective-permute-start(bf16[160,256]{1,0:T(8,128)(2,1)S(1)} %get-tuple-element.20), channel_id=1, source_target_pairs={{2,0},{3,1},{0,2},{1,3},{6,4},{7,5},{4,6},{5,7},{10,8},{11,9},{8,1... | collective-permute-start | bytes 245768 | tf_op jit(solution)/shard_map/ppermute | solution.py:210
  6.7 9.5 %collective-permute-done.5.refs_0_ = bf16[160,256]{1,0:T(8,128)(2,1)S(1)} collective-permute-done((bf16[160,256]{1,0:T(8,128)(2,1)S(1)}, bf16[160,256]{1,0:T(8,128)(2,1)S(1)}, u32[]{:S(2)}, u32[]{:S(2)}) %collective-permute-start.5) | collective-permute-done | bytes 81952 | tf_op jit(solution)/shard_map/ppermute | solution.py:210
  16.2 1.5 %collective-permute-start.6 = (bf16[160,256]{1,0:T(8,128)(2,1)S(1)}, bf16[160,256]{1,0:T(8,128)(2,1)S(1)}, u32[]{:S(2)}, u32[]{:S(2)}) collective-permute-start(bf16[160,256]{1,0:T(8,128)(2,1)S(1)} %collective-permute-done.5.refs_0_), channel_id=1, source_target_pairs={{0,8},{4,12},{8,0},{12,4},{16,24},{20,28},{24,16},{28,20},{1,9},{5... | collective-permute-start | bytes 245768 | tf_op jit(solution)/shard_map/ppermute | solution.py:194
  17.7 1.5 %collective-permute-start.7 = (bf16[160,256]{1,0:T(8,128)(2,1)S(1)}, bf16[160,256]{1,0:T(8,128)(2,1)S(1)}, u32[]{:S(2)}, u32[]{:S(2)}) collective-permute-start(bf16[160,256]{1,0:T(8,128)(2,1)S(1)} %collective-permute-done.5.refs_0_), channel_id=1, source_target_pairs={{0,16},{4,20},{8,24},{12,28},{16,0},{20,4},{24,8},{28,12},{1,17},{... | collective-permute-start | bytes 245768 | tf_op jit(solution)/shard_map/ppermute | solution.py:194
  19.2 0.7 %collective-permute-start = (bf16[8,2048]{1,0:T(8,128)(2,1)S(1)}, bf16[8,2048]{1,0:T(8,128)(2,1)S(1)}, u32[]{:S(2)}, u32[]{:S(2)}) collective-permute-start(bf16[8,2048]{1,0:T(8,128)(2,1)S(1)} %get-tuple-element.17), channel_id=1, source_target_pairs={{3,7},{7,11},{11,15},{15,19},{19,23},{23,27},{27,31}} | collective-permute-start | bytes 98312 | tf_op jit(solution)/shard_map/ppermute | solution.py:216
  20.9 2.1 %collective-permute-done.7.refs_2_ = bf16[160,256]{1,0:T(8,128)(2,1)S(1)} collective-permute-done((bf16[160,256]{1,0:T(8,128)(2,1)S(1)}, bf16[160,256]{1,0:T(8,128)(2,1)S(1)}, u32[]{:S(2)}, u32[]{:S(2)}) %collective-permute-start.7) | collective-permute-done | bytes 81952 | tf_op jit(solution)/shard_map/ppermute | solution.py:194
  23.0 2.3 %collective-permute-done.8.refs_3_ = bf16[160,256]{1,0:T(8,128)(2,1)S(1)} collective-permute-done((bf16[160,256]{1,0:T(8,128)(2,1)S(1)}, bf16[160,256]{1,0:T(8,128)(2,1)S(1)}, u32[]{:S(2)}, u32[]{:S(2)}) %collective-permute-start.8) | collective-permute-done | bytes 81952 | tf_op jit(solution)/shard_map/ppermute | solution.py:194
  25.3 0.7 %collective-permute-start.3 = (bf16[8,2048]{1,0:T(8,128)(2,1)S(1)}, bf16[8,2048]{1,0:T(8,128)(2,1)S(1)}, u32[]{:S(2)}, u32[]{:S(2)}) collective-permute-start(bf16[8,2048]{1,0:T(8,128)(2,1)S(1)} %collective-permute-done), channel_id=1, source_target_pairs={{7,6},{11,10},{15,14},{19,18},{23,22},{27,26},{31,30}} | collective-permute-start | bytes 98312 | tf_op jit(solution)/shard_map/ppermute | solution.py:220
  25.9 0.7 %collective-permute-start.2 = (bf16[8,2048]{1,0:T(8,128)(2,1)S(1)}, bf16[8,2048]{1,0:T(8,128)(2,1)S(1)}, u32[]{:S(2)}, u32[]{:S(2)}) collective-permute-start(bf16[8,2048]{1,0:T(8,128)(2,1)S(1)} %collective-permute-done), channel_id=1, source_target_pairs={{7,5},{11,9},{15,13},{19,17},{23,21},{27,25},{31,29}} | collective-permute-start | bytes 98312 | tf_op jit(solution)/shard_map/ppermute | solution.py:220
  26.6 0.7 %collective-permute-start.1 = (bf16[8,2048]{1,0:T(8,128)(2,1)S(1)}, bf16[8,2048]{1,0:T(8,128)(2,1)S(1)}, u32[]{:S(2)}, u32[]{:S(2)}) collective-permute-start(bf16[8,2048]{1,0:T(8,128)(2,1)S(1)} %collective-permute-done), channel_id=1, source_target_pairs={{7,4},{11,8},{15,12},{19,16},{23,20},{27,24},{31,28}} | collective-permute-start | bytes 98312 | tf_op jit(solution)/shard_map/ppermute | solution.py:220
  27.5 1.2 %collective-permute-done.12.refs_7_ = bf16[160,256]{1,0:T(8,128)(2,1)S(1)} collective-permute-done((bf16[160,256]{1,0:T(8,128)(2,1)S(1)}, bf16[160,256]{1,0:T(8,128)(2,1)S(1)}, u32[]{:S(2)}, u32[]{:S(2)}) %collective-permute-start.12) | collective-permute-done | bytes 81952 | tf_op jit(solution)/shard_map/ppermute | solution.py:194
  29.0 3.4 %collective-permute-start.13 = (bf16[160,128]{1,0:T(8,128)(2,1)S(1)}, bf16[160,128]{1,0:T(8,128)(2,1)S(1)}, u32[]{:S(2)}, u32[]{:S(2)}) collective-permute-start(bf16[160,128]{1,0:T(8,128)(2,1)S(1)} %shard_map.40), channel_id=1, source_target_pairs={{0,2},{1,3},{2,0},{3,1},{4,6},{5,7},{6,4},{7,5},{8,10},{9,11},{10,... | collective-permute-start | bytes 122888 | tf_op jit(solution)/shard_map/ppermute | solution.py:233
  33.6 1.1 %collective-permute-done.13.refs_2_ = bf16[160,128]{1,0:T(8,128)(2,1)S(1)} collective-permute-done((bf16[160,128]{1,0:T(8,128)(2,1)S(1)}, bf16[160,128]{1,0:T(8,128)(2,1)S(1)}, u32[]{:S(2)}, u32[]{:S(2)}) %collective-permute-start.13) | collective-permute-done | bytes 40992 | tf_op jit(solution)/shard_map/ppermute | solution.py:233
  34.7 3.3 %collective-permute-done.14.refs_3_ = bf16[160,128]{1,0:T(8,128)(2,1)S(1)} collective-permute-done((bf16[160,128]{1,0:T(8,128)(2,1)S(1)}, bf16[160,128]{1,0:T(8,128)(2,1)S(1)}, u32[]{:S(2)}, u32[]{:S(2)}) %collective-permute-start.14) | collective-permute-done | bytes 40992 | tf_op jit(solution)/shard_map/ppermute | solution.py:233
  37.9 1.3 %shard_map.41 = (bf16[512,160]{1,0:T(8,128)(2,1)S(1)}, bf16[160,512]{1,0:T(8,128)(2,1)S(1)}, bf16[128,512]{1,0:T(8,128)(2,1)S(1)}, f32[168,128]{1,0:T(8,128)S(1)}) custom-call(s32[4]{0:T(128)S(1)} %pad_add_fusion.place_ref, f32[4,160]{1,0:T(4,128)S(1)} %copy-done.2, bf16[160,128]{1,0:T(8,128)(2,1)S(1)} %get-tuple-element.18.halo_ref, ...), custom_call_target="tpu_custom_call" | custom-call | flops 1048576 | bytes 1048576 | tf_op jit(solution)/shard_map/pallas_call | solution.py:28
  39.4 1.3 %collective-permute-done.15 = f32[168,128]{1,0:T(8,128)S(1)} collective-permute-done((f32[168,128]{1,0:T(8,128)S(1)}, f32[168,128]{1,0:T(8,128)S(1)}, u32[]{:S(2)}, u32[]{:S(2)}) %collective-permute-start.15) | collective-permute-done | bytes 86048 | tf_op jit(solution)/shard_map/ppermute | solution.py:194
  40.7 1.8 %collective-permute-start.16 = (f32[168,128]{1,0:T(8,128)S(1)}, f32[168,128]{1,0:T(8,128)S(1)}, u32[]{:S(2)}, u32[]{:S(2)}) collective-permute-start(f32[168,128]{1,0:T(8,128)S(1)} %get-tuple-element.29), channel_id=1, source_target_pairs={{0,8},{4,12},{8,0},{12,4},{16,24},{20,28},{24,16},{28,20},{1,9},{5... | collective-permute-start | bytes 258056 | tf_op jit(solution)/shard_map/ppermute | solution.py:265
  42.4 0.6 %shard_map.42 = (f32[512,128]{1,0:T(8,128)S(1)}, f32[512,128]{1,0:T(8,128)S(1)}) custom-call(bf16[512,160]{1,0:T(8,128)(2,1)S(1)} %get-tuple-element.23.query_ref, bf16[160,512]{1,0:T(8,128)(2,1)S(1)} %get-tuple-element.24.key_ref, bf16[128,512]{1,0:T(8,128)(2,1)S(1)} %get-tuple-element.25.value_ref), custom_call_target="tpu_custom_call" | custom-call | flops 150994944 | bytes 1048576 | tf_op jit(solution)/shard_map/pallas_call | solution.py:28
  43.1 0.6 %collective-permute-start.17 = (f32[168,128]{1,0:T(8,128)S(1)}, f32[168,128]{1,0:T(8,128)S(1)}, u32[]{:S(2)}, u32[]{:S(2)}) collective-permute-start(f32[168,128]{1,0:T(8,128)S(1)} %get-tuple-element.29), channel_id=1, source_target_pairs={{0,16},{4,20},{8,24},{12,28},{16,0},{20,4},{24,8},{28,12},{1,17},{... | collective-permute-start | bytes 258056 | tf_op jit(solution)/shard_map/ppermute | solution.py:265
  43.7 1.3 %collective-permute-start.18 = (f32[168,128]{1,0:T(8,128)S(1)}, f32[168,128]{1,0:T(8,128)S(1)}, u32[]{:S(2)}, u32[]{:S(2)}) collective-permute-start(f32[168,128]{1,0:T(8,128)S(1)} %get-tuple-element.29), channel_id=1, source_target_pairs={{0,24},{4,28},{8,16},{12,20},{16,8},{20,12},{24,0},{28,4},{1,25},{... | collective-permute-start | bytes 258056 | tf_op jit(solution)/shard_map/ppermute | solution.py:265
  45.3 4.1 %collective-permute-done.17 = f32[168,128]{1,0:T(8,128)S(1)} collective-permute-done((f32[168,128]{1,0:T(8,128)S(1)}, f32[168,128]{1,0:T(8,128)S(1)}, u32[]{:S(2)}, u32[]{:S(2)}) %collective-permute-start.17) | collective-permute-done | bytes 86048 | tf_op jit(solution)/shard_map/ppermute | solution.py:265
  49.5 1.0 %shard_map.43 = bf16[512,128]{1,0:T(8,128)(2,1)} custom-call(bf16[512,160]{1,0:T(8,128)(2,1)S(1)} %get-tuple-element.23.query_ref, f32[512,128]{1,0:T(8,128)S(1)} %get-tuple-element.26.numerator_ref, f32[512,128]{1,0:T(8,128)S(1)} %get-tuple-element.27.denominator_ref, f32[168,128]{1,0:T(8,128)S(1)} %get-tuple-element.30.refs_0_, ...), custom_call_target="tpu_custom_call" | custom-call | flops 62914560 | bytes 1048576 | tf_op jit(solution)/shard_map/pallas_call | solution.py:28
  (33 shorter events, 3.2 us)
Async XLA Ops:
  0.0 32.5 %collective-permute-start.4 = (bf16[128,2048]{1,0:T(8,128)(2,1)}, bf16[128,2048]{1,0:T(8,128)(2,1)S(1)}, u32[]{:S(2)}, u32[]{:S(2)}) collective-permute-start(bf16[128,2048]{1,0:T(8,128)(2,1)} %tokens_ref.5), channel_id=1, source_target_pairs={{0,1},{1,0},{2,3},{3,2},{4,5},{5,4},{6,7},{7,6},{8,9},{9,8},{10,11... | collective-permute-start | bytes 1572872 | tf_op jit(solution)/shard_map/ppermute | solution.py:213
  3.1 25.6 %copy-start.1 = (bf16[128,2048]{1,0:T(8,128)(2,1)S(1)}, bf16[128,2048]{1,0:T(8,128)(2,1)}, u32[]{:S(2)}) copy-start(bf16[128,2048]{1,0:T(8,128)(2,1)} %tokens_ref.5) | copy-start | bytes 1572868
  4.0 28.4 %copy-start = (bf16[2048,160]{0,1:T(8,128)(2,1)S(1)}, bf16[2048,160]{0,1:T(8,128)(2,1)}, u32[]{:S(2)}) copy-start(bf16[2048,160]{0,1:T(8,128)(2,1)} %param.4) | copy-start | bytes 1966084
  4.0 12.2 %collective-permute-start.5 = (bf16[160,256]{1,0:T(8,128)(2,1)S(1)}, bf16[160,256]{1,0:T(8,128)(2,1)S(1)}, u32[]{:S(2)}, u32[]{:S(2)}) collective-permute-start(bf16[160,256]{1,0:T(8,128)(2,1)S(1)} %get-tuple-element.20), channel_id=1, source_target_pairs={{2,0},{3,1},{0,2},{1,3},{6,4},{7,5},{4,6},{5,7},{10,8},{11,9},{8,1... | collective-permute-start | bytes 245768 | tf_op jit(solution)/shard_map/ppermute | solution.py:210
  16.2 4.4 %collective-permute-start.6 = (bf16[160,256]{1,0:T(8,128)(2,1)S(1)}, bf16[160,256]{1,0:T(8,128)(2,1)S(1)}, u32[]{:S(2)}, u32[]{:S(2)}) collective-permute-start(bf16[160,256]{1,0:T(8,128)(2,1)S(1)} %collective-permute-done.5.refs_0_), channel_id=1, source_target_pairs={{0,8},{4,12},{8,0},{12,4},{16,24},{20,28},{24,16},{28,20},{1,9},{5... | collective-permute-start | bytes 245768 | tf_op jit(solution)/shard_map/ppermute | solution.py:194
  17.7 5.3 %collective-permute-start.7 = (bf16[160,256]{1,0:T(8,128)(2,1)S(1)}, bf16[160,256]{1,0:T(8,128)(2,1)S(1)}, u32[]{:S(2)}, u32[]{:S(2)}) collective-permute-start(bf16[160,256]{1,0:T(8,128)(2,1)S(1)} %collective-permute-done.5.refs_0_), channel_id=1, source_target_pairs={{0,16},{4,20},{8,24},{12,28},{16,0},{20,4},{24,8},{28,12},{1,17},{... | collective-permute-start | bytes 245768 | tf_op jit(solution)/shard_map/ppermute | solution.py:194
  19.2 1.2 %collective-permute-start = (bf16[8,2048]{1,0:T(8,128)(2,1)S(1)}, bf16[8,2048]{1,0:T(8,128)(2,1)S(1)}, u32[]{:S(2)}, u32[]{:S(2)}) collective-permute-start(bf16[8,2048]{1,0:T(8,128)(2,1)S(1)} %get-tuple-element.17), channel_id=1, source_target_pairs={{3,7},{7,11},{11,15},{15,19},{19,23},{23,27},{27,31}} | collective-permute-start | bytes 98312 | tf_op jit(solution)/shard_map/ppermute | solution.py:216
  19.9 5.4 %collective-permute-start.8 = (bf16[160,256]{1,0:T(8,128)(2,1)S(1)}, bf16[160,256]{1,0:T(8,128)(2,1)S(1)}, u32[]{:S(2)}, u32[]{:S(2)}) collective-permute-start(bf16[160,256]{1,0:T(8,128)(2,1)S(1)} %collective-permute-done.5.refs_0_), channel_id=1, source_target_pairs={{0,24},{4,28},{8,16},{12,20},{16,8},{20,12},{24,0},{28,4},{1,25},{... | collective-permute-start | bytes 245768 | tf_op jit(solution)/shard_map/ppermute | solution.py:194
  20.4 5.5 %collective-permute-start.9 = (bf16[160,256]{1,0:T(8,128)(2,1)S(1)}, bf16[160,256]{1,0:T(8,128)(2,1)S(1)}, u32[]{:S(2)}, u32[]{:S(2)}) collective-permute-start(bf16[160,256]{1,0:T(8,128)(2,1)S(1)} %collective-permute-done.5.refs_0_), channel_id=1, source_target_pairs={{0,4},{4,0},{8,12},{12,8},{16,20},{20,16},{24,28},{28,24},{1,5},{5... | collective-permute-start | bytes 245768 | tf_op jit(solution)/shard_map/ppermute | solution.py:194
  20.6 6.0 %collective-permute-start.10 = (bf16[160,256]{1,0:T(8,128)(2,1)S(1)}, bf16[160,256]{1,0:T(8,128)(2,1)S(1)}, u32[]{:S(2)}, u32[]{:S(2)}) collective-permute-start(bf16[160,256]{1,0:T(8,128)(2,1)S(1)} %collective-permute-done.6.refs_1_), channel_id=1, source_target_pairs={{0,4},{4,0},{8,12},{12,8},{16,20},{20,16},{24,28},{28,24},{1,5},{5... | collective-permute-start | bytes 245768 | tf_op jit(solution)/shard_map/ppermute | solution.py:194
  23.0 4.3 %collective-permute-start.11 = (bf16[160,256]{1,0:T(8,128)(2,1)S(1)}, bf16[160,256]{1,0:T(8,128)(2,1)S(1)}, u32[]{:S(2)}, u32[]{:S(2)}) collective-permute-start(bf16[160,256]{1,0:T(8,128)(2,1)S(1)} %collective-permute-done.7.refs_2_), channel_id=1, source_target_pairs={{0,4},{4,0},{8,12},{12,8},{16,20},{20,16},{24,28},{28,24},{1,5},{5... | collective-permute-start | bytes 245768 | tf_op jit(solution)/shard_map/ppermute | solution.py:194
  25.3 7.8 %collective-permute-start.3 = (bf16[8,2048]{1,0:T(8,128)(2,1)S(1)}, bf16[8,2048]{1,0:T(8,128)(2,1)S(1)}, u32[]{:S(2)}, u32[]{:S(2)}) collective-permute-start(bf16[8,2048]{1,0:T(8,128)(2,1)S(1)} %collective-permute-done), channel_id=1, source_target_pairs={{7,6},{11,10},{15,14},{19,18},{23,22},{27,26},{31,30}} | collective-permute-start | bytes 98312 | tf_op jit(solution)/shard_map/ppermute | solution.py:220
  25.9 7.1 %collective-permute-start.2 = (bf16[8,2048]{1,0:T(8,128)(2,1)S(1)}, bf16[8,2048]{1,0:T(8,128)(2,1)S(1)}, u32[]{:S(2)}, u32[]{:S(2)}) collective-permute-start(bf16[8,2048]{1,0:T(8,128)(2,1)S(1)} %collective-permute-done), channel_id=1, source_target_pairs={{7,5},{11,9},{15,13},{19,17},{23,21},{27,25},{31,29}} | collective-permute-start | bytes 98312 | tf_op jit(solution)/shard_map/ppermute | solution.py:220
  26.6 6.5 %collective-permute-start.1 = (bf16[8,2048]{1,0:T(8,128)(2,1)S(1)}, bf16[8,2048]{1,0:T(8,128)(2,1)S(1)}, u32[]{:S(2)}, u32[]{:S(2)}) collective-permute-start(bf16[8,2048]{1,0:T(8,128)(2,1)S(1)} %collective-permute-done), channel_id=1, source_target_pairs={{7,4},{11,8},{15,12},{19,16},{23,20},{27,24},{31,28}} | collective-permute-start | bytes 98312 | tf_op jit(solution)/shard_map/ppermute | solution.py:220
  27.3 1.3 %collective-permute-start.12 = (bf16[160,256]{1,0:T(8,128)(2,1)S(1)}, bf16[160,256]{1,0:T(8,128)(2,1)S(1)}, u32[]{:S(2)}, u32[]{:S(2)}) collective-permute-start(bf16[160,256]{1,0:T(8,128)(2,1)S(1)} %collective-permute-done.8.refs_3_), channel_id=1, source_target_pairs={{0,4},{4,0},{8,12},{12,8},{16,20},{20,16},{24,28},{28,24},{1,5},{5... | collective-permute-start | bytes 245768 | tf_op jit(solution)/shard_map/ppermute | solution.py:194
  29.0 5.7 %collective-permute-start.13 = (bf16[160,128]{1,0:T(8,128)(2,1)S(1)}, bf16[160,128]{1,0:T(8,128)(2,1)S(1)}, u32[]{:S(2)}, u32[]{:S(2)}) collective-permute-start(bf16[160,128]{1,0:T(8,128)(2,1)S(1)} %shard_map.40), channel_id=1, source_target_pairs={{0,2},{1,3},{2,0},{3,1},{4,6},{5,7},{6,4},{7,5},{8,10},{9,11},{10,... | collective-permute-start | bytes 122888 | tf_op jit(solution)/shard_map/ppermute | solution.py:233
  33.0 5.0 %collective-permute-start.14 = (bf16[160,128]{1,0:T(8,128)(2,1)S(1)}, bf16[160,128]{1,0:T(8,128)(2,1)S(1)}, u32[]{:S(2)}, u32[]{:S(2)}) collective-permute-start(bf16[160,128]{1,0:T(8,128)(2,1)S(1)} %get-tuple-element.22), channel_id=1, source_target_pairs={{0,2},{1,3},{2,0},{3,1},{4,6},{5,7},{6,4},{7,5},{8,10},{9,11},{10,... | collective-permute-start | bytes 122888 | tf_op jit(solution)/shard_map/ppermute | solution.py:233
  33.6 4.3 %copy-start.2 = (f32[4,160]{1,0:T(4,128)S(1)}, f32[4,160]{1,0:T(4,128)}, u32[]{:S(2)}) copy-start(f32[4,160]{1,0:T(4,128)} %conv_ref.1) | copy-start | bytes 7684
  39.3 1.3 %collective-permute-start.15 = (f32[168,128]{1,0:T(8,128)S(1)}, f32[168,128]{1,0:T(8,128)S(1)}, u32[]{:S(2)}, u32[]{:S(2)}) collective-permute-start(f32[168,128]{1,0:T(8,128)S(1)} %get-tuple-element.28), channel_id=1, source_target_pairs={{0,4},{4,0},{8,12},{12,8},{16,20},{20,16},{24,28},{28,24},{1,5},{5... | collective-permute-start | bytes 258056 | tf_op jit(solution)/shard_map/ppermute | solution.py:194
  40.7 4.7 %collective-permute-start.16 = (f32[168,128]{1,0:T(8,128)S(1)}, f32[168,128]{1,0:T(8,128)S(1)}, u32[]{:S(2)}, u32[]{:S(2)}) collective-permute-start(f32[168,128]{1,0:T(8,128)S(1)} %get-tuple-element.29), channel_id=1, source_target_pairs={{0,8},{4,12},{8,0},{12,4},{16,24},{20,28},{24,16},{28,20},{1,9},{5... | collective-permute-start | bytes 258056 | tf_op jit(solution)/shard_map/ppermute | solution.py:265
  43.1 6.4 %collective-permute-start.17 = (f32[168,128]{1,0:T(8,128)S(1)}, f32[168,128]{1,0:T(8,128)S(1)}, u32[]{:S(2)}, u32[]{:S(2)}) collective-permute-start(f32[168,128]{1,0:T(8,128)S(1)} %get-tuple-element.29), channel_id=1, source_target_pairs={{0,16},{4,20},{8,24},{12,28},{16,0},{20,4},{24,8},{28,12},{1,17},{... | collective-permute-start | bytes 258056 | tf_op jit(solution)/shard_map/ppermute | solution.py:265
  43.7 5.8 %collective-permute-start.18 = (f32[168,128]{1,0:T(8,128)S(1)}, f32[168,128]{1,0:T(8,128)S(1)}, u32[]{:S(2)}, u32[]{:S(2)}) collective-permute-start(f32[168,128]{1,0:T(8,128)S(1)} %get-tuple-element.29), channel_id=1, source_target_pairs={{0,24},{4,28},{8,16},{12,20},{16,8},{20,12},{24,0},{28,4},{1,25},{... | collective-permute-start | bytes 258056 | tf_op jit(solution)/shard_map/ppermute | solution.py:265

commit v8 on v3

--- a/solution.py
+++ b/solution.py
@@ -128,8 +128,7 @@
         convolved += taps[:, offset : offset + 1] * moved[:, width:]
     value = convolved[2 * FEAT :].astype(BF16)
     value_ref[...] = value
-    query = features(convolved[:FEAT], False)
-    query_ref[...] = query.T
+    query_ref[...] = convolved[:FEAT]
     key = features(convolved[FEAT : 2 * FEAT], True)
     key_ref[...] = key
     state_ref[:NUM_FEAT, :] = dot_last(key, value)
@@ -141,7 +140,8 @@
     state_ref[NUM_FEAT:, :] = jnp.where(row == 0, total[:, :lanes], jnp.where(row == 1, more, 0.0))
 
 
-def inner_kernel(query_ref, key_ref, value_ref, numerator_ref, denominator_ref):
+def inner_kernel(raw_ref, key_ref, value_ref, query_ref, numerator_ref, denominator_ref):
+    query_ref[...] = features(raw_ref[...], False).T
     local_rows = query_ref.shape[0]
     width = value_ref.shape[0]
     step = LANES
@@ -232,10 +232,10 @@
         blocks += [lax.ppermute(one, "tp", pairs), lax.ppermute(two, "tp", pairs)]
         places += [source, source ^ 1]
     place = jnp.stack(places).astype(jnp.int32)
-    query, key, value, state = call(
+    raw, key, value, state = call(
         feature_kernel,
         [
-            jax.ShapeDtypeStruct((local_rows, NUM_FEAT), BF16),
+            jax.ShapeDtypeStruct((FEAT, local_rows), F32),
             jax.ShapeDtypeStruct((NUM_FEAT, local_rows), BF16),
             jax.ShapeDtypeStruct((val_width, local_rows), BF16),
             jax.ShapeDtypeStruct((STATE_ROWS, val_width), F32),
@@ -244,10 +244,11 @@
         1,
         [pltpu.VMEM((row_width, rows + local_rows), F32)],
     )
-    numerator, denominator = call(
+    query, numerator, denominator = call(
         inner_kernel,
-        [jax.ShapeDtypeStruct((local_rows, val_width), F32)] * 2,
-        [query, key, value],
+        [jax.ShapeDtypeStruct((local_rows, NUM_FEAT), BF16)]
+        + [jax.ShapeDtypeStruct((local_rows, val_width), F32)] * 2,
+        [raw, key, value],
         flops=2 * local_rows * local_rows * (NUM_FEAT + val_width),
     )
     received = swap(state, 1)

time: 50.1 us -> 50.1 us (level)
  no operation moved by 1% of the time
where the time goes in v8:
time: 50.1 us; the launch traced here: 49.9 us
  waiting for transfers between devices  25 us (50%)
  starting transfers between devices  19.2 us (38%)
  Pallas kernels  5.35 us (11%)
    ppermute x1, waiting for transfers between devices, per_device(): lax.ppermute(mine, 'tp', [((z + 2 * turn) % tp, z) for z in range(tp)])  9.51 us
    ppermute x8, waiting for transfers between devices, swap(): return lax.ppermute(array, 'ctx', [(i, i ^ bit) for i in range(ctx)])  6.04 us
    ppermute x2, waiting for transfers between devices, per_device(): blocks += [lax.ppermute(one, 'tp', pairs), lax.ppermute(two, 'tp', pairs)]  5.82 us
    pallas_call x7, Pallas kernels, call(): pl.pallas_call(kernel, out_shape=outs, in_specs=[SMEM] * scalars + [space...  5.35 us
    ppermute x8, starting transfers between devices, swap(): return lax.ppermute(array, 'ctx', [(i, i ^ bit) for i in range(ctx)])  3.67 us
    ppermute x3, waiting for transfers between devices, per_device(): parts.append(lax.ppermute(total, 'ctx', pairs))  3.64 us
    ppermute x3, starting transfers between devices, per_device(): parts.append(lax.ppermute(total, 'ctx', pairs))  3.62 us
    ppermute x2, starting transfers between devices, per_device(): blocks += [lax.ppermute(one, 'tp', pairs), lax.ppermute(two, 'tp', pairs)]  3.54 us
  transfers between devices with their start and end apart: 19, of which 9 were waited for; matrix products, arithmetic and copies ran while one was open for 0% of the time, Pallas kernels for 6%

profile of v8, /device:TPU:0, one launch (start us, length us, event | category | flops | bytes accessed | tf_op | source)
XLA Modules:
  0.0 49.9 jit_solution(14710759639228135745)
XLA Ops:
  0.0 3.1 %collective-permute-start.4 = (bf16[128,2048]{1,0:T(8,128)(2,1)}, bf16[128,2048]{1,0:T(8,128)(2,1)S(1)}, u32[]{:S(2)}, u32[]{:S(2)}) collective-permute-start(bf16[128,2048]{1,0:T(8,128)(2,1)} %tokens_ref.5), channel_id=1, source_target_pairs={{0,1},{1,0},{2,3},{3,2},{4,5},{5,4},{6,7},{7,6},{8,9},{9,8},{10,11... | collective-permute-start | bytes 1572872 | tf_op jit(solution)/shard_map/ppermute | solution.py:213
  3.1 1.0 %shard_map.37 = (bf16[160,256]{1,0:T(8,128)(2,1)S(1)}, bf16[8,2048]{1,0:T(8,128)(2,1)S(1)}) custom-call(s32[1]{0:T(128)} %bitcast.4.share_ref, bf16[160,2048]{1,0:T(8,128)(2,1)} %bitcast.6, bf16[128,2048]{1,0:T(8,128)(2,1)} %tokens_ref.5), custom_call_target="tpu_custom_call" | custom-call | flops 1048576 | bytes 1048576 | tf_op jit(solution)/shard_map/pallas_call | solution.py:28
  4.0 2.7 %collective-permute-start.5 = (bf16[160,256]{1,0:T(8,128)(2,1)S(1)}, bf16[160,256]{1,0:T(8,128)(2,1)S(1)}, u32[]{:S(2)}, u32[]{:S(2)}) collective-permute-start(bf16[160,256]{1,0:T(8,128)(2,1)S(1)} %get-tuple-element.21), channel_id=1, source_target_pairs={{2,0},{3,1},{0,2},{1,3},{6,4},{7,5},{4,6},{5,7},{10,8},{11,9},{8,1... | collective-permute-start | bytes 245768 | tf_op jit(solution)/shard_map/ppermute | solution.py:210
  6.7 9.5 %collective-permute-done.5.refs_0_ = bf16[160,256]{1,0:T(8,128)(2,1)S(1)} collective-permute-done((bf16[160,256]{1,0:T(8,128)(2,1)S(1)}, bf16[160,256]{1,0:T(8,128)(2,1)S(1)}, u32[]{:S(2)}, u32[]{:S(2)}) %collective-permute-start.5) | collective-permute-done | bytes 81952 | tf_op jit(solution)/shard_map/ppermute | solution.py:210
  16.2 1.5 %collective-permute-start.6 = (bf16[160,256]{1,0:T(8,128)(2,1)S(1)}, bf16[160,256]{1,0:T(8,128)(2,1)S(1)}, u32[]{:S(2)}, u32[]{:S(2)}) collective-permute-start(bf16[160,256]{1,0:T(8,128)(2,1)S(1)} %collective-permute-done.5.refs_0_), channel_id=1, source_target_pairs={{0,8},{4,12},{8,0},{12,4},{16,24},{20,28},{24,16},{28,20},{1,9},{5... | collective-permute-start | bytes 245768 | tf_op jit(solution)/shard_map/ppermute | solution.py:194
  17.7 1.5 %collective-permute-start.7 = (bf16[160,256]{1,0:T(8,128)(2,1)S(1)}, bf16[160,256]{1,0:T(8,128)(2,1)S(1)}, u32[]{:S(2)}, u32[]{:S(2)}) collective-permute-start(bf16[160,256]{1,0:T(8,128)(2,1)S(1)} %collective-permute-done.5.refs_0_), channel_id=1, source_target_pairs={{0,16},{4,20},{8,24},{12,28},{16,0},{20,4},{24,8},{28,12},{1,17},{... | collective-permute-start | bytes 245768 | tf_op jit(solution)/shard_map/ppermute | solution.py:194
  19.7 1.4 %collective-permute-done.6.refs_1_ = bf16[160,256]{1,0:T(8,128)(2,1)S(1)} collective-permute-done((bf16[160,256]{1,0:T(8,128)(2,1)S(1)}, bf16[160,256]{1,0:T(8,128)(2,1)S(1)}, u32[]{:S(2)}, u32[]{:S(2)}) %collective-permute-start.6) | collective-permute-done | bytes 81952 | tf_op jit(solution)/shard_map/ppermute | solution.py:194
  21.1 1.8 %collective-permute-done.7.refs_2_ = bf16[160,256]{1,0:T(8,128)(2,1)S(1)} collective-permute-done((bf16[160,256]{1,0:T(8,128)(2,1)S(1)}, bf16[160,256]{1,0:T(8,128)(2,1)S(1)}, u32[]{:S(2)}, u32[]{:S(2)}) %collective-permute-start.7) | collective-permute-done | bytes 81952 | tf_op jit(solution)/shard_map/ppermute | solution.py:194
  22.9 1.6 %collective-permute-done.8.refs_3_ = bf16[160,256]{1,0:T(8,128)(2,1)S(1)} collective-permute-done((bf16[160,256]{1,0:T(8,128)(2,1)S(1)}, bf16[160,256]{1,0:T(8,128)(2,1)S(1)}, u32[]{:S(2)}, u32[]{:S(2)}) %collective-permute-start.8) | collective-permute-done | bytes 81952 | tf_op jit(solution)/shard_map/ppermute | solution.py:194
  24.6 0.7 %collective-permute-start.3 = (bf16[8,2048]{1,0:T(8,128)(2,1)S(1)}, bf16[8,2048]{1,0:T(8,128)(2,1)S(1)}, u32[]{:S(2)}, u32[]{:S(2)}) collective-permute-start(bf16[8,2048]{1,0:T(8,128)(2,1)S(1)} %get-tuple-element.18), channel_id=1, source_target_pairs={{3,7},{7,11},{11,15},{15,19},{19,23},{23,27},{27,31}} | collective-permute-start | bytes 98312 | tf_op jit(solution)/shard_map/ppermute | solution.py:218
  25.2 0.7 %collective-permute-start.2 = (bf16[8,2048]{1,0:T(8,128)(2,1)S(1)}, bf16[8,2048]{1,0:T(8,128)(2,1)S(1)}, u32[]{:S(2)}, u32[]{:S(2)}) collective-permute-start(bf16[8,2048]{1,0:T(8,128)(2,1)S(1)} %get-tuple-element.18), channel_id=1, source_target_pairs={{3,6},{7,10},{11,14},{15,18},{19,22},{23,26},{27,30}} | collective-permute-start | bytes 98312 | tf_op jit(solution)/shard_map/ppermute | solution.py:218
  25.9 0.7 %collective-permute-start = (bf16[8,2048]{1,0:T(8,128)(2,1)S(1)}, bf16[8,2048]{1,0:T(8,128)(2,1)S(1)}, u32[]{:S(2)}, u32[]{:S(2)}) collective-permute-start(bf16[8,2048]{1,0:T(8,128)(2,1)S(1)} %get-tuple-element.18), channel_id=1, source_target_pairs={{3,4},{7,8},{11,12},{15,16},{19,20},{23,24},{27,28}} | collective-permute-start | bytes 98312 | tf_op jit(solution)/shard_map/ppermute | solution.py:218
  26.6 0.7 %collective-permute-start.1 = (bf16[8,2048]{1,0:T(8,128)(2,1)S(1)}, bf16[8,2048]{1,0:T(8,128)(2,1)S(1)}, u32[]{:S(2)}, u32[]{:S(2)}) collective-permute-start(bf16[8,2048]{1,0:T(8,128)(2,1)S(1)} %get-tuple-element.18), channel_id=1, source_target_pairs={{3,5},{7,9},{11,13},{15,17},{19,21},{23,25},{27,29}} | collective-permute-start | bytes 98312 | tf_op jit(solution)/shard_map/ppermute | solution.py:218
  27.7 3.4 %collective-permute-start.13 = (bf16[160,128]{1,0:T(8,128)(2,1)S(1)}, bf16[160,128]{1,0:T(8,128)(2,1)S(1)}, u32[]{:S(2)}, u32[]{:S(2)}) collective-permute-start(bf16[160,128]{1,0:T(8,128)(2,1)S(1)} %shard_map.40), channel_id=1, source_target_pairs={{0,2},{1,3},{2,0},{3,1},{4,6},{5,7},{6,4},{7,5},{8,10},{9,11},{10,... | collective-permute-start | bytes 122888 | tf_op jit(solution)/shard_map/ppermute | solution.py:232
  31.2 0.5 %shard_map.39 = (bf16[160,128]{1,0:T(8,128)(2,1)S(1)}, bf16[160,128]{1,0:T(8,128)(2,1)S(1)}) custom-call(s32[1]{0:T(128)} %bitcast.4.share_ref, bf16[128,2048]{1,0:T(8,128)(2,1)S(1)} %collective-permute-done.4.tokens_ref, bf16[160,2048]{1,0:T(8,128)(2,1)S(1)} %bitcast.7, bf16[160,256]{1,0:T(8,128)(2,1)S(1)} %collective-permute-done.5.refs_0_, ...), custom_call_target="tpu_custom_call" | custom-call | flops 167772160 | bytes 1048576 | tf_op jit(solution)/shard_map/pallas_call | solution.py:28
  32.3 0.8 %collective-permute-done.13.refs_2_ = bf16[160,128]{1,0:T(8,128)(2,1)S(1)} collective-permute-done((bf16[160,128]{1,0:T(8,128)(2,1)S(1)}, bf16[160,128]{1,0:T(8,128)(2,1)S(1)}, u32[]{:S(2)}, u32[]{:S(2)}) %collective-permute-start.13) | collective-permute-done | bytes 40992 | tf_op jit(solution)/shard_map/ppermute | solution.py:232
  33.1 5.0 %collective-permute-done.14.refs_3_ = bf16[160,128]{1,0:T(8,128)(2,1)S(1)} collective-permute-done((bf16[160,128]{1,0:T(8,128)(2,1)S(1)}, bf16[160,128]{1,0:T(8,128)(2,1)S(1)}, u32[]{:S(2)}, u32[]{:S(2)}) %collective-permute-start.14) | collective-permute-done | bytes 40992 | tf_op jit(solution)/shard_map/ppermute | solution.py:232
  38.2 1.3 %shard_map.41 = (f32[16,512]{1,0:T(8,128)S(1)}, bf16[160,512]{1,0:T(8,128)(2,1)S(1)}, bf16[128,512]{1,0:T(8,128)(2,1)S(1)}, f32[168,128]{1,0:T(8,128)S(1)}) custom-call(s32[4]{0:T(128)S(1)} %pad_add_fusion.place_ref, f32[4,160]{1,0:T(4,128)S(1)} %copy-done.2, bf16[160,128]{1,0:T(8,128)(2,1)S(1)} %get-tuple-element.19.halo_ref, ...), custom_call_target="tpu_custom_call" | custom-call | flops 1048576 | bytes 1048576 | tf_op jit(solution)/shard_map/pallas_call | solution.py:28
  39.7 1.2 %collective-permute-done.15 = f32[168,128]{1,0:T(8,128)S(1)} collective-permute-done((f32[168,128]{1,0:T(8,128)S(1)}, f32[168,128]{1,0:T(8,128)S(1)}, u32[]{:S(2)}, u32[]{:S(2)}) %collective-permute-start.15) | collective-permute-done | bytes 86048 | tf_op jit(solution)/shard_map/ppermute | solution.py:194
  40.9 1.0 %collective-permute-start.16 = (f32[168,128]{1,0:T(8,128)S(1)}, f32[168,128]{1,0:T(8,128)S(1)}, u32[]{:S(2)}, u32[]{:S(2)}) collective-permute-start(f32[168,128]{1,0:T(8,128)S(1)} %get-tuple-element.31), channel_id=1, source_target_pairs={{0,8},{4,12},{8,0},{12,4},{16,24},{20,28},{24,16},{28,20},{1,9},{5... | collective-permute-start | bytes 258056 | tf_op jit(solution)/shard_map/ppermute | solution.py:265
  41.8 0.7 %shard_map.42 = (bf16[512,160]{1,0:T(8,128)(2,1)S(1)}, f32[512,128]{1,0:T(8,128)S(1)}, f32[512,128]{1,0:T(8,128)S(1)}) custom-call(f32[16,512]{1,0:T(8,128)S(1)} %get-tuple-element.24.raw_ref, bf16[160,512]{1,0:T(8,128)(2,1)S(1)} %get-tuple-element.25.key_ref, bf16[128,512]{1,0:T(8,128)(2,1)S(1)} %get-tuple-element.26.value_ref), custom_call_target="tpu_custom_call" | custom-call | flops 150994944 | bytes 1048576 | tf_op jit(solution)/shard_map/pallas_call | solution.py:28
  42.6 2.5 %collective-permute-start.18 = (f32[168,128]{1,0:T(8,128)S(1)}, f32[168,128]{1,0:T(8,128)S(1)}, u32[]{:S(2)}, u32[]{:S(2)}) collective-permute-start(f32[168,128]{1,0:T(8,128)S(1)} %get-tuple-element.31), channel_id=1, source_target_pairs={{0,24},{4,28},{8,16},{12,20},{16,8},{20,12},{24,0},{28,4},{1,25},{... | collective-permute-start | bytes 258056 | tf_op jit(solution)/shard_map/ppermute | solution.py:265
  45.5 3.3 %collective-permute-done.17 = f32[168,128]{1,0:T(8,128)S(1)} collective-permute-done((f32[168,128]{1,0:T(8,128)S(1)}, f32[168,128]{1,0:T(8,128)S(1)}, u32[]{:S(2)}, u32[]{:S(2)}) %collective-permute-start.17) | collective-permute-done | bytes 86048 | tf_op jit(solution)/shard_map/ppermute | solution.py:265
  48.9 1.0 %shard_map.43 = bf16[512,128]{1,0:T(8,128)(2,1)} custom-call(bf16[512,160]{1,0:T(8,128)(2,1)S(1)} %get-tuple-element.27.query_ref, f32[512,128]{1,0:T(8,128)S(1)} %get-tuple-element.28.numerator_ref, f32[512,128]{1,0:T(8,128)S(1)} %get-tuple-element.29.denominator_ref, f32[168,128]{1,0:T(8,128)S(1)} %get-tuple-element.32.refs_0_, ...), custom_call_target="tpu_custom_call" | custom-call | flops 62914560 | bytes 1048576 | tf_op jit(solution)/shard_map/pallas_call | solution.py:28
  (33 shorter events, 2.2 us)
Async XLA Ops:
  0.0 27.7 %collective-permute-start.4 = (bf16[128,2048]{1,0:T(8,128)(2,1)}, bf16[128,2048]{1,0:T(8,128)(2,1)S(1)}, u32[]{:S(2)}, u32[]{:S(2)}) collective-permute-start(bf16[128,2048]{1,0:T(8,128)(2,1)} %tokens_ref.5), channel_id=1, source_target_pairs={{0,1},{1,0},{2,3},{3,2},{4,5},{5,4},{6,7},{7,6},{8,9},{9,8},{10,11... | collective-permute-start | bytes 1572872 | tf_op jit(solution)/shard_map/ppermute | solution.py:213
  3.1 24.3 %copy-start.1 = (bf16[128,2048]{1,0:T(8,128)(2,1)S(1)}, bf16[128,2048]{1,0:T(8,128)(2,1)}, u32[]{:S(2)}) copy-start(bf16[128,2048]{1,0:T(8,128)(2,1)} %tokens_ref.5) | copy-start | bytes 1572868
  4.0 27.1 %copy-start = (bf16[2048,160]{0,1:T(8,128)(2,1)S(1)}, bf16[2048,160]{0,1:T(8,128)(2,1)}, u32[]{:S(2)}) copy-start(bf16[2048,160]{0,1:T(8,128)(2,1)} %param.4) | copy-start | bytes 1966084
  4.0 12.2 %collective-permute-start.5 = (bf16[160,256]{1,0:T(8,128)(2,1)S(1)}, bf16[160,256]{1,0:T(8,128)(2,1)S(1)}, u32[]{:S(2)}, u32[]{:S(2)}) collective-permute-start(bf16[160,256]{1,0:T(8,128)(2,1)S(1)} %get-tuple-element.21), channel_id=1, source_target_pairs={{2,0},{3,1},{0,2},{1,3},{6,4},{7,5},{4,6},{5,7},{10,8},{11,9},{8,1... | collective-permute-start | bytes 245768 | tf_op jit(solution)/shard_map/ppermute | solution.py:210
  16.2 4.9 %collective-permute-start.6 = (bf16[160,256]{1,0:T(8,128)(2,1)S(1)}, bf16[160,256]{1,0:T(8,128)(2,1)S(1)}, u32[]{:S(2)}, u32[]{:S(2)}) collective-permute-start(bf16[160,256]{1,0:T(8,128)(2,1)S(1)} %collective-permute-done.5.refs_0_), channel_id=1, source_target_pairs={{0,8},{4,12},{8,0},{12,4},{16,24},{20,28},{24,16},{28,20},{1,9},{5... | collective-permute-start | bytes 245768 | tf_op jit(solution)/shard_map/ppermute | solution.py:194
  17.7 5.3 %collective-permute-start.7 = (bf16[160,256]{1,0:T(8,128)(2,1)S(1)}, bf16[160,256]{1,0:T(8,128)(2,1)S(1)}, u32[]{:S(2)}, u32[]{:S(2)}) collective-permute-start(bf16[160,256]{1,0:T(8,128)(2,1)S(1)} %collective-permute-done.5.refs_0_), channel_id=1, source_target_pairs={{0,16},{4,20},{8,24},{12,28},{16,0},{20,4},{24,8},{28,12},{1,17},{... | collective-permute-start | bytes 245768 | tf_op jit(solution)/shard_map/ppermute | solution.py:194
  19.2 5.3 %collective-permute-start.8 = (bf16[160,256]{1,0:T(8,128)(2,1)S(1)}, bf16[160,256]{1,0:T(8,128)(2,1)S(1)}, u32[]{:S(2)}, u32[]{:S(2)}) collective-permute-start(bf16[160,256]{1,0:T(8,128)(2,1)S(1)} %collective-permute-done.5.refs_0_), channel_id=1, source_target_pairs={{0,24},{4,28},{8,16},{12,20},{16,8},{20,12},{24,0},{28,4},{1,25},{... | collective-permute-start | bytes 245768 | tf_op jit(solution)/shard_map/ppermute | solution.py:194
  19.7 4.9 %collective-permute-start.9 = (bf16[160,256]{1,0:T(8,128)(2,1)S(1)}, bf16[160,256]{1,0:T(8,128)(2,1)S(1)}, u32[]{:S(2)}, u32[]{:S(2)}) collective-permute-start(bf16[160,256]{1,0:T(8,128)(2,1)S(1)} %collective-permute-done.5.refs_0_), channel_id=1, source_target_pairs={{0,4},{4,0},{8,12},{12,8},{16,20},{20,16},{24,28},{28,24},{1,5},{5... | collective-permute-start | bytes 245768 | tf_op jit(solution)/shard_map/ppermute | solution.py:194
  21.1 4.1 %collective-permute-start.10 = (bf16[160,256]{1,0:T(8,128)(2,1)S(1)}, bf16[160,256]{1,0:T(8,128)(2,1)S(1)}, u32[]{:S(2)}, u32[]{:S(2)}) collective-permute-start(bf16[160,256]{1,0:T(8,128)(2,1)S(1)} %collective-permute-done.6.refs_1_), channel_id=1, source_target_pairs={{0,4},{4,0},{8,12},{12,8},{16,20},{20,16},{24,28},{28,24},{1,5},{5... | collective-permute-start | bytes 245768 | tf_op jit(solution)/shard_map/ppermute | solution.py:194
  22.9 3.0 %collective-permute-start.11 = (bf16[160,256]{1,0:T(8,128)(2,1)S(1)}, bf16[160,256]{1,0:T(8,128)(2,1)S(1)}, u32[]{:S(2)}, u32[]{:S(2)}) collective-permute-start(bf16[160,256]{1,0:T(8,128)(2,1)S(1)} %collective-permute-done.7.refs_2_), channel_id=1, source_target_pairs={{0,4},{4,0},{8,12},{12,8},{16,20},{20,16},{24,28},{28,24},{1,5},{5... | collective-permute-start | bytes 245768 | tf_op jit(solution)/shard_map/ppermute | solution.py:194
  24.6 2.0 %collective-permute-start.12 = (bf16[160,256]{1,0:T(8,128)(2,1)S(1)}, bf16[160,256]{1,0:T(8,128)(2,1)S(1)}, u32[]{:S(2)}, u32[]{:S(2)}) collective-permute-start(bf16[160,256]{1,0:T(8,128)(2,1)S(1)} %collective-permute-done.8.refs_3_), channel_id=1, source_target_pairs={{0,4},{4,0},{8,12},{12,8},{16,20},{20,16},{24,28},{28,24},{1,5},{5... | collective-permute-start | bytes 245768 | tf_op jit(solution)/shard_map/ppermute | solution.py:194
  24.6 7.1 %collective-permute-start.3 = (bf16[8,2048]{1,0:T(8,128)(2,1)S(1)}, bf16[8,2048]{1,0:T(8,128)(2,1)S(1)}, u32[]{:S(2)}, u32[]{:S(2)}) collective-permute-start(bf16[8,2048]{1,0:T(8,128)(2,1)S(1)} %get-tuple-element.18), channel_id=1, source_target_pairs={{3,7},{7,11},{11,15},{15,19},{19,23},{23,27},{27,31}} | collective-permute-start | bytes 98312 | tf_op jit(solution)/shard_map/ppermute | solution.py:218
  25.2 6.5 %collective-permute-start.2 = (bf16[8,2048]{1,0:T(8,128)(2,1)S(1)}, bf16[8,2048]{1,0:T(8,128)(2,1)S(1)}, u32[]{:S(2)}, u32[]{:S(2)}) collective-permute-start(bf16[8,2048]{1,0:T(8,128)(2,1)S(1)} %get-tuple-element.18), channel_id=1, source_target_pairs={{3,6},{7,10},{11,14},{15,18},{19,22},{23,26},{27,30}} | collective-permute-start | bytes 98312 | tf_op jit(solution)/shard_map/ppermute | solution.py:218
  25.9 5.9 %collective-permute-start = (bf16[8,2048]{1,0:T(8,128)(2,1)S(1)}, bf16[8,2048]{1,0:T(8,128)(2,1)S(1)}, u32[]{:S(2)}, u32[]{:S(2)}) collective-permute-start(bf16[8,2048]{1,0:T(8,128)(2,1)S(1)} %get-tuple-element.18), channel_id=1, source_target_pairs={{3,4},{7,8},{11,12},{15,16},{19,20},{23,24},{27,28}} | collective-permute-start | bytes 98312 | tf_op jit(solution)/shard_map/ppermute | solution.py:218
  26.6 5.2 %collective-permute-start.1 = (bf16[8,2048]{1,0:T(8,128)(2,1)S(1)}, bf16[8,2048]{1,0:T(8,128)(2,1)S(1)}, u32[]{:S(2)}, u32[]{:S(2)}) collective-permute-start(bf16[8,2048]{1,0:T(8,128)(2,1)S(1)} %get-tuple-element.18), channel_id=1, source_target_pairs={{3,5},{7,9},{11,13},{15,17},{19,21},{23,25},{27,29}} | collective-permute-start | bytes 98312 | tf_op jit(solution)/shard_map/ppermute | solution.py:218
  27.7 5.4 %collective-permute-start.13 = (bf16[160,128]{1,0:T(8,128)(2,1)S(1)}, bf16[160,128]{1,0:T(8,128)(2,1)S(1)}, u32[]{:S(2)}, u32[]{:S(2)}) collective-permute-start(bf16[160,128]{1,0:T(8,128)(2,1)S(1)} %shard_map.40), channel_id=1, source_target_pairs={{0,2},{1,3},{2,0},{3,1},{4,6},{5,7},{6,4},{7,5},{8,10},{9,11},{10,... | collective-permute-start | bytes 122888 | tf_op jit(solution)/shard_map/ppermute | solution.py:232
  31.7 6.5 %collective-permute-start.14 = (bf16[160,128]{1,0:T(8,128)(2,1)S(1)}, bf16[160,128]{1,0:T(8,128)(2,1)S(1)}, u32[]{:S(2)}, u32[]{:S(2)}) collective-permute-start(bf16[160,128]{1,0:T(8,128)(2,1)S(1)} %get-tuple-element.23), channel_id=1, source_target_pairs={{0,2},{1,3},{2,0},{3,1},{4,6},{5,7},{6,4},{7,5},{8,10},{9,11},{10,... | collective-permute-start | bytes 122888 | tf_op jit(solution)/shard_map/ppermute | solution.py:232
  32.3 5.8 %copy-start.2 = (f32[4,160]{1,0:T(4,128)S(1)}, f32[4,160]{1,0:T(4,128)}, u32[]{:S(2)}) copy-start(f32[4,160]{1,0:T(4,128)} %conv_ref.1) | copy-start | bytes 7684
  39.5 1.3 %collective-permute-start.15 = (f32[168,128]{1,0:T(8,128)S(1)}, f32[168,128]{1,0:T(8,128)S(1)}, u32[]{:S(2)}, u32[]{:S(2)}) collective-permute-start(f32[168,128]{1,0:T(8,128)S(1)} %get-tuple-element.30), channel_id=1, source_target_pairs={{0,4},{4,0},{8,12},{12,8},{16,20},{20,16},{24,28},{28,24},{1,5},{5... | collective-permute-start | bytes 258056 | tf_op jit(solution)/shard_map/ppermute | solution.py:194
  40.9 4.7 %collective-permute-start.16 = (f32[168,128]{1,0:T(8,128)S(1)}, f32[168,128]{1,0:T(8,128)S(1)}, u32[]{:S(2)}, u32[]{:S(2)}) collective-permute-start(f32[168,128]{1,0:T(8,128)S(1)} %get-tuple-element.31), channel_id=1, source_target_pairs={{0,8},{4,12},{8,0},{12,4},{16,24},{20,28},{24,16},{28,20},{1,9},{5... | collective-permute-start | bytes 258056 | tf_op jit(solution)/shard_map/ppermute | solution.py:265
  42.5 6.3 %collective-permute-start.17 = (f32[168,128]{1,0:T(8,128)S(1)}, f32[168,128]{1,0:T(8,128)S(1)}, u32[]{:S(2)}, u32[]{:S(2)}) collective-permute-start(f32[168,128]{1,0:T(8,128)S(1)} %get-tuple-element.31), channel_id=1, source_target_pairs={{0,16},{4,20},{8,24},{12,28},{16,0},{20,4},{24,8},{28,12},{1,17},{... | collective-permute-start | bytes 258056 | tf_op jit(solution)/shard_map/ppermute | solution.py:265
  42.6 6.2 %collective-permute-start.18 = (f32[168,128]{1,0:T(8,128)S(1)}, f32[168,128]{1,0:T(8,128)S(1)}, u32[]{:S(2)}, u32[]{:S(2)}) collective-permute-start(f32[168,128]{1,0:T(8,128)S(1)} %get-tuple-element.31), channel_id=1, source_target_pairs={{0,24},{4,28},{8,16},{12,20},{16,8},{20,12},{24,0},{28,4},{1,25},{... | collective-permute-start | bytes 258056 | tf_op jit(solution)/shard_map/ppermute | solution.py:265
